TPU v7x, 32 devices: a whole 2x2x4 slice. The times are simulated.
32 devices in a mesh: leaf: 4 (over y, core), panel: 8 (over z, x).
Axes of the slice: x: 2, y: 2, z: 4, core: 2. Of those that a mesh axis runs over, the one named last changes fastest.
Arguments:
- root_entries: float32 [2048, 2048], P('leaf', 'panel'), as said below
- child_updates: bfloat16 [2048, 1024], P('leaf', 'panel'), as said below
- child_map: int32 [2, 1024], replicated, may hold values from 0 to 2047, as said below
- tile_pattern: int32 [2, 8, 8], replicated, may hold values 0 or 1
Outputs:
- factored: float32 [2048, 2048], P('leaf', 'panel')
Inputs may be any that keep to these rules, and one draw needn't show every extreme that they name: `root_entries`: symmetric and positive definite. `child_updates`: each child's block of 1024 rows is symmetric. `child_map`: each row holds 1024 distinct rows of the root front.
All inputs are finite; a program needn't handle non-finite values.
Results may differ from a plain program's by a relative error of at most 0.0003.
Values may be sent and summed in bfloat16 or wider, within the bound.
No kernel may reach another device: no remote copies, remote signals or barrier semaphores. Data moves between devices by JAX's collectives and lax.ppermute only.
A program may use at most 64 MiB of HBM per device.

v0:
```python
import functools

import jax
import jax.numpy as jnp
from jax import lax
from jax.experimental import pallas as pl
from jax.experimental.pallas import tpu as pltpu
from jax.sharding import PartitionSpec as P

PANEL = 256
STEPS = 5
HALF = PANEL // 2
SUB = 8
BAND = 32
DONE = STEPS * PANEL
HIGHEST = lax.Precision.HIGHEST
F32 = jnp.float32
BF16 = jnp.bfloat16
SMEM_SPEC = pl.BlockSpec(memory_space=pltpu.SMEM)
VMEM_SPEC = pl.BlockSpec(memory_space=pltpu.VMEM)


def mm(a, b, precision=None):
    return lax.dot_general(
        a, b, (((1,), (0,)), ((), ())), precision=precision, preferred_element_type=F32
    )


def mm_nt(a, b, precision=None):
    return lax.dot_general(
        a, b, (((1,), (1,)), ((), ())), precision=precision, preferred_element_type=F32
    )


def thirds(x):
    high = x.astype(BF16)
    rest = x - high.astype(F32)
    middle = rest.astype(BF16)
    return high, middle, (rest - middle.astype(F32)).astype(BF16)


def mm3_nt(a, b):
    ah, bh = a.astype(BF16), b.astype(BF16)
    al, bl = (a - ah.astype(F32)).astype(BF16), (b - bh.astype(F32)).astype(BF16)
    return mm_nt(jnp.concatenate([ah, ah, al], 1), jnp.concatenate([bh, bl, bh], 1))


def mm3(a, b):
    ah, bh = a.astype(BF16), b.astype(BF16)
    al, bl = (a - ah.astype(F32)).astype(BF16), (b - bh.astype(F32)).astype(BF16)
    return mm(jnp.concatenate([ah, ah, al], 1), jnp.concatenate([bh, bl, bh], 0))


def factor_half(a):
    n = a.shape[0]
    groups = BAND // SUB
    lane = lax.broadcasted_iota(jnp.int32, (SUB, n), 1)
    sub = lax.broadcasted_iota(jnp.int32, (SUB, n), 0)
    band_lane = lax.broadcasted_iota(jnp.int32, (BAND, n), 1)
    band_sub = lax.broadcasted_iota(jnp.int32, (BAND, n), 0)

    def full(v):
        return jnp.broadcast_to(v, (SUB, n))

    left = a
    uppers, inverses = [], []
    for base in range(0, n, BAND):
        rows = [left[SUB * g : SUB * g + SUB, :] for g in range(groups)]
        inv = [
            jnp.where(lane < base, rows[g], jnp.where(lane == sub + (base + SUB * g), 1.0, 0.0))
            for g in range(groups)
        ]
        for g in range(groups):
            below = groups - g
            at = base + SUB * g
            col = [
                [full(rows[g + h][:, at + q : at + q + 1]) for h in range(below)] for q in range(SUB)
            ]
            tip = [
                [full(col[q][0][r : r + 1, :]) if r >= q else None for r in range(SUB)]
                for q in range(SUB)
            ]
            for q in range(SUB):
                scale = lax.rsqrt(tip[q][q])
                part = [tip[q][r] * scale if r > q else None for r in range(SUB)]
                for q2 in range(q + 1, SUB):
                    for r in range(q2, SUB):
                        tip[q2][r] = tip[q2][r] - part[r] * part[q2]
                mult = [col[q][h] * scale for h in range(below)]
                mult[0] = jnp.where(sub > q, mult[0], 0.0)
                for q2 in range(q + 1, SUB):
                    for h in range(below):
                        col[q2][h] = col[q2][h] - mult[h] * part[q2]
                for x in (rows, inv):
                    row = full(x[g][q : q + 1, :]) * scale
                    x[g] = jnp.where(sub == q, row, x[g] - mult[0] * row)
                    for h in range(1, below):
                        x[g + h] = x[g + h] - mult[h] * row
        upper = jnp.concatenate(rows, 0)
        inverse = jnp.concatenate(inv, 0)
        uppers.append(jnp.where(band_lane >= band_sub + base, upper, 0.0))
        inverses.append(inverse)
        if base + BAND < n:
            both = jnp.where(band_lane < base + BAND, inverse, upper)
            uh, um, ul = thirds(upper)
            bh, bm, bl = thirds(both)
            product = lax.dot_general(
                jnp.concatenate([uh, uh, um, uh, ul, um], 0),
                jnp.concatenate([bh, bm, bh, bl, bh, bm], 0),
                (((0,), (0,)), ((), ())),
                preferred_element_type=F32,
            )
            left = left[BAND:, :]
            at = lax.broadcasted_iota(jnp.int32, left.shape, 1)
            left = jnp.where((at >= base) & (at < base + BAND), 0.0, left) - product[base + BAND :, :]
    return jnp.concatenate(uppers, 0), jnp.concatenate(inverses, 0)


def select_kernel(bases_ref, keep_ref, map_ref, *refs):
    count = bases_ref.shape[0]
    pieces, outs = refs[:-count], refs[-count:]
    width = pieces[0].shape[1]
    tiles = keep_ref.shape[0]
    tile = pieces[0].shape[0] // tiles
    kept = []
    for k, piece in enumerate(pieces):
        kept.append(
            jnp.concatenate(
                [
                    piece[t * tile : (t + 1) * tile, :] * keep_ref[t, k].astype(F32).astype(BF16)
                    for t in range(tiles)
                ],
                0,
            )
        )
    kept = jnp.concatenate(kept, 1)
    ids = lax.broadcasted_iota(jnp.int32, (PANEL, 1), 0)
    for block in range(count):
        hot = (ids + bases_ref[block] == map_ref[...]).astype(F32).astype(BF16)
        outs[block][...] = mm_nt(kept, hot).astype(BF16)


def placed(row_base, count, map_ref, pieces, lanes=slice(None)):
    width = pieces[0].shape[0]
    ids = lax.broadcasted_iota(jnp.int32, (count, 1), 0) + row_base
    total = None
    for x, piece in enumerate(pieces):
        hot = (ids == map_ref[:, x * width : (x + 1) * width]).astype(F32).astype(BF16)
        term = mm(hot, piece[:, lanes])
        total = term if total is None else total + term
    return total


def solve_right(g, i1, l21, i2):
    one = mm3_nt(g[:, :HALF], i1)
    two = mm3_nt(g[:, HALF:] - mm3_nt(one, l21), i2)
    return jnp.concatenate([one, two], 1)


def solve_left(h, i1, l21, i2):
    one = mm3(i1, h[:HALF, :])
    two = mm3(i2, h[HALF:, :] - mm3(l21, one))
    return jnp.concatenate([one, two], 0)


def step_kernel(step, leaves, spots, *refs):
    refs = list(refs)

    def take(count):
        out = refs[:count]
        del refs[:count]
        return out

    (place_ref, map_ref) = take(2)
    step_col, root_step, (root_mine,) = take(leaves), take(spots), take(1)
    prev = step - 1
    last = step == STEPS - 1
    if step:
        own_col, root_own = take(leaves), take(spots)
        before_a, before_r, before_y = take(step), take(prev), take(prev)
        (sum_ref, rest_ref) = take(2)
        factors = take(step)
    if last:
        (out_ref,) = take(1)
        (fac_ref, gr_ref, xr_ref, y_ref, t_ref, h_ref) = refs[-6:]
    else:
        (xa_ref, gr_ref, fac_ref) = take(3)
        if step:
            (xr_ref, y_ref, t_ref) = take(3)
    (root_s, d_s) = take(2)
    if step:
        (rown_s,) = take(1)
    if not last:
        (g_s,) = take(1)
    device_rows = step_col[0].shape[0]
    per_leaf = device_rows // PANEL
    panel = place_ref[1]
    base = place_ref[0] * device_rows
    for x in range(spots):
        leaf = place_ref[2 + x]
        root_s[leaf] = root_step[x][...]
        if step:
            rown_s[leaf] = root_own[x][...]

    def panel_rows(m, r):
        return before_a[m][(r - m - 1) * PANEL : (r - m) * PANEL, :]

    def own_rows(r, lanes):
        return rown_s[r // per_leaf, pl.ds(r % per_leaf * PANEL, PANEL), lanes].astype(F32)

    share = root_s.shape[1] - device_rows
    if share == PANEL:
        rest = root_s[step // per_leaf, pl.ds(device_rows, PANEL), :]
    else:
        rest = jnp.concatenate(
            [root_s[x, pl.ds(device_rows, share), :] for x in range(PANEL // share)], 0
        )
    diag = root_s[step // per_leaf, pl.ds(step % per_leaf * PANEL, PANEL), :].astype(F32)
    diag = diag + rest.astype(F32) + placed(step * PANEL, PANEL, map_ref, step_col)
    for m in range(step):
        diag = diag - mm_nt(panel_rows(m, step), panel_rows(m, step))
    d_s[0] = diag[:HALF, :HALF]
    d_s[1] = diag[HALF:, HALF:]
    fac_ref[1] = diag[HALF:, :HALF]
    pieces = STEPS - 1 - step
    part = device_rows // 2

    def half(n, carry):
        upper, inverse = factor_half(d_s[n])
        fac_ref[2 * n] = upper
        fac_ref[3 + n] = inverse
        if not last:
            count = pieces * HALF
            here = pl.ds(pl.multiple_of(n * count, HALF), count)
            start = (step + 1) * PANEL + n * count
            found = []
            for c in range(pieces):
                row = start + c * HALF
                at = pl.ds(pl.multiple_of(row % device_rows, HALF), HALF)
                found.append(root_s[row // device_rows, at, :])
            g = jnp.concatenate(found, 0).astype(F32) + placed(start, count, map_ref, step_col)
            for m in range(step):
                at = pl.ds(pl.multiple_of((step - m) * PANEL + n * count, HALF), count)
                g = g - mm_nt(before_a[m][at, :], panel_rows(m, step))
            g_s[here, :] = g
        rows = pl.ds(pl.multiple_of(n * part, HALF), part)
        mine = root_mine[rows, :].astype(F32) + placed(base + n * part, part, map_ref, step_col)
        if step:
            fac = factors[prev]
            p1, pl21, p2 = fac[3], fac[1], fac[4]
            xr = solve_right(sum_ref[rows, :], p1, pl21, p2).astype(BF16)
            for m in range(prev):
                mine = mine - mm_nt(before_r[m][rows, :], panel_rows(m, step))
            mine = mine - mm_nt(xr, panel_rows(prev, step))
            xr_ref[rows, :] = xr
            lanes = pl.ds(pl.multiple_of(n * HALF, HALF), HALF)
            h = own_rows(prev, lanes) + placed(prev * PANEL, PANEL, map_ref, own_col, lanes)
            for m in range(prev):
                h = h - mm(panel_rows(m, prev), before_y[m][:, lanes])
            y = solve_left(h, p1, pl21, p2).astype(BF16)
            y_ref[:, lanes] = y
            t = rest_ref[rows, :]
            if step == 1:
                t = t + placed(base + n * part, part, map_ref, own_col)
            else:
                use = jnp.where(step - 2 < panel, 1.0, 0.0).astype(BF16)
                t = t - mm(before_r[step - 2][rows, :], before_y[step - 2][...] * use)
            t_ref[rows, :] = t
            if last:
                h = own_rows(step, lanes) + placed(step * PANEL, PANEL, map_ref, own_col, lanes)
                for m in range(prev):
                    h = h - mm(panel_rows(m, step), before_y[m][:, lanes])
                h_ref[:, lanes] = h - mm(panel_rows(prev, step), y)
        gr_ref[rows, :] = mine

        @pl.when(n == 0)
        def _():
            low = mm3_nt(fac_ref[1], inverse)
            fac_ref[1] = low
            d_s[1] = d_s[1] - mm3_nt(low, low)

        return carry

    lax.fori_loop(0, 2, half, 0)
    l21, i1, i2 = fac_ref[1], fac_ref[3], fac_ref[4]
    if not last:
        xa_ref[...] = solve_right(g_s[...], i1, l21, i2).astype(BF16)
        return
    rows = lax.broadcasted_iota(jnp.int32, (device_rows, 1), 0) + base
    use = jnp.where(prev < panel, 1.0, 0.0).astype(BF16)
    t = t_ref[...] - mm(xr_ref[...], y_ref[...] * use)

    @pl.when(panel >= STEPS)
    def _():
        xr = solve_right(gr_ref[...], i1, l21, i2).astype(BF16)
        y = solve_left(h_ref[...], i1, l21, i2).astype(BF16)
        out_ref[...] = jnp.where(rows >= DONE, t - mm(xr, y), 0.0)

    for m in range(STEPS - 1):

        @pl.when(panel == m)
        def _():
            fac_ref[...] = factors[m][...]

    @pl.when(panel < STEPS)
    def _():
        solved = solve_right(t, fac_ref[3], fac_ref[1], fac_ref[4])
        out_ref[...] = jnp.where(rows >= (panel + 1) * PANEL, solved, 0.0)
        for part in range(device_rows // PANEL):
            start = part * PANEL

            @pl.when(base + start == panel * PANEL)
            def _():
                out_ref[start : start + HALF, :HALF] = fac_ref[0].T
                out_ref[start + HALF : start + PANEL, :HALF] = fac_ref[1]
                out_ref[start + HALF : start + PANEL, HALF:] = fac_ref[2].T


def flip(value, axis, bits, count):
    return lax.ppermute(value, axis, [(i, i ^ bits) for i in range(count)])


def after(value, *held):
    return lax.optimization_barrier((value, *held))[0]


def over_leaf(value, leaf_count, first=None, second=None):
    if first is not None:
        value = after(value, first)
    parts = {0: value}
    bit = leaf_count // 2
    while bit:
        for have in list(parts):
            part = parts[have] if second is None or not have else after(parts[have], second)
            parts[have | bit] = flip(part, "leaf", bit, leaf_count)
        bit //= 2
    return [parts[x] for x in range(leaf_count)]


def over_panel(value, panel_count):
    parts = {0: value}
    bit = panel_count // 2
    while bit > 2:
        for have in list(parts):
            parts[have | bit] = flip(parts[have], "panel", bit, panel_count)
        bit //= 2
    for have in list(parts):
        for near in range(1, 2 * bit):
            parts[have | near] = flip(parts[have], "panel", near, panel_count)
    return [parts[x] for x in range(panel_count)]


def per_device(root_entries, child_updates, child_map, tile_pattern):
    device_rows, panel_width = root_entries.shape
    child_cols = child_updates.shape[1]
    leaf_count = lax.axis_size("leaf")
    panel_count = lax.axis_size("panel")
    leaf = lax.axis_index("leaf")
    panel = lax.axis_index("panel")
    child_order = child_cols * panel_count
    half_leaf = leaf_count // 2
    tile_width = child_order // tile_pattern.shape[1]
    tiles = device_rows // tile_width
    child = leaf // half_leaf
    small = leaf_count == 4 and panel_count == 8
    params = pltpu.CompilerParams(vmem_limit_bytes=56 * 2**20)

    high = lax.reduce_precision(root_entries, 8, 7)
    offset = panel * PANEL % device_rows
    rest = lax.dynamic_slice_in_dim(root_entries - high, offset, PANEL, 0)
    rest = rest.astype(BF16)
    if small:
        share = PANEL // leaf_count
        holder = jnp.minimum(panel * PANEL // device_rows, leaf_count - 1)
        shares = [
            lax.dynamic_slice_in_dim(rest, (leaf ^ x) * share, share, 0) for x in range(leaf_count)
        ]
        shares = shares[:1] + [flip(shares[x], "leaf", x, leaf_count) for x in range(1, leaf_count)]
        rest = shares[0]
        for x in range(1, leaf_count):
            rest = jnp.where(leaf ^ x == holder, shares[x], rest)
    column = jnp.concatenate([high.astype(BF16), rest], 0)

    pieces = over_panel(child_updates, panel_count)
    if small:
        columns = over_panel(after(column, pieces[4]), panel_count)
        root_all = jnp.zeros((STEPS + 1, *column.shape), BF16)
        for x in (0, 4, 1, 2, 3, 5, 6, 7):
            slot = jnp.minimum(panel ^ x, STEPS)
            root_all = lax.dynamic_update_slice(root_all, columns[x][None], (slot, 0, 0))
    else:
        root_all = lax.all_gather(column, "panel", axis=0)
    order = panel ^ jnp.arange(panel_count, dtype=jnp.int32)
    own_map = lax.dynamic_index_in_dim(child_map, child, 0, keepdims=False)
    col_map = own_map.reshape(panel_count, child_cols)[order].reshape(1, child_order)
    pattern = lax.dynamic_index_in_dim(tile_pattern, child, 0, keepdims=False)
    mirrored = jnp.maximum(pattern, pattern.T)
    keep = lax.dynamic_slice_in_dim(mirrored, leaf % half_leaf * tiles, tiles, 0)[:, order]
    keep = (keep > 0).astype(jnp.int32)

    def select(bases):
        count = bases.shape[0]
        return pl.pallas_call(
            select_kernel,
            in_specs=[SMEM_SPEC, SMEM_SPEC, VMEM_SPEC] + [VMEM_SPEC] * panel_count,
            out_specs=[VMEM_SPEC] * count,
            out_shape=[jax.ShapeDtypeStruct((device_rows, PANEL), BF16)] * count,
            compiler_params=params,
            cost_estimate=pl.CostEstimate(
                flops=10**9 * count, transcendentals=0, bytes_accessed=2**20
            ),
        )(bases, keep, col_map, *pieces)

    starts = jnp.arange(STEPS, dtype=jnp.int32) * PANEL
    picked = select(starts[:1])
    picked += select(jnp.concatenate([starts[1:], (panel * PANEL)[None].astype(jnp.int32)]))

    leaf_order = leaf ^ jnp.arange(leaf_count, dtype=jnp.int32)
    row_map = child_map.reshape(leaf_count, device_rows)[leaf_order].reshape(1, 2 * child_order)
    need = -(-DONE // device_rows)
    spots = leaf_count if small else need
    slots = max(spots, need)
    spot_order = leaf_order if small else jnp.arange(need, dtype=jnp.int32)
    place = jnp.concatenate([jnp.stack([leaf, panel]).astype(jnp.int32), spot_order])

    def root_pieces(value, first=None, second=None):
        if small:
            return over_leaf(value, leaf_count, first, second)
        every = lax.all_gather(value if first is None else after(value, first), "leaf", axis=0)
        return [every[x] for x in range(need)]

    xa, xr, ys, factors = [], [], [], []
    early = 2 if small else 1
    cols = [over_leaf(picked[step], leaf_count) for step in range(early)]
    if small:
        own_col = over_leaf(picked[STEPS], leaf_count)
        root_own = root_pieces(after(high.astype(BF16), pieces[1]))
        root_all = after(root_all, row_map, place, own_col[-1], *[c[-1] for c in cols])
        roots = [root_pieces(root_all[0])]
    else:
        roots = [root_pieces(root_all[0])]
    done = [roots[0][-1]]
    for step in range(STEPS):
        if step and not small:
            cols.append(over_leaf(after(picked[step], done[-1]), leaf_count))
            roots.append(root_pieces(root_all[step], done[-1]))
        if step == 1 and not small:
            own_part = after(picked[STEPS], done[-1])
            own_col = over_leaf(own_part, leaf_count)
            root_own = root_pieces(high.astype(BF16), own_part)
        root_mine = root_all[step]
        root_step = roots[step]
        step_col = cols[step]
        last = step == STEPS - 1
        args = [*step_col, *root_step, root_mine]
        scratch = [
            pltpu.VMEM((slots, column.shape[0], PANEL), BF16),
            pltpu.VMEM((2, HALF, HALF), F32),
        ]
        if step:
            args += [*own_col, *root_own, *xa, *xr, *ys, mine, rest_block, *factors]
            scratch += [pltpu.VMEM((slots, device_rows, PANEL), BF16)]
        block = jax.ShapeDtypeStruct((device_rows, PANEL), F32)
        if last:
            shapes = [block]
            scratch += [
                pltpu.VMEM((5, HALF, HALF), F32),
                pltpu.VMEM((device_rows, PANEL), F32),
                pltpu.VMEM((device_rows, PANEL), BF16),
                pltpu.VMEM((PANEL, PANEL), BF16),
                pltpu.VMEM((device_rows, PANEL), F32),
                pltpu.VMEM((PANEL, PANEL), F32),
            ]
        else:
            scratch += [pltpu.VMEM(((STEPS - 1 - step) * PANEL, PANEL), F32)]
            shapes = [
                jax.ShapeDtypeStruct(((STEPS - 1 - step) * PANEL, PANEL), BF16),
                block,
                jax.ShapeDtypeStruct((5, HALF, HALF), F32),
            ]
            if step:
                shapes += [
                    jax.ShapeDtypeStruct((device_rows, PANEL), BF16),
                    jax.ShapeDtypeStruct((PANEL, PANEL), BF16),
                    block,
                ]
        out = pl.pallas_call(
            functools.partial(step_kernel, step, leaf_count, spots),
            in_specs=[SMEM_SPEC] + [VMEM_SPEC] * (1 + len(args)),
            out_specs=[VMEM_SPEC] * len(shapes),
            out_shape=shapes,
            scratch_shapes=scratch,
            compiler_params=params,
            cost_estimate=pl.CostEstimate(
                flops=15 * 10**9, transcendentals=0, bytes_accessed=4 * 2**20
            ),
        )(place, row_map, *args)
        if last:
            return out[0]
        xa.append(out[0])
        mine = out[1]
        factors.append(out[2])
        rest_block = root_entries
        if step:
            xr.append(out[3])
            ys.append(out[4])
            rest_block = out[5]
        done.append(out[0])
        if small and not last:
            if step + 2 < STEPS:
                cols.append(over_leaf(picked[step + 2], leaf_count, done[step], done[step + 1]))
            roots.append(root_pieces(root_all[step + 1], done[step], done[step + 1]))


def solution(mesh):
    spots = (P("leaf", "panel"), P("leaf", "panel"), P(), P())
    return jax.shard_map(
        per_device, mesh=mesh, in_specs=spots, out_specs=P("leaf", "panel"), check_vma=False
    )
```

profile of v0, /device:TPU:0, one launch (start us, length us, event | category | flops | bytes accessed | tf_op | source)
XLA Modules:
  0.0 168.9 jit_solution(9972783794760633833)
XLA Ops:
  0.0 4.1 %collective-permute-start.3 = (bf16[512,128]{1,0:T(8,128)(2,1)}, bf16[512,128]{1,0:T(8,128)(2,1)S(1)}, u32[]{:S(2)}, u32[]{:S(2)}) collective-permute-start(bf16[512,128]{1,0:T(8,128)(2,1)} %refs_0_.3), channel_id=1, source_target_pairs={{0,4},{1,5},{2,6},{3,7},{4,0},{5,1},{6,2},{7,3},{8,12},{9,13},{10,... | collective-permute-start | bytes 393224 | tf_op jit(solution)/shard_map/ppermute | solution.py:320
  4.1 1.5 collective-permute-start
  5.6 1.1 reduce-precision_convert_fusion
  6.7 1.1 fusion
  7.8 0.5 collective-permute-start.10
  8.3 1.2 collective-permute-start.11
  10.0 0.6 gather_fusion.1
  10.6 0.6 convert_bitcast_fusion.keep_ref
  11.3 0.6 pad_add_fusion.1.bases_ref
  11.9 0.7 pad_add_fusion.refs_0_
  12.6 1.1 gather_fusion.2
  13.7 0.6 gather_fusion
  14.3 0.6 copy.7
  14.9 1.6 collective-permute-start.1
  17.0 1.6 collective-permute-start.4
  18.6 1.6 collective-permute-start.5
  20.7 0.5 collective-permute-done.1.refs_2_
  21.6 2.3 %collective-permute-done.2.refs_3_ = bf16[512,128]{1,0:T(8,128)(2,1)S(1)} collective-permute-done((bf16[512,128]{1,0:T(8,128)(2,1)S(1)}, bf16[512,128]{1,0:T(8,128)(2,1)S(1)}, u32[]{:S(2)}, u32[]{:S(2)}) %collective-permute-start.2) | collective-permute-done | bytes 131104 | tf_op jit(solution)/shard_map/ppermute | solution.py:320
  23.9 6.9 %collective-permute-start.14 = (bf16[576,256]{1,0:T(8,128)(2,1)S(1)}, bf16[576,256]{1,0:T(8,128)(2,1)S(1)}, u32[]{:S(2)}, u32[]{:S(2)}) collective-permute-start(bf16[576,256]{1,0:T(8,128)(2,1)S(1)} %pad_maximum_fusion), channel_id=1, source_target_pairs={{0,1},{1,0},{2,3},{3,2},{4,5},{5,4},{6,7},{7,6},{8,9},{9,8},{10,11... | collective-permute-start | bytes 884744 | tf_op jit(solution)/shard_map/ppermute | solution.py:320
  30.8 1.6 collective-permute-done.5.refs_6_
  32.3 2.0 %collective-permute-done.6.refs_7_ = bf16[512,128]{1,0:T(8,128)(2,1)S(1)} collective-permute-done((bf16[512,128]{1,0:T(8,128)(2,1)S(1)}, bf16[512,128]{1,0:T(8,128)(2,1)S(1)}, u32[]{:S(2)}, u32[]{:S(2)}) %collective-permute-start.6) | collective-permute-done | bytes 131104 | tf_op jit(solution)/shard_map/ppermute | solution.py:320
  34.4 0.6 copy-done.57
  35.0 3.7 %shard_map.46 = (bf16[512,256]{1,0:T(8,128)(2,1)}, bf16[512,256]{1,0:T(8,128)(2,1)}, bf16[512,256]{1,0:T(8,128)(2,1)}, bf16[512,256]{1,0:T(8,128)(2,1)}, bf16[512,256]{1,0:T(8,128)(2,1)}) custom-call(s32[5]{0:T(128)} %pad_add_fusion.1.bases_ref, s32[4,8]{1,0:T(4,128)} %convert_bitcast_fusion.keep_ref, s32[1,1024]{1,0:T(1,128)} %bitcast.53, ...), custom_call_target="tpu_custom_call" | custom-call | flops 5000000000 | bytes 1048576 | tf_op jit(solution)/shard_map/pallas_call | solution.py:403
  38.6 1.5 collective-permute-start.20
  40.1 3.1 %shard_map.47.refs_2_ = bf16[512,256]{1,0:T(8,128)(2,1)} custom-call(s32[1]{0:T(128)} %bitcast.55, s32[4,8]{1,0:T(4,128)} %convert_bitcast_fusion.keep_ref, s32[1,1024]{1,0:T(1,128)} %bitcast.54, bf16[512,128]{1,0:T(8,128)(2,1)} %refs_0_.3, bf16[512,128]{1,0:T(8,128)(2,1)} %copy-done.52, bf16[512,128]{1,0:T(8,128)(2,1)} %copy-done.53, ...), custom_call_target="tpu_custom_call" | custom-call | flops 1000000000 | bytes 1048576 | tf_op jit(solution)/shard_map/pallas_call | solution.py:403
  43.2 0.6 collective-permute-start.8
  43.9 1.5 collective-permute-start.22
  45.4 3.3 %collective-permute-start.17 = (bf16[576,256]{1,0:T(8,128)(2,1)S(1)}, bf16[576,256]{1,0:T(8,128)(2,1)S(1)}, u32[]{:S(2)}, u32[]{:S(2)}) collective-permute-start(bf16[576,256]{1,0:T(8,128)(2,1)S(1)} %collective-permute-done.13), channel_id=1, source_target_pairs={{0,1},{1,0},{2,3},{3,2},{4,5},{5,4},{6,7},{7,6},{8,9},{9,8},{10,11... | collective-permute-start | bytes 884744 | tf_op jit(solution)/shard_map/ppermute | solution.py:320
  48.8 0.9 collective-permute-start.18
  49.7 1.4 collective-permute-start.19
  51.1 2.4 %collective-permute-done.8.refs_4_ = bf16[512,256]{1,0:T(8,128)(2,1)S(1)} collective-permute-done((bf16[512,256]{1,0:T(8,128)(2,1)S(1)}, bf16[512,256]{1,0:T(8,128)(2,1)S(1)}, u32[]{:S(2)}, u32[]{:S(2)}) %collective-permute-start.8) | collective-permute-done | bytes 262176 | tf_op jit(solution)/shard_map/ppermute | solution.py:320
  53.5 3.9 %collective-permute-done.22.refs_4_ = bf16[512,256]{1,0:T(8,128)(2,1)S(1)} collective-permute-done((bf16[512,256]{1,0:T(8,128)(2,1)}, bf16[512,256]{1,0:T(8,128)(2,1)S(1)}, u32[]{:S(2)}, u32[]{:S(2)}) %collective-permute-start.22) | collective-permute-done | bytes 262176 | tf_op jit(solution)/shard_map/ppermute | solution.py:320
  57.4 0.5 collective-permute-start.23
  57.9 0.8 collective-permute-done.18
  58.8 4.8 %collective-permute-done.19 = bf16[576,256]{1,0:T(8,128)(2,1)S(1)} collective-permute-done((bf16[576,256]{1,0:T(8,128)(2,1)S(1)}, bf16[576,256]{1,0:T(8,128)(2,1)S(1)}, u32[]{:S(2)}, u32[]{:S(2)}) %collective-permute-start.19) | collective-permute-done | bytes 294944 | tf_op jit(solution)/shard_map/ppermute | solution.py:320
  63.8 1.0 collective-permute-start.24
  64.9 6.3 %collective-permute-done.24.refs_8_ = bf16[576,256]{1,0:T(8,128)(2,1)S(1)} collective-permute-done((bf16[576,256]{1,0:T(8,128)(2,1)S(1)}, bf16[576,256]{1,0:T(8,128)(2,1)S(1)}, u32[]{:S(2)}, u32[]{:S(2)}) %collective-permute-start.24) | collective-permute-done | bytes 294944 | tf_op jit(solution)/shard_map/ppermute | solution.py:320
  71.2 0.5 collective-permute-start.29
  71.7 0.7 collective-permute-start.33
  72.8 1.3 collective-permute-start.27
  74.1 0.6 copy-done.49
  74.8 0.7 copy-done.22
  75.5 12.1 %shard_map.48 = (bf16[1024,256]{1,0:T(8,128)(2,1)}, f32[512,256]{1,0:T(8,128)}, f32[5,128,128]{2,1,0:T(8,128)}) custom-call(s32[6]{0:T(128)} %pad_add_fusion.refs_0_, s32[1,2048]{1,0:T(1,128)} %bitcast.48, bf16[512,256]{1,0:T(8,128)(2,1)} %shard_map.47.refs_2_, bf16[512,256]{1,0:T(8,128)(2,1)} %copy-done.49, bf16[512,256]{1,0:T(8,128)(2,1)} %copy-done.37, ...), custom_call_target="tpu_custom_call" | custom-call | flops 15000000512 | bytes 4194304 | tf_op jit(solution)/shard_map/pallas_call | solution.py:487
  87.8 0.5 collective-permute-start.31
  88.8 0.9 collective-permute-done.31.refs_12_
  89.7 0.8 collective-permute-start.41
  90.6 1.3 collective-permute-start.38
  92.0 0.6 copy-done.13
  92.7 15.9 %shard_map.49 = (bf16[768,256]{1,0:T(8,128)(2,1)}, f32[512,256]{1,0:T(8,128)}, f32[5,128,128]{2,1,0:T(8,128)}, bf16[512,256]{1,0:T(8,128)(2,1)}, bf16[256,256]{1,0:T(8,128)(2,1)}, /*index=5*/f32[512,256]{1,0:T(8,128)}) custom-call(s32[6]{0:T(128)} %pad_add_fusion.refs_0_, s32[1,2048]{1,0:T(1,128)} %bitcast.49, bf16[512,256]{1,0:T(8,128)(2,1)} %get-tuple-element.49.refs_2_, ...), custom_call_target="tpu_custom_call" | custom-call | flops 15000000512 | bytes 4194304 | tf_op jit(solution)/shard_map/pallas_call | solution.py:487
  109.5 0.8 collective-permute-start.47
  110.3 0.5 collective-permute-done.37.refs_3_
  110.7 0.8 collective-permute-start.50
  111.7 0.6 copy-done.12
  112.4 15.7 %shard_map.50 = (bf16[512,256]{1,0:T(8,128)(2,1)}, f32[512,256]{1,0:T(8,128)}, f32[5,128,128]{2,1,0:T(8,128)}, bf16[512,256]{1,0:T(8,128)(2,1)}, bf16[256,256]{1,0:T(8,128)(2,1)}, /*index=5*/f32[512,256]{1,0:T(8,128)}) custom-call(s32[6]{0:T(128)} %pad_add_fusion.refs_0_, s32[1,2048]{1,0:T(1,128)} %bitcast.50, bf16[512,256]{1,0:T(8,128)(2,1)} %get-tuple-element.62.refs_2_, ...), custom_call_target="tpu_custom_call" | custom-call | flops 15000000512 | bytes 4194304 | tf_op jit(solution)/shard_map/pallas_call | solution.py:487
  128.1 0.6 collective-permute-start.51
  128.7 0.4 collective-permute-start.48
  129.2 1.2 collective-permute-start.36
  130.4 1.1 collective-permute-start.45
  131.7 0.5 copy-done.47
  132.5 15.4 %shard_map.51 = (bf16[256,256]{1,0:T(8,128)(2,1)}, f32[512,256]{1,0:T(8,128)}, f32[5,128,128]{2,1,0:T(8,128)}, bf16[512,256]{1,0:T(8,128)(2,1)}, bf16[256,256]{1,0:T(8,128)(2,1)}, /*index=5*/f32[512,256]{1,0:T(8,128)}) custom-call(s32[6]{0:T(128)} %pad_add_fusion.refs_0_, s32[1,2048]{1,0:T(1,128)} %bitcast.51, bf16[512,256]{1,0:T(8,128)(2,1)} %get-tuple-element.75.refs_2_, ...), custom_call_target="tpu_custom_call" | custom-call | flops 15000000512 | bytes 4194304 | tf_op jit(solution)/shard_map/pallas_call | solution.py:487
  147.9 0.5 collective-permute-start.52
  148.5 0.4 collective-permute-start.43
  148.9 1.1 collective-permute-done.35.refs_3_
  151.3 17.4 %shard_map.52 = f32[512,256]{1,0:T(8,128)} custom-call(s32[6]{0:T(128)} %pad_add_fusion.refs_0_, s32[1,2048]{1,0:T(1,128)} %bitcast.52, bf16[512,256]{1,0:T(8,128)(2,1)} %get-tuple-element.60.refs_2_, bf16[512,256]{1,0:T(8,128)(2,1)} %copy-done.42, bf16[512,256]{1,0:T(8,128)(2,1)} %copy-done.38, bf16[512,256]{1,0:T(8,128)(2,1)} %copy-done.46, ...), custom_call_target="tpu_custom_call" | custom-call | flops 15000000512 | bytes 4194304 | tf_op jit(solution)/shard_map/pallas_call | solution.py:487
  (203 shorter events, 6.5 us)
Async XLA Ops:
  0.0 17.0 %collective-permute-start.3 = (bf16[512,128]{1,0:T(8,128)(2,1)}, bf16[512,128]{1,0:T(8,128)(2,1)S(1)}, u32[]{:S(2)}, u32[]{:S(2)}) collective-permute-start(bf16[512,128]{1,0:T(8,128)(2,1)} %refs_0_.3), channel_id=1, source_target_pairs={{0,4},{1,5},{2,6},{3,7},{4,0},{5,1},{6,2},{7,3},{8,12},{9,13},{10,... | collective-permute-start | bytes 393224 | tf_op jit(solution)/shard_map/ppermute | solution.py:320
  4.1 16.0 %collective-permute-start = (bf16[512,128]{1,0:T(8,128)(2,1)}, bf16[512,128]{1,0:T(8,128)(2,1)S(1)}, u32[]{:S(2)}, u32[]{:S(2)}) collective-permute-start(bf16[512,128]{1,0:T(8,128)(2,1)} %refs_0_.3), channel_id=1, source_target_pairs={{0,1},{1,0},{2,3},{3,2},{4,5},{5,4},{6,7},{7,6},{8,9},{9,8},{10,11... | collective-permute-start | bytes 393224 | tf_op jit(solution)/shard_map/ppermute | solution.py:320
  6.7 65.7 %copy-start = (bf16[512,256]{1,0:T(8,128)(2,1)}, bf16[512,256]{1,0:T(8,128)(2,1)S(1)}, u32[]{:S(2)}) copy-start(bf16[512,256]{1,0:T(8,128)(2,1)S(1)} %get-tuple-element.56.refs_15_) | copy-start | bytes 786436
  7.8 7.1 %collective-permute-start.10 = (bf16[64,256]{1,0:T(8,128)(2,1)S(1)}, bf16[64,256]{1,0:T(8,128)(2,1)S(1)}, u32[]{:S(2)}, u32[]{:S(2)}) collective-permute-start(bf16[64,256]{1,0:T(8,128)(2,1)S(1)} %get-tuple-element.100), channel_id=1, source_target_pairs={{0,24},{8,16},{16,8},{24,0},{1,25},{9,17},{17,9},{25,1},{2,26},{10... | collective-permute-start | bytes 98312 | tf_op jit(solution)/shard_map/ppermute | solution.py:320
  8.3 8.2 %collective-permute-start.11 = (bf16[64,256]{1,0:T(8,128)(2,1)S(1)}, bf16[64,256]{1,0:T(8,128)(2,1)S(1)}, u32[]{:S(2)}, u32[]{:S(2)}) collective-permute-start(bf16[64,256]{1,0:T(8,128)(2,1)S(1)} %get-tuple-element.99), channel_id=1, source_target_pairs={{0,16},{8,24},{16,0},{24,8},{1,17},{9,25},{17,1},{25,9},{2,18},{10... | collective-permute-start | bytes 98312 | tf_op jit(solution)/shard_map/ppermute | solution.py:320
  9.5 7.4 %collective-permute-start.12 = (bf16[64,256]{1,0:T(8,128)(2,1)S(1)}, bf16[64,256]{1,0:T(8,128)(2,1)S(1)}, u32[]{:S(2)}, u32[]{:S(2)}) collective-permute-start(bf16[64,256]{1,0:T(8,128)(2,1)S(1)} %get-tuple-element.98), channel_id=1, source_target_pairs={{0,8},{8,0},{16,24},{24,16},{1,9},{9,1},{17,25},{25,17},{2,10},{10... | collective-permute-start | bytes 98312 | tf_op jit(solution)/shard_map/ppermute | solution.py:320
  9.8 28.9 %copy-start.58 = (s32[5]{0:T(128)}, s32[5]{0:T(128)S(1)}, u32[]{:S(2)}) copy-start(s32[5]{0:T(128)S(1)} %iota_multiply_fusion) | copy-start | bytes 64
  14.9 6.3 %collective-permute-start.1 = (bf16[512,128]{1,0:T(8,128)(2,1)S(1)}, bf16[512,128]{1,0:T(8,128)(2,1)S(1)}, u32[]{:S(2)}, u32[]{:S(2)}) collective-permute-start(bf16[512,128]{1,0:T(8,128)(2,1)S(1)} %copy-done.50), channel_id=1, source_target_pairs={{0,2},{1,3},{2,0},{3,1},{4,6},{5,7},{6,4},{7,5},{8,10},{9,11},{10,... | collective-permute-start | bytes 393224 | tf_op jit(solution)/shard_map/ppermute | solution.py:320
  16.5 7.4 %collective-permute-start.2 = (bf16[512,128]{1,0:T(8,128)(2,1)S(1)}, bf16[512,128]{1,0:T(8,128)(2,1)S(1)}, u32[]{:S(2)}, u32[]{:S(2)}) collective-permute-start(bf16[512,128]{1,0:T(8,128)(2,1)S(1)} %copy-done.50), channel_id=1, source_target_pairs={{0,3},{1,2},{2,1},{3,0},{4,7},{5,6},{6,5},{7,4},{8,11},{9,10},{10,... | collective-permute-start | bytes 393224 | tf_op jit(solution)/shard_map/ppermute | solution.py:320
  17.0 17.3 %copy-start.51 = (bf16[512,128]{1,0:T(8,128)(2,1)}, bf16[512,128]{1,0:T(8,128)(2,1)S(1)}, u32[]{:S(2)}) copy-start(bf16[512,128]{1,0:T(8,128)(2,1)S(1)} %collective-permute-done.3.refs_4_) | copy-start | bytes 393220
  17.0 13.8 %collective-permute-start.4 = (bf16[512,128]{1,0:T(8,128)(2,1)S(1)}, bf16[512,128]{1,0:T(8,128)(2,1)S(1)}, u32[]{:S(2)}, u32[]{:S(2)}) collective-permute-start(bf16[512,128]{1,0:T(8,128)(2,1)S(1)} %collective-permute-done.3.refs_4_), channel_id=1, source_target_pairs={{0,1},{1,0},{2,3},{3,2},{4,5},{5,4},{6,7},{7,6},{8,9},{9,8},{10,11... | collective-permute-start | bytes 393224 | tf_op jit(solution)/shard_map/ppermute | solution.py:320
  18.6 13.8 %collective-permute-start.5 = (bf16[512,128]{1,0:T(8,128)(2,1)S(1)}, bf16[512,128]{1,0:T(8,128)(2,1)S(1)}, u32[]{:S(2)}, u32[]{:S(2)}) collective-permute-start(bf16[512,128]{1,0:T(8,128)(2,1)S(1)} %collective-permute-done.3.refs_4_), channel_id=1, source_target_pairs={{0,2},{1,3},{2,0},{3,1},{4,6},{5,7},{6,4},{7,5},{8,10},{9,11},{10,... | collective-permute-start | bytes 393224 | tf_op jit(solution)/shard_map/ppermute | solution.py:320
  20.1 14.2 %collective-permute-start.6 = (bf16[512,128]{1,0:T(8,128)(2,1)S(1)}, bf16[512,128]{1,0:T(8,128)(2,1)S(1)}, u32[]{:S(2)}, u32[]{:S(2)}) collective-permute-start(bf16[512,128]{1,0:T(8,128)(2,1)S(1)} %collective-permute-done.3.refs_4_), channel_id=1, source_target_pairs={{0,3},{1,2},{2,1},{3,0},{4,7},{5,6},{6,5},{7,4},{8,11},{9,10},{10,... | collective-permute-start | bytes 393224 | tf_op jit(solution)/shard_map/ppermute | solution.py:320
  21.3 22.0 %collective-permute-start.13 = (bf16[576,256]{1,0:T(8,128)(2,1)S(1)}, bf16[576,256]{1,0:T(8,128)(2,1)S(1)}, u32[]{:S(2)}, u32[]{:S(2)}) collective-permute-start(bf16[576,256]{1,0:T(8,128)(2,1)S(1)} %pad_maximum_fusion), channel_id=1, source_target_pairs={{0,4},{1,5},{2,6},{3,7},{4,0},{5,1},{6,2},{7,3},{8,12},{9,13},{10,... | collective-permute-start | bytes 884744 | tf_op jit(solution)/shard_map/ppermute | solution.py:320
  23.9 19.9 %collective-permute-start.14 = (bf16[576,256]{1,0:T(8,128)(2,1)S(1)}, bf16[576,256]{1,0:T(8,128)(2,1)S(1)}, u32[]{:S(2)}, u32[]{:S(2)}) collective-permute-start(bf16[576,256]{1,0:T(8,128)(2,1)S(1)} %pad_maximum_fusion), channel_id=1, source_target_pairs={{0,1},{1,0},{2,3},{3,2},{4,5},{5,4},{6,7},{7,6},{8,9},{9,8},{10,11... | collective-permute-start | bytes 884744 | tf_op jit(solution)/shard_map/ppermute | solution.py:320
  30.8 14.7 %collective-permute-start.15 = (bf16[576,256]{1,0:T(8,128)(2,1)S(1)}, bf16[576,256]{1,0:T(8,128)(2,1)S(1)}, u32[]{:S(2)}, u32[]{:S(2)}) collective-permute-start(bf16[576,256]{1,0:T(8,128)(2,1)S(1)} %pad_maximum_fusion), channel_id=1, source_target_pairs={{0,2},{1,3},{2,0},{3,1},{4,6},{5,7},{6,4},{7,5},{8,10},{9,11},{10,... | collective-permute-start | bytes 884744 | tf_op jit(solution)/shard_map/ppermute | solution.py:320
  32.3 16.4 %collective-permute-start.16 = (bf16[576,256]{1,0:T(8,128)(2,1)S(1)}, bf16[576,256]{1,0:T(8,128)(2,1)S(1)}, u32[]{:S(2)}, u32[]{:S(2)}) collective-permute-start(bf16[576,256]{1,0:T(8,128)(2,1)S(1)} %pad_maximum_fusion), channel_id=1, source_target_pairs={{0,3},{1,2},{2,1},{3,0},{4,7},{5,6},{6,5},{7,4},{8,11},{9,10},{10,... | collective-permute-start | bytes 884744 | tf_op jit(solution)/shard_map/ppermute | solution.py:320
  38.6 11.1 %collective-permute-start.20 = (bf16[512,256]{1,0:T(8,128)(2,1)}, bf16[512,256]{1,0:T(8,128)(2,1)S(1)}, u32[]{:S(2)}, u32[]{:S(2)}) collective-permute-start(bf16[512,256]{1,0:T(8,128)(2,1)} %get-tuple-element.51.refs_11_), channel_id=1, source_target_pairs={{0,16},{8,24},{16,0},{24,8},{1,17},{9,25},{17,1},{25,9},{2,18},{10... | collective-permute-start | bytes 786440 | tf_op jit(solution)/shard_map/ppermute | solution.py:320
  43.2 10.3 %collective-permute-start.8 = (bf16[512,256]{1,0:T(8,128)(2,1)S(1)}, bf16[512,256]{1,0:T(8,128)(2,1)S(1)}, u32[]{:S(2)}, u32[]{:S(2)}) collective-permute-start(bf16[512,256]{1,0:T(8,128)(2,1)S(1)} %copy-done.31), channel_id=1, source_target_pairs={{0,16},{8,24},{16,0},{24,8},{1,17},{9,25},{17,1},{25,9},{2,18},{10... | collective-permute-start | bytes 786440 | tf_op jit(solution)/shard_map/ppermute | solution.py:320
  43.9 13.5 %collective-permute-start.22 = (bf16[512,256]{1,0:T(8,128)(2,1)}, bf16[512,256]{1,0:T(8,128)(2,1)S(1)}, u32[]{:S(2)}, u32[]{:S(2)}) collective-permute-start(bf16[512,256]{1,0:T(8,128)(2,1)} %shard_map.47.refs_2_), channel_id=1, source_target_pairs={{0,16},{8,24},{16,0},{24,8},{1,17},{9,25},{17,1},{25,9},{2,18},{10... | collective-permute-start | bytes 786440 | tf_op jit(solution)/shard_map/ppermute | solution.py:320
  45.4 11.9 %collective-permute-start.17 = (bf16[576,256]{1,0:T(8,128)(2,1)S(1)}, bf16[576,256]{1,0:T(8,128)(2,1)S(1)}, u32[]{:S(2)}, u32[]{:S(2)}) collective-permute-start(bf16[576,256]{1,0:T(8,128)(2,1)S(1)} %collective-permute-done.13), channel_id=1, source_target_pairs={{0,1},{1,0},{2,3},{3,2},{4,5},{5,4},{6,7},{7,6},{8,9},{9,8},{10,11... | collective-permute-start | bytes 884744 | tf_op jit(solution)/shard_map/ppermute | solution.py:320
  48.8 10.0 %collective-permute-start.18 = (bf16[576,256]{1,0:T(8,128)(2,1)S(1)}, bf16[576,256]{1,0:T(8,128)(2,1)S(1)}, u32[]{:S(2)}, u32[]{:S(2)}) collective-permute-start(bf16[576,256]{1,0:T(8,128)(2,1)S(1)} %collective-permute-done.13), channel_id=1, source_target_pairs={{0,2},{1,3},{2,0},{3,1},{4,6},{5,7},{6,4},{7,5},{8,10},{9,11},{10,... | collective-permute-start | bytes 884744 | tf_op jit(solution)/shard_map/ppermute | solution.py:320
  49.7 13.8 %collective-permute-start.19 = (bf16[576,256]{1,0:T(8,128)(2,1)S(1)}, bf16[576,256]{1,0:T(8,128)(2,1)S(1)}, u32[]{:S(2)}, u32[]{:S(2)}) collective-permute-start(bf16[576,256]{1,0:T(8,128)(2,1)S(1)} %collective-permute-done.13), channel_id=1, source_target_pairs={{0,3},{1,2},{2,1},{3,0},{4,7},{5,6},{6,5},{7,4},{8,11},{9,10},{10,... | collective-permute-start | bytes 884744 | tf_op jit(solution)/shard_map/ppermute | solution.py:320
  53.5 10.1 %collective-permute-start.21 = (bf16[512,256]{1,0:T(8,128)(2,1)S(1)}, bf16[512,256]{1,0:T(8,128)(2,1)S(1)}, u32[]{:S(2)}, u32[]{:S(2)}) collective-permute-start(bf16[512,256]{1,0:T(8,128)(2,1)S(1)} %collective-permute-done.20.refs_13_), channel_id=1, source_target_pairs={{0,8},{8,0},{16,24},{24,16},{1,9},{9,1},{17,25},{25,17},{2,10},{10... | collective-permute-start | bytes 786440 | tf_op jit(solution)/shard_map/ppermute | solution.py:320
  57.4 6.2 %collective-permute-start.9 = (bf16[512,256]{1,0:T(8,128)(2,1)S(1)}, bf16[512,256]{1,0:T(8,128)(2,1)S(1)}, u32[]{:S(2)}, u32[]{:S(2)}) collective-permute-start(bf16[512,256]{1,0:T(8,128)(2,1)S(1)} %collective-permute-done.8.refs_4_), channel_id=1, source_target_pairs={{0,8},{8,0},{16,24},{24,16},{1,9},{9,1},{17,25},{25,17},{2,10},{10... | collective-permute-start | bytes 786440 | tf_op jit(solution)/shard_map/ppermute | solution.py:320
  57.4 6.2 %collective-permute-start.23 = (bf16[512,256]{1,0:T(8,128)(2,1)S(1)}, bf16[512,256]{1,0:T(8,128)(2,1)S(1)}, u32[]{:S(2)}, u32[]{:S(2)}) collective-permute-start(bf16[512,256]{1,0:T(8,128)(2,1)S(1)} %collective-permute-done.22.refs_4_), channel_id=1, source_target_pairs={{0,8},{8,0},{16,24},{24,16},{1,9},{9,1},{17,25},{25,17},{2,10},{10... | collective-permute-start | bytes 786440 | tf_op jit(solution)/shard_map/ppermute | solution.py:320
  63.6 24.0 %copy-start.27 = (bf16[512,256]{1,0:T(8,128)(2,1)}, bf16[512,256]{1,0:T(8,128)(2,1)S(1)}, u32[]{:S(2)}) copy-start(bf16[512,256]{1,0:T(8,128)(2,1)S(1)} %collective-permute-done.21.refs_14_) | copy-start | bytes 786436
  63.6 24.0 %copy-start.36 = (bf16[512,256]{1,0:T(8,128)(2,1)}, bf16[512,256]{1,0:T(8,128)(2,1)S(1)}, u32[]{:S(2)}) copy-start(bf16[512,256]{1,0:T(8,128)(2,1)S(1)} %collective-permute-done.9.refs_5_) | copy-start | bytes 786436
  63.8 23.8 %copy-start.4 = (bf16[576,256]{1,0:T(8,128)(2,1)}, bf16[576,256]{1,0:T(8,128)(2,1)S(1)}, u32[]{:S(2)}) copy-start(bf16[576,256]{1,0:T(8,128)(2,1)S(1)} %get-tuple-element.53.refs_6_.refs_10_) | copy-start | bytes 884740
  63.8 26.7 %copy-start.3 = (bf16[576,256]{1,0:T(8,128)(2,1)}, bf16[576,256]{1,0:T(8,128)(2,1)S(1)}, u32[]{:S(2)}) copy-start(bf16[576,256]{1,0:T(8,128)(2,1)S(1)} %get-tuple-element.64.refs_6_.refs_10_) | copy-start | bytes 884740
  63.8 47.7 %copy-start.2 = (bf16[576,256]{1,0:T(8,128)(2,1)}, bf16[576,256]{1,0:T(8,128)(2,1)S(1)}, u32[]{:S(2)}) copy-start(bf16[576,256]{1,0:T(8,128)(2,1)S(1)} %get-tuple-element.77.refs_6_.refs_10_) | copy-start | bytes 884740
  63.8 67.7 %copy-start.1 = (bf16[576,256]{1,0:T(8,128)(2,1)}, bf16[576,256]{1,0:T(8,128)(2,1)S(1)}, u32[]{:S(2)}) copy-start(bf16[576,256]{1,0:T(8,128)(2,1)S(1)} %get-tuple-element.73.refs_6_.refs_10_) | copy-start | bytes 884740
  63.8 7.4 %collective-permute-start.24 = (bf16[576,256]{1,0:T(8,128)(2,1)S(1)}, bf16[576,256]{1,0:T(8,128)(2,1)S(1)}, u32[]{:S(2)}, u32[]{:S(2)}) collective-permute-start(bf16[576,256]{1,0:T(8,128)(2,1)S(1)} %get-tuple-element.94.refs_6_.refs_10_), channel_id=1, source_target_pairs={{0,16},{8,24},{16,0},{24,8},{1,17},{9,25},{17,1},{25,9},{2,18},{10... | collective-permute-start | bytes 884744 | tf_op jit(solution)/shard_map/ppermute | solution.py:320
  71.2 1.6 collective-permute-start.25
  71.2 2.9 %collective-permute-start.29 = (bf16[576,256]{1,0:T(8,128)(2,1)S(1)}, bf16[576,256]{1,0:T(8,128)(2,1)S(1)}, u32[]{:S(2)}, u32[]{:S(2)}) collective-permute-start(bf16[576,256]{1,0:T(8,128)(2,1)S(1)} %get-tuple-element.94.refs_6_.refs_10_), channel_id=1, source_target_pairs={{0,8},{8,0},{16,24},{24,16},{1,9},{9,1},{17,25},{25,17},{2,10},{10... | collective-permute-start | bytes 884744 | tf_op jit(solution)/shard_map/ppermute | solution.py:320
  71.7 2.3 %collective-permute-start.28 = (bf16[512,256]{1,0:T(8,128)(2,1)S(1)}, bf16[512,256]{1,0:T(8,128)(2,1)S(1)}, u32[]{:S(2)}, u32[]{:S(2)}) collective-permute-start(bf16[512,256]{1,0:T(8,128)(2,1)S(1)} %copy-done.35), channel_id=1, source_target_pairs={{0,8},{8,0},{16,24},{24,16},{1,9},{9,1},{17,25},{25,17},{2,10},{10... | collective-permute-start | bytes 786440 | tf_op jit(solution)/shard_map/ppermute | solution.py:320
  71.7 16.5 %collective-permute-start.33 = (bf16[512,256]{1,0:T(8,128)(2,1)S(1)}, bf16[512,256]{1,0:T(8,128)(2,1)S(1)}, u32[]{:S(2)}, u32[]{:S(2)}) collective-permute-start(bf16[512,256]{1,0:T(8,128)(2,1)S(1)} %get-tuple-element.56.refs_15_), channel_id=1, source_target_pairs={{0,16},{8,24},{16,0},{24,8},{1,17},{9,25},{17,1},{25,9},{2,18},{10... | collective-permute-start | bytes 786440 | tf_op jit(solution)/shard_map/ppermute | solution.py:320
  72.4 15.9 %collective-permute-start.32 = (bf16[512,256]{1,0:T(8,128)(2,1)S(1)}, bf16[512,256]{1,0:T(8,128)(2,1)S(1)}, u32[]{:S(2)}, u32[]{:S(2)}) collective-permute-start(bf16[512,256]{1,0:T(8,128)(2,1)S(1)} %get-tuple-element.56.refs_15_), channel_id=1, source_target_pairs={{0,8},{8,0},{16,24},{24,16},{1,9},{9,1},{17,25},{25,17},{2,10},{10... | collective-permute-start | bytes 786440 | tf_op jit(solution)/shard_map/ppermute | solution.py:320
  72.8 17.7 %copy-start.28 = (bf16[512,256]{1,0:T(8,128)(2,1)S(1)}, bf16[512,256]{1,0:T(8,128)(2,1)}, u32[]{:S(2)}) copy-start(bf16[512,256]{1,0:T(8,128)(2,1)} %get-tuple-element.62.refs_2_) | copy-start | bytes 786436
  72.8 14.8 %collective-permute-start.27 = (bf16[576,256]{1,0:T(8,128)(2,1)S(1)}, bf16[576,256]{1,0:T(8,128)(2,1)S(1)}, u32[]{:S(2)}, u32[]{:S(2)}) collective-permute-start(bf16[576,256]{1,0:T(8,128)(2,1)S(1)} %get-tuple-element.53.refs_6_.refs_10_), channel_id=1, source_target_pairs={{0,16},{8,24},{16,0},{24,8},{1,17},{9,25},{17,1},{25,9},{2,18},{10... | collective-permute-start | bytes 884744 | tf_op jit(solution)/shard_map/ppermute | solution.py:320
  74.1 17.8 %collective-permute-start.26 = (bf16[576,256]{1,0:T(8,128)(2,1)S(1)}, bf16[576,256]{1,0:T(8,128)(2,1)S(1)}, u32[]{:S(2)}, u32[]{:S(2)}) collective-permute-start(bf16[576,256]{1,0:T(8,128)(2,1)S(1)} %get-tuple-element.53.refs_6_.refs_10_), channel_id=1, source_target_pairs={{0,8},{8,0},{16,24},{24,16},{1,9},{9,1},{17,25},{25,17},{2,10},{10... | collective-permute-start | bytes 884744 | tf_op jit(solution)/shard_map/ppermute | solution.py:320
  87.7 4.2 %collective-permute-start.30 = (bf16[576,256]{1,0:T(8,128)(2,1)S(1)}, bf16[576,256]{1,0:T(8,128)(2,1)S(1)}, u32[]{:S(2)}, u32[]{:S(2)}) collective-permute-start(bf16[576,256]{1,0:T(8,128)(2,1)S(1)} %collective-permute-done.27.refs_8_), channel_id=1, source_target_pairs={{0,8},{8,0},{16,24},{24,16},{1,9},{9,1},{17,25},{25,17},{2,10},{10... | collective-permute-start | bytes 884744 | tf_op jit(solution)/shard_map/ppermute | solution.py:320
  87.8 1.9 %collective-permute-start.31 = (bf16[512,256]{1,0:T(8,128)(2,1)S(1)}, bf16[512,256]{1,0:T(8,128)(2,1)S(1)}, u32[]{:S(2)}, u32[]{:S(2)}) collective-permute-start(bf16[512,256]{1,0:T(8,128)(2,1)S(1)} %copy-done.24), channel_id=1, source_target_pairs={{0,8},{8,0},{16,24},{24,16},{1,9},{9,1},{17,25},{25,17},{2,10},{10... | collective-permute-start | bytes 786440 | tf_op jit(solution)/shard_map/ppermute | solution.py:320
  88.3 2.2 %collective-permute-start.7 = (bf16[512,256]{1,0:T(8,128)(2,1)S(1)}, bf16[512,256]{1,0:T(8,128)(2,1)S(1)}, u32[]{:S(2)}, u32[]{:S(2)}) collective-permute-start(bf16[512,256]{1,0:T(8,128)(2,1)S(1)} %copy-done.31), channel_id=1, source_target_pairs={{0,8},{8,0},{16,24},{24,16},{1,9},{9,1},{17,25},{25,17},{2,10},{10... | collective-permute-start | bytes 786440 | tf_op jit(solution)/shard_map/ppermute | solution.py:320
  88.3 2.2 %collective-permute-start.34 = (bf16[512,256]{1,0:T(8,128)(2,1)S(1)}, bf16[512,256]{1,0:T(8,128)(2,1)S(1)}, u32[]{:S(2)}, u32[]{:S(2)}) collective-permute-start(bf16[512,256]{1,0:T(8,128)(2,1)S(1)} %collective-permute-done.33.refs_17_), channel_id=1, source_target_pairs={{0,8},{8,0},{16,24},{24,16},{1,9},{9,1},{17,25},{25,17},{2,10},{10... | collective-permute-start | bytes 786440 | tf_op jit(solution)/shard_map/ppermute | solution.py:320
  89.7 19.0 %collective-permute-start.41 = (bf16[576,256]{1,0:T(8,128)(2,1)S(1)}, bf16[576,256]{1,0:T(8,128)(2,1)S(1)}, u32[]{:S(2)}, u32[]{:S(2)}) collective-permute-start(bf16[576,256]{1,0:T(8,128)(2,1)S(1)} %get-tuple-element.64.refs_6_.refs_10_), channel_id=1, source_target_pairs={{0,16},{8,24},{16,0},{24,8},{1,17},{9,25},{17,1},{25,9},{2,18},{10... | collective-permute-start | bytes 884744 | tf_op jit(solution)/shard_map/ppermute | solution.py:320
  90.5 21.0 %collective-permute-start.40 = (bf16[576,256]{1,0:T(8,128)(2,1)S(1)}, bf16[576,256]{1,0:T(8,128)(2,1)S(1)}, u32[]{:S(2)}, u32[]{:S(2)}) collective-permute-start(bf16[576,256]{1,0:T(8,128)(2,1)S(1)} %get-tuple-element.64.refs_6_.refs_10_), channel_id=1, source_target_pairs={{0,8},{8,0},{16,24},{24,16},{1,9},{9,1},{17,25},{25,17},{2,10},{10... | collective-permute-start | bytes 884744 | tf_op jit(solution)/shard_map/ppermute | solution.py:320
  90.6 18.7 %collective-permute-start.38 = (bf16[512,256]{1,0:T(8,128)(2,1)S(1)}, bf16[512,256]{1,0:T(8,128)(2,1)S(1)}, u32[]{:S(2)}, u32[]{:S(2)}) collective-permute-start(bf16[512,256]{1,0:T(8,128)(2,1)S(1)} %copy-done.28), channel_id=1, source_target_pairs={{0,16},{8,24},{16,0},{24,8},{1,17},{9,25},{17,1},{25,9},{2,18},{10... | collective-permute-start | bytes 786440 | tf_op jit(solution)/shard_map/ppermute | solution.py:320
  108.7 2.9 %collective-permute-start.42 = (bf16[576,256]{1,0:T(8,128)(2,1)S(1)}, bf16[576,256]{1,0:T(8,128)(2,1)S(1)}, u32[]{:S(2)}, u32[]{:S(2)}) collective-permute-start(bf16[576,256]{1,0:T(8,128)(2,1)S(1)} %collective-permute-done.41.refs_8_), channel_id=1, source_target_pairs={{0,8},{8,0},{16,24},{24,16},{1,9},{9,1},{17,25},{25,17},{2,10},{10... | collective-permute-start | bytes 884744 | tf_op jit(solution)/shard_map/ppermute | solution.py:320
  109.0 1.8 %collective-permute-start.37 = (bf16[512,256]{1,0:T(8,128)(2,1)S(1)}, bf16[512,256]{1,0:T(8,128)(2,1)S(1)}, u32[]{:S(2)}, u32[]{:S(2)}) collective-permute-start(bf16[512,256]{1,0:T(8,128)(2,1)S(1)} %copy-done.28), channel_id=1, source_target_pairs={{0,8},{8,0},{16,24},{24,16},{1,9},{9,1},{17,25},{25,17},{2,10},{10... | collective-permute-start | bytes 786440 | tf_op jit(solution)/shard_map/ppermute | solution.py:320
  109.3 2.3 %collective-permute-start.39 = (bf16[512,256]{1,0:T(8,128)(2,1)S(1)}, bf16[512,256]{1,0:T(8,128)(2,1)S(1)}, u32[]{:S(2)}, u32[]{:S(2)}) collective-permute-start(bf16[512,256]{1,0:T(8,128)(2,1)S(1)} %collective-permute-done.38.refs_4_), channel_id=1, source_target_pairs={{0,8},{8,0},{16,24},{24,16},{1,9},{9,1},{17,25},{25,17},{2,10},{10... | collective-permute-start | bytes 786440 | tf_op jit(solution)/shard_map/ppermute | solution.py:320
  109.5 19.3 %collective-permute-start.47 = (bf16[512,256]{1,0:T(8,128)(2,1)S(1)}, bf16[512,256]{1,0:T(8,128)(2,1)S(1)}, u32[]{:S(2)}, u32[]{:S(2)}) collective-permute-start(bf16[512,256]{1,0:T(8,128)(2,1)S(1)} %copy-done.26), channel_id=1, source_target_pairs={{0,16},{8,24},{16,0},{24,8},{1,17},{9,25},{17,1},{25,9},{2,18},{10... | collective-permute-start | bytes 786440 | tf_op jit(solution)/shard_map/ppermute | solution.py:320
  110.7 17.3 %collective-permute-start.50 = (bf16[576,256]{1,0:T(8,128)(2,1)S(1)}, bf16[576,256]{1,0:T(8,128)(2,1)S(1)}, u32[]{:S(2)}, u32[]{:S(2)}) collective-permute-start(bf16[576,256]{1,0:T(8,128)(2,1)S(1)} %get-tuple-element.77.refs_6_.refs_10_), channel_id=1, source_target_pairs={{0,16},{8,24},{16,0},{24,8},{1,17},{9,25},{17,1},{25,9},{2,18},{10... | collective-permute-start | bytes 884744 | tf_op jit(solution)/shard_map/ppermute | solution.py:320
  111.5 20.1 %collective-permute-start.49 = (bf16[576,256]{1,0:T(8,128)(2,1)S(1)}, bf16[576,256]{1,0:T(8,128)(2,1)S(1)}, u32[]{:S(2)}, u32[]{:S(2)}) collective-permute-start(bf16[576,256]{1,0:T(8,128)(2,1)S(1)} %get-tuple-element.77.refs_6_.refs_10_), channel_id=1, source_target_pairs={{0,8},{8,0},{16,24},{24,16},{1,9},{9,1},{17,25},{25,17},{2,10},{10... | collective-permute-start | bytes 884744 | tf_op jit(solution)/shard_map/ppermute | solution.py:320
  112.4 16.7 %copy-start.23 = (bf16[512,256]{1,0:T(8,128)(2,1)S(1)}, bf16[512,256]{1,0:T(8,128)(2,1)}, u32[]{:S(2)}) copy-start(bf16[512,256]{1,0:T(8,128)(2,1)} %get-tuple-element.60.refs_2_) | copy-start | bytes 786436
  128.1 3.6 %collective-permute-start.51 = (bf16[576,256]{1,0:T(8,128)(2,1)S(1)}, bf16[576,256]{1,0:T(8,128)(2,1)S(1)}, u32[]{:S(2)}, u32[]{:S(2)}) collective-permute-start(bf16[576,256]{1,0:T(8,128)(2,1)S(1)} %collective-permute-done.50.refs_8_), channel_id=1, source_target_pairs={{0,8},{8,0},{16,24},{24,16},{1,9},{9,1},{17,25},{25,17},{2,10},{10... | collective-permute-start | bytes 884744 | tf_op jit(solution)/shard_map/ppermute | solution.py:320
  128.7 1.8 %collective-permute-start.46 = (bf16[512,256]{1,0:T(8,128)(2,1)S(1)}, bf16[512,256]{1,0:T(8,128)(2,1)S(1)}, u32[]{:S(2)}, u32[]{:S(2)}) collective-permute-start(bf16[512,256]{1,0:T(8,128)(2,1)S(1)} %copy-done.26), channel_id=1, source_target_pairs={{0,8},{8,0},{16,24},{24,16},{1,9},{9,1},{17,25},{25,17},{2,10},{10... | collective-permute-start | bytes 786440 | tf_op jit(solution)/shard_map/ppermute | solution.py:320
  128.7 2.8 %collective-permute-start.48 = (bf16[512,256]{1,0:T(8,128)(2,1)S(1)}, bf16[512,256]{1,0:T(8,128)(2,1)S(1)}, u32[]{:S(2)}, u32[]{:S(2)}) collective-permute-start(bf16[512,256]{1,0:T(8,128)(2,1)S(1)} %collective-permute-done.47.refs_4_), channel_id=1, source_target_pairs={{0,8},{8,0},{16,24},{24,16},{1,9},{9,1},{17,25},{25,17},{2,10},{10... | collective-permute-start | bytes 786440 | tf_op jit(solution)/shard_map/ppermute | solution.py:320
  129.2 19.3 %collective-permute-start.36 = (bf16[512,256]{1,0:T(8,128)(2,1)S(1)}, bf16[512,256]{1,0:T(8,128)(2,1)S(1)}, u32[]{:S(2)}, u32[]{:S(2)}) collective-permute-start(bf16[512,256]{1,0:T(8,128)(2,1)S(1)} %copy-done.23), channel_id=1, source_target_pairs={{0,16},{8,24},{16,0},{24,8},{1,17},{9,25},{17,1},{25,9},{2,18},{10... | collective-permute-start | bytes 786440 | tf_op jit(solution)/shard_map/ppermute | solution.py:320
  130.4 17.5 %collective-permute-start.45 = (bf16[576,256]{1,0:T(8,128)(2,1)S(1)}, bf16[576,256]{1,0:T(8,128)(2,1)S(1)}, u32[]{:S(2)}, u32[]{:S(2)}) collective-permute-start(bf16[576,256]{1,0:T(8,128)(2,1)S(1)} %get-tuple-element.73.refs_6_.refs_10_), channel_id=1, source_target_pairs={{0,16},{8,24},{16,0},{24,8},{1,17},{9,25},{17,1},{25,9},{2,18},{10... | collective-permute-start | bytes 884744 | tf_op jit(solution)/shard_map/ppermute | solution.py:320
  131.5 18.9 %collective-permute-start.44 = (bf16[576,256]{1,0:T(8,128)(2,1)S(1)}, bf16[576,256]{1,0:T(8,128)(2,1)S(1)}, u32[]{:S(2)}, u32[]{:S(2)}) collective-permute-start(bf16[576,256]{1,0:T(8,128)(2,1)S(1)} %get-tuple-element.73.refs_6_.refs_10_), channel_id=1, source_target_pairs={{0,8},{8,0},{16,24},{24,16},{1,9},{9,1},{17,25},{25,17},{2,10},{10... | collective-permute-start | bytes 884744 | tf_op jit(solution)/shard_map/ppermute | solution.py:320
  147.9 2.5 %collective-permute-start.52 = (bf16[576,256]{1,0:T(8,128)(2,1)S(1)}, bf16[576,256]{1,0:T(8,128)(2,1)S(1)}, u32[]{:S(2)}, u32[]{:S(2)}) collective-permute-start(bf16[576,256]{1,0:T(8,128)(2,1)S(1)} %collective-permute-done.45.refs_8_), channel_id=1, source_target_pairs={{0,8},{8,0},{16,24},{24,16},{1,9},{9,1},{17,25},{25,17},{2,10},{10... | collective-permute-start | bytes 884744 | tf_op jit(solution)/shard_map/ppermute | solution.py:320
  148.4 1.6 collective-permute-start.35
  148.5 1.9 %collective-permute-start.43 = (bf16[512,256]{1,0:T(8,128)(2,1)S(1)}, bf16[512,256]{1,0:T(8,128)(2,1)S(1)}, u32[]{:S(2)}, u32[]{:S(2)}) collective-permute-start(bf16[512,256]{1,0:T(8,128)(2,1)S(1)} %collective-permute-done.36.refs_4_), channel_id=1, source_target_pairs={{0,8},{8,0},{16,24},{24,16},{1,9},{9,1},{17,25},{25,17},{2,10},{10... | collective-permute-start | bytes 786440 | tf_op jit(solution)/shard_map/ppermute | solution.py:320
  (48 other events, 229.1 us)
where the time goes:
time: 169 us
  Pallas kernels  83.3 us (49%)
  starting transfers between devices  43.9 us (26%)
  waiting for transfers between devices  27.7 us (16%)
  local copies, waits for them, and re-layouts  8.92 us (5%)
  other arithmetic  4.11 us (2%)
    pallas_call x5, Pallas kernels, per_device(): pl.pallas_call(functools.partial(step_kernel, step, leaf_count, spots), i...  76.5 us
    ppermute x53, starting transfers between devices, flip(): return lax.ppermute(value, axis, [(i, i ^ bits) for i in range(count)])  43.9 us
    ppermute x53, waiting for transfers between devices, flip(): return lax.ppermute(value, axis, [(i, i ^ bits) for i in range(count)])  27.7 us
    pallas_call x2, Pallas kernels, select(): pl.pallas_call(select_kernel, in_specs=[SMEM_SPEC, SMEM_SPEC, VMEM_SPEC]...  6.74 us
    unnamed x119, local copies, waits for them, and re-layouts  5.93 us
  transfers between devices with their start and end apart: 53, of which 14 were waited for; matrix products, arithmetic and copies ran while one was open for 5% of the time, Pallas kernels for 39%

commit v1 on v0

--- a/solution.py
+++ b/solution.py
@@ -363,7 +363,10 @@
     tiles = device_rows // tile_width
     child = leaf // half_leaf
     small = leaf_count == 4 and panel_count == 8
-    params = pltpu.CompilerParams(vmem_limit_bytes=56 * 2**20)
+    params = pltpu.CompilerParams(vmem_limit_bytes=(20 if small else 56) * 2**20)
+
+    def near(x):
+        return pltpu.with_memory_space_constraint(x, pltpu.VMEM) if small else x
 
     high = lax.reduce_precision(root_entries, 8, 7)
     offset = panel * PANEL % device_rows
@@ -494,7 +497,7 @@
             cost_estimate=pl.CostEstimate(
                 flops=15 * 10**9, transcendentals=0, bytes_accessed=4 * 2**20
             ),
-        )(place, row_map, *args)
+        )(place, row_map, *[near(x) for x in args])
         if last:
             return out[0]
         xa.append(out[0])

time: 169 us -> 149 us (0.88)
  Pallas kernels: 83.3 us -> 64.6 us
  waiting for transfers between devices: 27.7 us -> 36.6 us
  local copies, waits for them, and re-layouts: 8.92 us -> 2.45 us
  other arithmetic: 4.11 us -> 2.33 us
  starting transfers between devices: 43.9 us -> 42.2 us
    pallas_call x5, Pallas kernels: 76.5 us -> 61.4 us  [per_device(): pl.pallas_call(functools.partial(step_kernel, step, leaf_count, spots), i...]
    ppermute x53, waiting for transfers between devices: 27.7 us -> 36.6 us  [flip(): return lax.ppermute(value, axis, [(i, i ^ bits) for i in range(count)])]
    unnamed x119 -> x9, local copies, waits for them, and re-layouts: 5.93 us -> 0.03 us
    pallas_call x2, Pallas kernels: 6.74 us -> 3.22 us  [select(): pl.pallas_call(select_kernel, in_specs=[SMEM_SPEC, SMEM_SPEC, VMEM_SPEC]...]
    ppermute x53, starting transfers between devices: 43.9 us -> 42.2 us  [flip(): return lax.ppermute(value, axis, [(i, i ^ bits) for i in range(count)])]
  transfers between devices with their start and end apart: 53 -> 53, of which waited for: 14 -> 20; matrix products, arithmetic and copies ran while one was open for 5% -> 3% of each run, Pallas kernels for 39% -> 34%
where the time goes in v1:
time: 149 us
  Pallas kernels  64.6 us (43%)
  starting transfers between devices  42.2 us (28%)
  waiting for transfers between devices  36.6 us (25%)
  local copies, waits for them, and re-layouts  2.45 us (2%)
  other arithmetic  2.33 us (2%)
    pallas_call x5, Pallas kernels, per_device(): pl.pallas_call(functools.partial(step_kernel, step, leaf_count, spots), i...  61.4 us
    ppermute x53, starting transfers between devices, flip(): return lax.ppermute(value, axis, [(i, i ^ bits) for i in range(count)])  42.2 us
    ppermute x53, waiting for transfers between devices, flip(): return lax.ppermute(value, axis, [(i, i ^ bits) for i in range(count)])  36.6 us
    pallas_call x2, Pallas kernels, select(): pl.pallas_call(select_kernel, in_specs=[SMEM_SPEC, SMEM_SPEC, VMEM_SPEC]...  3.22 us
  transfers between devices with their start and end apart: 53, of which 20 were waited for; matrix products, arithmetic and copies ran while one was open for 3% of the time, Pallas kernels for 34%

profile of v1, /device:TPU:0, one launch (start us, length us, event | category | flops | bytes accessed | tf_op | source)
XLA Modules:
  0.0 148.6 jit_solution(10852668136528643712)
XLA Ops:
  0.0 4.1 %collective-permute-start.3 = (bf16[512,128]{1,0:T(8,128)(2,1)}, bf16[512,128]{1,0:T(8,128)(2,1)S(1)}, u32[]{:S(2)}, u32[]{:S(2)}) collective-permute-start(bf16[512,128]{1,0:T(8,128)(2,1)} %refs_0_.3), channel_id=1, source_target_pairs={{0,4},{1,5},{2,6},{3,7},{4,0},{5,1},{6,2},{7,3},{8,12},{9,13},{10,... | collective-permute-start | bytes 393224 | tf_op jit(solution)/shard_map/ppermute | solution.py:320
  4.1 1.5 %collective-permute-start = (bf16[512,128]{1,0:T(8,128)(2,1)}, bf16[512,128]{1,0:T(8,128)(2,1)S(1)}, u32[]{:S(2)}, u32[]{:S(2)}) collective-permute-start(bf16[512,128]{1,0:T(8,128)(2,1)} %refs_0_.3), channel_id=1, source_target_pairs={{0,1},{1,0},{2,3},{3,2},{4,5},{5,4},{6,7},{7,6},{8,9},{9,8},{10,11... | collective-permute-start | bytes 393224 | tf_op jit(solution)/shard_map/ppermute | solution.py:320
  5.6 1.1 reduce-precision_convert_fusion
  6.7 1.0 fusion
  7.7 0.5 collective-permute-start.10
  8.2 1.2 collective-permute-start.11
  9.4 0.3 collective-permute-start.12
  9.9 0.6 gather_fusion.1
  10.8 0.6 gather_fusion.2
  11.4 0.6 gather_fusion
  12.0 1.6 %collective-permute-start.1 = (bf16[512,128]{1,0:T(8,128)(2,1)S(1)}, bf16[512,128]{1,0:T(8,128)(2,1)S(1)}, u32[]{:S(2)}, u32[]{:S(2)}) collective-permute-start(bf16[512,128]{1,0:T(8,128)(2,1)S(1)} %copy-done.1), channel_id=1, source_target_pairs={{0,2},{1,3},{2,0},{3,1},{4,6},{5,7},{6,4},{7,5},{8,10},{9,11},{10,... | collective-permute-start | bytes 393224 | tf_op jit(solution)/shard_map/ppermute | solution.py:320
  13.7 0.4 collective-permute-start.2
  14.2 1.6 %collective-permute-start.4 = (bf16[512,128]{1,0:T(8,128)(2,1)S(1)}, bf16[512,128]{1,0:T(8,128)(2,1)S(1)}, u32[]{:S(2)}, u32[]{:S(2)}) collective-permute-start(bf16[512,128]{1,0:T(8,128)(2,1)S(1)} %collective-permute-done.3.refs_4_), channel_id=1, source_target_pairs={{0,1},{1,0},{2,3},{3,2},{4,5},{5,4},{6,7},{7,6},{8,9},{9,8},{10,11... | collective-permute-start | bytes 393224 | tf_op jit(solution)/shard_map/ppermute | solution.py:320
  15.7 1.6 %collective-permute-start.5 = (bf16[512,128]{1,0:T(8,128)(2,1)S(1)}, bf16[512,128]{1,0:T(8,128)(2,1)S(1)}, u32[]{:S(2)}, u32[]{:S(2)}) collective-permute-start(bf16[512,128]{1,0:T(8,128)(2,1)S(1)} %collective-permute-done.3.refs_4_), channel_id=1, source_target_pairs={{0,2},{1,3},{2,0},{3,1},{4,6},{5,7},{6,4},{7,5},{8,10},{9,11},{10,... | collective-permute-start | bytes 393224 | tf_op jit(solution)/shard_map/ppermute | solution.py:320
  17.3 0.4 collective-permute-start.6
  17.9 0.5 collective-permute-done.1.refs_2_
  18.4 0.3 collective-permute-start.13
  18.7 2.3 %collective-permute-done.2.refs_3_ = bf16[512,128]{1,0:T(8,128)(2,1)S(1)} collective-permute-done((bf16[512,128]{1,0:T(8,128)(2,1)S(1)}, bf16[512,128]{1,0:T(8,128)(2,1)S(1)}, u32[]{:S(2)}, u32[]{:S(2)}) %collective-permute-start.2) | collective-permute-done | bytes 131104 | tf_op jit(solution)/shard_map/ppermute | solution.py:320
  21.1 6.9 %collective-permute-start.14 = (bf16[576,256]{1,0:T(8,128)(2,1)S(1)}, bf16[576,256]{1,0:T(8,128)(2,1)S(1)}, u32[]{:S(2)}, u32[]{:S(2)}) collective-permute-start(bf16[576,256]{1,0:T(8,128)(2,1)S(1)} %pad_maximum_fusion), channel_id=1, source_target_pairs={{0,1},{1,0},{2,3},{3,2},{4,5},{5,4},{6,7},{7,6},{8,9},{9,8},{10,11... | collective-permute-start | bytes 884744 | tf_op jit(solution)/shard_map/ppermute | solution.py:320
  27.9 1.6 %collective-permute-done.5.refs_6_ = bf16[512,128]{1,0:T(8,128)(2,1)S(1)} collective-permute-done((bf16[512,128]{1,0:T(8,128)(2,1)S(1)}, bf16[512,128]{1,0:T(8,128)(2,1)S(1)}, u32[]{:S(2)}, u32[]{:S(2)}) %collective-permute-start.5) | collective-permute-done | bytes 131104 | tf_op jit(solution)/shard_map/ppermute | solution.py:320
  29.5 2.0 %collective-permute-done.6.refs_7_ = bf16[512,128]{1,0:T(8,128)(2,1)S(1)} collective-permute-done((bf16[512,128]{1,0:T(8,128)(2,1)S(1)}, bf16[512,128]{1,0:T(8,128)(2,1)S(1)}, u32[]{:S(2)}, u32[]{:S(2)}) %collective-permute-start.6) | collective-permute-done | bytes 131104 | tf_op jit(solution)/shard_map/ppermute | solution.py:320
  31.5 2.1 %shard_map.46 = (bf16[512,256]{1,0:T(8,128)(2,1)S(1)}, bf16[512,256]{1,0:T(8,128)(2,1)S(1)}, bf16[512,256]{1,0:T(8,128)(2,1)S(1)}, bf16[512,256]{1,0:T(8,128)(2,1)S(1)}, bf16[512,256]{1,0:T(8,128)(2,1)S(1)}) custom-call(s32[5]{0:T(128)S(1)} %pad_add_fusion.1.bases_ref, s32[4,8]{1,0:T(4,128)S(1)} %convert_bitcast_fusion.keep_ref, s32[1,1024]{1,0:T(1,128)S(1)} %bitcast.51, ...), custom_call_target="tpu_custom_call" | custom-call | flops 5000000000 | bytes 1048576 | tf_op jit(solution)/shard_map/pallas_call | solution.py:406
  33.7 1.5 %collective-permute-start.20 = (bf16[512,256]{1,0:T(8,128)(2,1)S(1)}, bf16[512,256]{1,0:T(8,128)(2,1)S(1)}, u32[]{:S(2)}, u32[]{:S(2)}) collective-permute-start(bf16[512,256]{1,0:T(8,128)(2,1)S(1)} %get-tuple-element.51.refs_11_), channel_id=1, source_target_pairs={{0,16},{8,24},{16,0},{24,8},{1,17},{9,25},{17,1},{25,9},{2,18},{10... | collective-permute-start | bytes 786440 | tf_op jit(solution)/shard_map/ppermute | solution.py:320
  35.2 1.1 shard_map.47.refs_2_
  36.3 0.6 collective-permute-start.8
  37.0 1.5 %collective-permute-start.22 = (bf16[512,256]{1,0:T(8,128)(2,1)S(1)}, bf16[512,256]{1,0:T(8,128)(2,1)S(1)}, u32[]{:S(2)}, u32[]{:S(2)}) collective-permute-start(bf16[512,256]{1,0:T(8,128)(2,1)S(1)} %shard_map.47.refs_2_), channel_id=1, source_target_pairs={{0,16},{8,24},{16,0},{24,8},{1,17},{9,25},{17,1},{25,9},{2,18},{10... | collective-permute-start | bytes 786440 | tf_op jit(solution)/shard_map/ppermute | solution.py:320
  38.5 1.0 collective-permute-done.15
  39.5 2.2 %collective-permute-start.17 = (bf16[576,256]{1,0:T(8,128)(2,1)S(1)}, bf16[576,256]{1,0:T(8,128)(2,1)S(1)}, u32[]{:S(2)}, u32[]{:S(2)}) collective-permute-start(bf16[576,256]{1,0:T(8,128)(2,1)S(1)} %collective-permute-done.13), channel_id=1, source_target_pairs={{0,1},{1,0},{2,3},{3,2},{4,5},{5,4},{6,7},{7,6},{8,9},{9,8},{10,11... | collective-permute-start | bytes 884744 | tf_op jit(solution)/shard_map/ppermute | solution.py:320
  41.8 3.4 %collective-permute-done.16 = bf16[576,256]{1,0:T(8,128)(2,1)S(1)} collective-permute-done((bf16[576,256]{1,0:T(8,128)(2,1)S(1)}, bf16[576,256]{1,0:T(8,128)(2,1)S(1)}, u32[]{:S(2)}, u32[]{:S(2)}) %collective-permute-start.16) | collective-permute-done | bytes 294944 | tf_op jit(solution)/shard_map/ppermute | solution.py:320
  45.2 1.6 %collective-permute-start.18 = (bf16[576,256]{1,0:T(8,128)(2,1)S(1)}, bf16[576,256]{1,0:T(8,128)(2,1)S(1)}, u32[]{:S(2)}, u32[]{:S(2)}) collective-permute-start(bf16[576,256]{1,0:T(8,128)(2,1)S(1)} %collective-permute-done.13), channel_id=1, source_target_pairs={{0,2},{1,3},{2,0},{3,1},{4,6},{5,7},{6,4},{7,5},{8,10},{9,11},{10,... | collective-permute-start | bytes 884744 | tf_op jit(solution)/shard_map/ppermute | solution.py:320
  46.9 1.4 collective-permute-start.19
  48.3 0.3 collective-permute-done.8.refs_4_
  48.6 3.7 %collective-permute-done.22.refs_4_ = bf16[512,256]{1,0:T(8,128)(2,1)S(1)} collective-permute-done((bf16[512,256]{1,0:T(8,128)(2,1)S(1)}, bf16[512,256]{1,0:T(8,128)(2,1)S(1)}, u32[]{:S(2)}, u32[]{:S(2)}) %collective-permute-start.22) | collective-permute-done | bytes 262176 | tf_op jit(solution)/shard_map/ppermute | solution.py:320
  52.3 0.5 collective-permute-start.23
  52.8 2.4 %collective-permute-done.18 = bf16[576,256]{1,0:T(8,128)(2,1)S(1)} collective-permute-done((bf16[576,256]{1,0:T(8,128)(2,1)S(1)}, bf16[576,256]{1,0:T(8,128)(2,1)S(1)}, u32[]{:S(2)}, u32[]{:S(2)}) %collective-permute-start.18) | collective-permute-done | bytes 294944 | tf_op jit(solution)/shard_map/ppermute | solution.py:320
  55.2 5.6 %collective-permute-done.19 = bf16[576,256]{1,0:T(8,128)(2,1)S(1)} collective-permute-done((bf16[576,256]{1,0:T(8,128)(2,1)S(1)}, bf16[576,256]{1,0:T(8,128)(2,1)S(1)}, u32[]{:S(2)}, u32[]{:S(2)}) %collective-permute-start.19) | collective-permute-done | bytes 294944 | tf_op jit(solution)/shard_map/ppermute | solution.py:320
  60.9 1.0 collective-permute-start.24
  62.0 6.4 %collective-permute-done.24.refs_8_ = bf16[576,256]{1,0:T(8,128)(2,1)S(1)} collective-permute-done((bf16[576,256]{1,0:T(8,128)(2,1)S(1)}, bf16[576,256]{1,0:T(8,128)(2,1)S(1)}, u32[]{:S(2)}, u32[]{:S(2)}) %collective-permute-start.24) | collective-permute-done | bytes 294944 | tf_op jit(solution)/shard_map/ppermute | solution.py:320
  68.4 0.5 collective-permute-start.29
  68.9 0.7 collective-permute-start.33
  69.9 1.2 collective-permute-start.27
  71.1 10.2 %shard_map.48 = (bf16[1024,256]{1,0:T(8,128)(2,1)S(1)}, f32[512,256]{1,0:T(8,128)S(1)}, f32[5,128,128]{2,1,0:T(8,128)S(1)}) custom-call(s32[6]{0:T(128)S(1)} %pad_add_fusion.refs_0_, s32[1,2048]{1,0:T(1,128)S(1)} %bitcast.46, bf16[512,256]{1,0:T(8,128)(2,1)S(1)} %shard_map.47.refs_2_, bf16[512,256]{1,0:T(8,128)(2,1)S(1)} %collective-permute-done.28.refs_3_, ...), custom_call_target="tpu_custom_call" | custom-call | flops 15000000512 | bytes 4194304 | tf_op jit(solution)/shard_map/pallas_call | solution.py:490
  81.4 2.5 %collective-permute-done.27.refs_8_ = bf16[576,256]{1,0:T(8,128)(2,1)S(1)} collective-permute-done((bf16[576,256]{1,0:T(8,128)(2,1)S(1)}, bf16[576,256]{1,0:T(8,128)(2,1)S(1)}, u32[]{:S(2)}, u32[]{:S(2)}) %collective-permute-start.27) | collective-permute-done | bytes 294944 | tf_op jit(solution)/shard_map/ppermute | solution.py:320
  83.9 0.5 collective-permute-start.31
  84.4 0.5 collective-permute-start.34
  84.9 0.9 collective-permute-done.31.refs_12_
  85.9 0.7 collective-permute-start.41
  86.6 1.4 collective-permute-start.38
  88.0 12.9 %shard_map.49 = (bf16[768,256]{1,0:T(8,128)(2,1)S(1)}, f32[512,256]{1,0:T(8,128)S(1)}, f32[5,128,128]{2,1,0:T(8,128)S(1)}, bf16[512,256]{1,0:T(8,128)(2,1)S(1)},...) custom-call(s32[6]{0:T(128)S(1)} %pad_add_fusion.refs_0_, s32[1,2048]{1,0:T(1,128)S(1)} %bitcast.47, ...), custom_call_target="tpu_custom_call" | custom-call | flops 15000000512 | bytes 4194304 | tf_op jit(solution)/shard_map/pallas_call | solution.py:490
  101.1 0.4 collective-permute-start.37
  101.7 0.7 collective-permute-start.47
  102.4 0.6 collective-permute-done.37.refs_3_
  102.9 0.7 collective-permute-start.50
  103.7 12.3 %shard_map.50 = (bf16[512,256]{1,0:T(8,128)(2,1)S(1)}, f32[512,256]{1,0:T(8,128)S(1)}, f32[5,128,128]{2,1,0:T(8,128)S(1)}, bf16[512,256]{1,0:T(8,128)(2,1)S(1)},...) custom-call(s32[6]{0:T(128)S(1)} %pad_add_fusion.refs_0_, s32[1,2048]{1,0:T(1,128)S(1)} %bitcast.48, ...), custom_call_target="tpu_custom_call" | custom-call | flops 15000000512 | bytes 4194304 | tf_op jit(solution)/shard_map/pallas_call | solution.py:490
  116.1 0.5 collective-permute-done.50.refs_8_
  116.6 0.5 collective-permute-start.46
  117.1 1.3 collective-permute-start.36
  118.5 1.0 collective-permute-start.45
  119.6 11.7 %shard_map.51 = (bf16[256,256]{1,0:T(8,128)(2,1)S(1)}, f32[512,256]{1,0:T(8,128)S(1)}, f32[5,128,128]{2,1,0:T(8,128)S(1)}, bf16[512,256]{1,0:T(8,128)(2,1)S(1)},...) custom-call(s32[6]{0:T(128)S(1)} %pad_add_fusion.refs_0_, s32[1,2048]{1,0:T(1,128)S(1)} %bitcast.49, ...), custom_call_target="tpu_custom_call" | custom-call | flops 15000000512 | bytes 4194304 | tf_op jit(solution)/shard_map/pallas_call | solution.py:490
  131.3 0.8 collective-permute-done.45.refs_8_
  132.1 0.5 collective-permute-start.35
  132.6 1.4 collective-permute-done.35.refs_3_
  134.1 0.4 collective-permute-done.43.refs_5_
  134.4 14.2 %shard_map.52 = f32[512,256]{1,0:T(8,128)} custom-call(s32[6]{0:T(128)S(1)} %pad_add_fusion.refs_0_, s32[1,2048]{1,0:T(1,128)S(1)} %bitcast.50, bf16[512,256]{1,0:T(8,128)(2,1)S(1)} %get-tuple-element.60.refs_2_, bf16[512,256]{1,0:T(8,128)(2,1)S(1)} %collective-permute-done.35.refs_3_, bf16[512,256]{1,0:T(8,128)(2,1)S(1)} %collective-permute-done.36.refs_4_, ...), custom_call_target="tpu_custom_call" | custom-call | flops 15000000512 | bytes 4194304 | tf_op jit(solution)/shard_map/pallas_call | solution.py:490
  (93 shorter events, 2.2 us)
Async XLA Ops:
  0.0 12.0 %copy-start.1 = (bf16[512,128]{1,0:T(8,128)(2,1)S(1)}, bf16[512,128]{1,0:T(8,128)(2,1)}, u32[]{:S(2)}) copy-start(bf16[512,128]{1,0:T(8,128)(2,1)} %refs_0_.3) | copy-start | bytes 393220
  0.0 9.7 %copy-start.3 = (s32[2,8,8]{2,1,0:T(8,128)S(1)}, s32[2,8,8]{2,1,0:T(8,128)}, u32[]{:S(2)}) copy-start(s32[2,8,8]{2,1,0:T(8,128)} %param.7) | copy-start | bytes 1540
  0.0 10.5 %copy-start.2 = (s32[2,1024]{1,0:T(2,128)S(1)}, s32[2,1024]{1,0:T(2,128)}, u32[]{:S(2)}) copy-start(s32[2,1024]{1,0:T(2,128)} %param.6) | copy-start | bytes 24580
  0.0 14.1 %collective-permute-start.3 = (bf16[512,128]{1,0:T(8,128)(2,1)}, bf16[512,128]{1,0:T(8,128)(2,1)S(1)}, u32[]{:S(2)}, u32[]{:S(2)}) collective-permute-start(bf16[512,128]{1,0:T(8,128)(2,1)} %refs_0_.3), channel_id=1, source_target_pairs={{0,4},{1,5},{2,6},{3,7},{4,0},{5,1},{6,2},{7,3},{8,12},{9,13},{10,... | collective-permute-start | bytes 393224 | tf_op jit(solution)/shard_map/ppermute | solution.py:320
  4.1 13.2 %collective-permute-start = (bf16[512,128]{1,0:T(8,128)(2,1)}, bf16[512,128]{1,0:T(8,128)(2,1)S(1)}, u32[]{:S(2)}, u32[]{:S(2)}) collective-permute-start(bf16[512,128]{1,0:T(8,128)(2,1)} %refs_0_.3), channel_id=1, source_target_pairs={{0,1},{1,0},{2,3},{3,2},{4,5},{5,4},{6,7},{7,6},{8,9},{9,8},{10,11... | collective-permute-start | bytes 393224 | tf_op jit(solution)/shard_map/ppermute | solution.py:320
  7.7 4.3 %collective-permute-start.10 = (bf16[64,256]{1,0:T(8,128)(2,1)S(1)}, bf16[64,256]{1,0:T(8,128)(2,1)S(1)}, u32[]{:S(2)}, u32[]{:S(2)}) collective-permute-start(bf16[64,256]{1,0:T(8,128)(2,1)S(1)} %get-tuple-element.100), channel_id=1, source_target_pairs={{0,24},{8,16},{16,8},{24,0},{1,25},{9,17},{17,9},{25,1},{2,26},{10... | collective-permute-start | bytes 98312 | tf_op jit(solution)/shard_map/ppermute | solution.py:320
  8.2 5.5 %collective-permute-start.11 = (bf16[64,256]{1,0:T(8,128)(2,1)S(1)}, bf16[64,256]{1,0:T(8,128)(2,1)S(1)}, u32[]{:S(2)}, u32[]{:S(2)}) collective-permute-start(bf16[64,256]{1,0:T(8,128)(2,1)S(1)} %get-tuple-element.99), channel_id=1, source_target_pairs={{0,16},{8,24},{16,0},{24,8},{1,17},{9,25},{17,1},{25,9},{2,18},{10... | collective-permute-start | bytes 98312 | tf_op jit(solution)/shard_map/ppermute | solution.py:320
  9.4 4.7 %collective-permute-start.12 = (bf16[64,256]{1,0:T(8,128)(2,1)S(1)}, bf16[64,256]{1,0:T(8,128)(2,1)S(1)}, u32[]{:S(2)}, u32[]{:S(2)}) collective-permute-start(bf16[64,256]{1,0:T(8,128)(2,1)S(1)} %get-tuple-element.98), channel_id=1, source_target_pairs={{0,8},{8,0},{16,24},{24,16},{1,9},{9,1},{17,25},{25,17},{2,10},{10... | collective-permute-start | bytes 98312 | tf_op jit(solution)/shard_map/ppermute | solution.py:320
  12.0 6.4 %collective-permute-start.1 = (bf16[512,128]{1,0:T(8,128)(2,1)S(1)}, bf16[512,128]{1,0:T(8,128)(2,1)S(1)}, u32[]{:S(2)}, u32[]{:S(2)}) collective-permute-start(bf16[512,128]{1,0:T(8,128)(2,1)S(1)} %copy-done.1), channel_id=1, source_target_pairs={{0,2},{1,3},{2,0},{3,1},{4,6},{5,7},{6,4},{7,5},{8,10},{9,11},{10,... | collective-permute-start | bytes 393224 | tf_op jit(solution)/shard_map/ppermute | solution.py:320
  13.7 7.4 %collective-permute-start.2 = (bf16[512,128]{1,0:T(8,128)(2,1)S(1)}, bf16[512,128]{1,0:T(8,128)(2,1)S(1)}, u32[]{:S(2)}, u32[]{:S(2)}) collective-permute-start(bf16[512,128]{1,0:T(8,128)(2,1)S(1)} %copy-done.1), channel_id=1, source_target_pairs={{0,3},{1,2},{2,1},{3,0},{4,7},{5,6},{6,5},{7,4},{8,11},{9,10},{10,... | collective-permute-start | bytes 393224 | tf_op jit(solution)/shard_map/ppermute | solution.py:320
  14.2 13.8 %collective-permute-start.4 = (bf16[512,128]{1,0:T(8,128)(2,1)S(1)}, bf16[512,128]{1,0:T(8,128)(2,1)S(1)}, u32[]{:S(2)}, u32[]{:S(2)}) collective-permute-start(bf16[512,128]{1,0:T(8,128)(2,1)S(1)} %collective-permute-done.3.refs_4_), channel_id=1, source_target_pairs={{0,1},{1,0},{2,3},{3,2},{4,5},{5,4},{6,7},{7,6},{8,9},{9,8},{10,11... | collective-permute-start | bytes 393224 | tf_op jit(solution)/shard_map/ppermute | solution.py:320
  15.7 13.8 %collective-permute-start.5 = (bf16[512,128]{1,0:T(8,128)(2,1)S(1)}, bf16[512,128]{1,0:T(8,128)(2,1)S(1)}, u32[]{:S(2)}, u32[]{:S(2)}) collective-permute-start(bf16[512,128]{1,0:T(8,128)(2,1)S(1)} %collective-permute-done.3.refs_4_), channel_id=1, source_target_pairs={{0,2},{1,3},{2,0},{3,1},{4,6},{5,7},{6,4},{7,5},{8,10},{9,11},{10,... | collective-permute-start | bytes 393224 | tf_op jit(solution)/shard_map/ppermute | solution.py:320
  17.3 14.2 %collective-permute-start.6 = (bf16[512,128]{1,0:T(8,128)(2,1)S(1)}, bf16[512,128]{1,0:T(8,128)(2,1)S(1)}, u32[]{:S(2)}, u32[]{:S(2)}) collective-permute-start(bf16[512,128]{1,0:T(8,128)(2,1)S(1)} %collective-permute-done.3.refs_4_), channel_id=1, source_target_pairs={{0,3},{1,2},{2,1},{3,0},{4,7},{5,6},{6,5},{7,4},{8,11},{9,10},{10,... | collective-permute-start | bytes 393224 | tf_op jit(solution)/shard_map/ppermute | solution.py:320
  18.4 17.9 %collective-permute-start.13 = (bf16[576,256]{1,0:T(8,128)(2,1)S(1)}, bf16[576,256]{1,0:T(8,128)(2,1)S(1)}, u32[]{:S(2)}, u32[]{:S(2)}) collective-permute-start(bf16[576,256]{1,0:T(8,128)(2,1)S(1)} %pad_maximum_fusion), channel_id=1, source_target_pairs={{0,4},{1,5},{2,6},{3,7},{4,0},{5,1},{6,2},{7,3},{8,12},{9,13},{10,... | collective-permute-start | bytes 884744 | tf_op jit(solution)/shard_map/ppermute | solution.py:320
  21.1 15.9 %collective-permute-start.14 = (bf16[576,256]{1,0:T(8,128)(2,1)S(1)}, bf16[576,256]{1,0:T(8,128)(2,1)S(1)}, u32[]{:S(2)}, u32[]{:S(2)}) collective-permute-start(bf16[576,256]{1,0:T(8,128)(2,1)S(1)} %pad_maximum_fusion), channel_id=1, source_target_pairs={{0,1},{1,0},{2,3},{3,2},{4,5},{5,4},{6,7},{7,6},{8,9},{9,8},{10,11... | collective-permute-start | bytes 884744 | tf_op jit(solution)/shard_map/ppermute | solution.py:320
  27.9 11.6 %collective-permute-start.15 = (bf16[576,256]{1,0:T(8,128)(2,1)S(1)}, bf16[576,256]{1,0:T(8,128)(2,1)S(1)}, u32[]{:S(2)}, u32[]{:S(2)}) collective-permute-start(bf16[576,256]{1,0:T(8,128)(2,1)S(1)} %pad_maximum_fusion), channel_id=1, source_target_pairs={{0,2},{1,3},{2,0},{3,1},{4,6},{5,7},{6,4},{7,5},{8,10},{9,11},{10,... | collective-permute-start | bytes 884744 | tf_op jit(solution)/shard_map/ppermute | solution.py:320
  29.5 15.7 %collective-permute-start.16 = (bf16[576,256]{1,0:T(8,128)(2,1)S(1)}, bf16[576,256]{1,0:T(8,128)(2,1)S(1)}, u32[]{:S(2)}, u32[]{:S(2)}) collective-permute-start(bf16[576,256]{1,0:T(8,128)(2,1)S(1)} %pad_maximum_fusion), channel_id=1, source_target_pairs={{0,3},{1,2},{2,1},{3,0},{4,7},{5,6},{6,5},{7,4},{8,11},{9,10},{10,... | collective-permute-start | bytes 884744 | tf_op jit(solution)/shard_map/ppermute | solution.py:320
  33.7 13.2 %collective-permute-start.20 = (bf16[512,256]{1,0:T(8,128)(2,1)S(1)}, bf16[512,256]{1,0:T(8,128)(2,1)S(1)}, u32[]{:S(2)}, u32[]{:S(2)}) collective-permute-start(bf16[512,256]{1,0:T(8,128)(2,1)S(1)} %get-tuple-element.51.refs_11_), channel_id=1, source_target_pairs={{0,16},{8,24},{16,0},{24,8},{1,17},{9,25},{17,1},{25,9},{2,18},{10... | collective-permute-start | bytes 786440 | tf_op jit(solution)/shard_map/ppermute | solution.py:320
  36.3 12.3 %collective-permute-start.8 = (bf16[512,256]{1,0:T(8,128)(2,1)S(1)}, bf16[512,256]{1,0:T(8,128)(2,1)S(1)}, u32[]{:S(2)}, u32[]{:S(2)}) collective-permute-start(bf16[512,256]{1,0:T(8,128)(2,1)S(1)} %get-tuple-element.49.refs_2_), channel_id=1, source_target_pairs={{0,16},{8,24},{16,0},{24,8},{1,17},{9,25},{17,1},{25,9},{2,18},{10... | collective-permute-start | bytes 786440 | tf_op jit(solution)/shard_map/ppermute | solution.py:320
  37.0 15.3 %collective-permute-start.22 = (bf16[512,256]{1,0:T(8,128)(2,1)S(1)}, bf16[512,256]{1,0:T(8,128)(2,1)S(1)}, u32[]{:S(2)}, u32[]{:S(2)}) collective-permute-start(bf16[512,256]{1,0:T(8,128)(2,1)S(1)} %shard_map.47.refs_2_), channel_id=1, source_target_pairs={{0,16},{8,24},{16,0},{24,8},{1,17},{9,25},{17,1},{25,9},{2,18},{10... | collective-permute-start | bytes 786440 | tf_op jit(solution)/shard_map/ppermute | solution.py:320
  39.5 12.7 %collective-permute-start.17 = (bf16[576,256]{1,0:T(8,128)(2,1)S(1)}, bf16[576,256]{1,0:T(8,128)(2,1)S(1)}, u32[]{:S(2)}, u32[]{:S(2)}) collective-permute-start(bf16[576,256]{1,0:T(8,128)(2,1)S(1)} %collective-permute-done.13), channel_id=1, source_target_pairs={{0,1},{1,0},{2,3},{3,2},{4,5},{5,4},{6,7},{7,6},{8,9},{9,8},{10,11... | collective-permute-start | bytes 884744 | tf_op jit(solution)/shard_map/ppermute | solution.py:320
  45.2 9.9 %collective-permute-start.18 = (bf16[576,256]{1,0:T(8,128)(2,1)S(1)}, bf16[576,256]{1,0:T(8,128)(2,1)S(1)}, u32[]{:S(2)}, u32[]{:S(2)}) collective-permute-start(bf16[576,256]{1,0:T(8,128)(2,1)S(1)} %collective-permute-done.13), channel_id=1, source_target_pairs={{0,2},{1,3},{2,0},{3,1},{4,6},{5,7},{6,4},{7,5},{8,10},{9,11},{10,... | collective-permute-start | bytes 884744 | tf_op jit(solution)/shard_map/ppermute | solution.py:320
  46.9 13.9 %collective-permute-start.19 = (bf16[576,256]{1,0:T(8,128)(2,1)S(1)}, bf16[576,256]{1,0:T(8,128)(2,1)S(1)}, u32[]{:S(2)}, u32[]{:S(2)}) collective-permute-start(bf16[576,256]{1,0:T(8,128)(2,1)S(1)} %collective-permute-done.13), channel_id=1, source_target_pairs={{0,3},{1,2},{2,1},{3,0},{4,7},{5,6},{6,5},{7,4},{8,11},{9,10},{10,... | collective-permute-start | bytes 884744 | tf_op jit(solution)/shard_map/ppermute | solution.py:320
  48.6 12.2 %collective-permute-start.21 = (bf16[512,256]{1,0:T(8,128)(2,1)S(1)}, bf16[512,256]{1,0:T(8,128)(2,1)S(1)}, u32[]{:S(2)}, u32[]{:S(2)}) collective-permute-start(bf16[512,256]{1,0:T(8,128)(2,1)S(1)} %collective-permute-done.20.refs_13_), channel_id=1, source_target_pairs={{0,8},{8,0},{16,24},{24,16},{1,9},{9,1},{17,25},{25,17},{2,10},{10... | collective-permute-start | bytes 786440 | tf_op jit(solution)/shard_map/ppermute | solution.py:320
  52.3 8.5 %collective-permute-start.9 = (bf16[512,256]{1,0:T(8,128)(2,1)S(1)}, bf16[512,256]{1,0:T(8,128)(2,1)S(1)}, u32[]{:S(2)}, u32[]{:S(2)}) collective-permute-start(bf16[512,256]{1,0:T(8,128)(2,1)S(1)} %collective-permute-done.8.refs_4_), channel_id=1, source_target_pairs={{0,8},{8,0},{16,24},{24,16},{1,9},{9,1},{17,25},{25,17},{2,10},{10... | collective-permute-start | bytes 786440 | tf_op jit(solution)/shard_map/ppermute | solution.py:320
  52.3 8.5 %collective-permute-start.23 = (bf16[512,256]{1,0:T(8,128)(2,1)S(1)}, bf16[512,256]{1,0:T(8,128)(2,1)S(1)}, u32[]{:S(2)}, u32[]{:S(2)}) collective-permute-start(bf16[512,256]{1,0:T(8,128)(2,1)S(1)} %collective-permute-done.22.refs_4_), channel_id=1, source_target_pairs={{0,8},{8,0},{16,24},{24,16},{1,9},{9,1},{17,25},{25,17},{2,10},{10... | collective-permute-start | bytes 786440 | tf_op jit(solution)/shard_map/ppermute | solution.py:320
  60.9 7.4 %collective-permute-start.24 = (bf16[576,256]{1,0:T(8,128)(2,1)S(1)}, bf16[576,256]{1,0:T(8,128)(2,1)S(1)}, u32[]{:S(2)}, u32[]{:S(2)}) collective-permute-start(bf16[576,256]{1,0:T(8,128)(2,1)S(1)} %get-tuple-element.94.refs_6_.refs_10_), channel_id=1, source_target_pairs={{0,16},{8,24},{16,0},{24,8},{1,17},{9,25},{17,1},{25,9},{2,18},{10... | collective-permute-start | bytes 884744 | tf_op jit(solution)/shard_map/ppermute | solution.py:320
  68.4 1.6 %collective-permute-start.25 = (bf16[576,256]{1,0:T(8,128)(2,1)S(1)}, bf16[576,256]{1,0:T(8,128)(2,1)S(1)}, u32[]{:S(2)}, u32[]{:S(2)}) collective-permute-start(bf16[576,256]{1,0:T(8,128)(2,1)S(1)} %collective-permute-done.24.refs_8_), channel_id=1, source_target_pairs={{0,8},{8,0},{16,24},{24,16},{1,9},{9,1},{17,25},{25,17},{2,10},{10... | collective-permute-start | bytes 884744 | tf_op jit(solution)/shard_map/ppermute | solution.py:320
  68.4 2.8 %collective-permute-start.29 = (bf16[576,256]{1,0:T(8,128)(2,1)S(1)}, bf16[576,256]{1,0:T(8,128)(2,1)S(1)}, u32[]{:S(2)}, u32[]{:S(2)}) collective-permute-start(bf16[576,256]{1,0:T(8,128)(2,1)S(1)} %get-tuple-element.94.refs_6_.refs_10_), channel_id=1, source_target_pairs={{0,8},{8,0},{16,24},{24,16},{1,9},{9,1},{17,25},{25,17},{2,10},{10... | collective-permute-start | bytes 884744 | tf_op jit(solution)/shard_map/ppermute | solution.py:320
  68.9 2.3 %collective-permute-start.28 = (bf16[512,256]{1,0:T(8,128)(2,1)S(1)}, bf16[512,256]{1,0:T(8,128)(2,1)S(1)}, u32[]{:S(2)}, u32[]{:S(2)}) collective-permute-start(bf16[512,256]{1,0:T(8,128)(2,1)S(1)} %shard_map.47.refs_2_), channel_id=1, source_target_pairs={{0,8},{8,0},{16,24},{24,16},{1,9},{9,1},{17,25},{25,17},{2,10},{10... | collective-permute-start | bytes 786440 | tf_op jit(solution)/shard_map/ppermute | solution.py:320
  68.9 15.6 %collective-permute-start.33 = (bf16[512,256]{1,0:T(8,128)(2,1)S(1)}, bf16[512,256]{1,0:T(8,128)(2,1)S(1)}, u32[]{:S(2)}, u32[]{:S(2)}) collective-permute-start(bf16[512,256]{1,0:T(8,128)(2,1)S(1)} %get-tuple-element.56.refs_15_), channel_id=1, source_target_pairs={{0,16},{8,24},{16,0},{24,8},{1,17},{9,25},{17,1},{25,9},{2,18},{10... | collective-permute-start | bytes 786440 | tf_op jit(solution)/shard_map/ppermute | solution.py:320
  69.6 14.9 %collective-permute-start.32 = (bf16[512,256]{1,0:T(8,128)(2,1)S(1)}, bf16[512,256]{1,0:T(8,128)(2,1)S(1)}, u32[]{:S(2)}, u32[]{:S(2)}) collective-permute-start(bf16[512,256]{1,0:T(8,128)(2,1)S(1)} %get-tuple-element.56.refs_15_), channel_id=1, source_target_pairs={{0,8},{8,0},{16,24},{24,16},{1,9},{9,1},{17,25},{25,17},{2,10},{10... | collective-permute-start | bytes 786440 | tf_op jit(solution)/shard_map/ppermute | solution.py:320
  69.9 18.0 %copy-start = (f32[512,256]{1,0:T(8,128)S(1)}, f32[512,256]{1,0:T(8,128)}, u32[]{:S(2)}) copy-start(f32[512,256]{1,0:T(8,128)} %refs_21_.1) | copy-start | bytes 1572868
  69.9 14.0 %collective-permute-start.27 = (bf16[576,256]{1,0:T(8,128)(2,1)S(1)}, bf16[576,256]{1,0:T(8,128)(2,1)S(1)}, u32[]{:S(2)}, u32[]{:S(2)}) collective-permute-start(bf16[576,256]{1,0:T(8,128)(2,1)S(1)} %get-tuple-element.53.refs_6_.refs_10_), channel_id=1, source_target_pairs={{0,16},{8,24},{16,0},{24,8},{1,17},{9,25},{17,1},{25,9},{2,18},{10... | collective-permute-start | bytes 884744 | tf_op jit(solution)/shard_map/ppermute | solution.py:320
  71.1 16.8 %collective-permute-start.26 = (bf16[576,256]{1,0:T(8,128)(2,1)S(1)}, bf16[576,256]{1,0:T(8,128)(2,1)S(1)}, u32[]{:S(2)}, u32[]{:S(2)}) collective-permute-start(bf16[576,256]{1,0:T(8,128)(2,1)S(1)} %get-tuple-element.53.refs_6_.refs_10_), channel_id=1, source_target_pairs={{0,8},{8,0},{16,24},{24,16},{1,9},{9,1},{17,25},{25,17},{2,10},{10... | collective-permute-start | bytes 884744 | tf_op jit(solution)/shard_map/ppermute | solution.py:320
  83.9 4.1 %collective-permute-start.30 = (bf16[576,256]{1,0:T(8,128)(2,1)S(1)}, bf16[576,256]{1,0:T(8,128)(2,1)S(1)}, u32[]{:S(2)}, u32[]{:S(2)}) collective-permute-start(bf16[576,256]{1,0:T(8,128)(2,1)S(1)} %collective-permute-done.27.refs_8_), channel_id=1, source_target_pairs={{0,8},{8,0},{16,24},{24,16},{1,9},{9,1},{17,25},{25,17},{2,10},{10... | collective-permute-start | bytes 884744 | tf_op jit(solution)/shard_map/ppermute | solution.py:320
  83.9 2.0 %collective-permute-start.31 = (bf16[512,256]{1,0:T(8,128)(2,1)S(1)}, bf16[512,256]{1,0:T(8,128)(2,1)S(1)}, u32[]{:S(2)}, u32[]{:S(2)}) collective-permute-start(bf16[512,256]{1,0:T(8,128)(2,1)S(1)} %get-tuple-element.51.refs_11_), channel_id=1, source_target_pairs={{0,8},{8,0},{16,24},{24,16},{1,9},{9,1},{17,25},{25,17},{2,10},{10... | collective-permute-start | bytes 786440 | tf_op jit(solution)/shard_map/ppermute | solution.py:320
  84.4 2.2 %collective-permute-start.7 = (bf16[512,256]{1,0:T(8,128)(2,1)S(1)}, bf16[512,256]{1,0:T(8,128)(2,1)S(1)}, u32[]{:S(2)}, u32[]{:S(2)}) collective-permute-start(bf16[512,256]{1,0:T(8,128)(2,1)S(1)} %get-tuple-element.49.refs_2_), channel_id=1, source_target_pairs={{0,8},{8,0},{16,24},{24,16},{1,9},{9,1},{17,25},{25,17},{2,10},{10... | collective-permute-start | bytes 786440 | tf_op jit(solution)/shard_map/ppermute | solution.py:320
  84.4 2.2 %collective-permute-start.34 = (bf16[512,256]{1,0:T(8,128)(2,1)S(1)}, bf16[512,256]{1,0:T(8,128)(2,1)S(1)}, u32[]{:S(2)}, u32[]{:S(2)}) collective-permute-start(bf16[512,256]{1,0:T(8,128)(2,1)S(1)} %collective-permute-done.33.refs_17_), channel_id=1, source_target_pairs={{0,8},{8,0},{16,24},{24,16},{1,9},{9,1},{17,25},{25,17},{2,10},{10... | collective-permute-start | bytes 786440 | tf_op jit(solution)/shard_map/ppermute | solution.py:320
  85.9 15.0 %collective-permute-start.41 = (bf16[576,256]{1,0:T(8,128)(2,1)S(1)}, bf16[576,256]{1,0:T(8,128)(2,1)S(1)}, u32[]{:S(2)}, u32[]{:S(2)}) collective-permute-start(bf16[576,256]{1,0:T(8,128)(2,1)S(1)} %get-tuple-element.64.refs_6_.refs_10_), channel_id=1, source_target_pairs={{0,16},{8,24},{16,0},{24,8},{1,17},{9,25},{17,1},{25,9},{2,18},{10... | collective-permute-start | bytes 884744 | tf_op jit(solution)/shard_map/ppermute | solution.py:320
  86.6 17.1 %collective-permute-start.40 = (bf16[576,256]{1,0:T(8,128)(2,1)S(1)}, bf16[576,256]{1,0:T(8,128)(2,1)S(1)}, u32[]{:S(2)}, u32[]{:S(2)}) collective-permute-start(bf16[576,256]{1,0:T(8,128)(2,1)S(1)} %get-tuple-element.64.refs_6_.refs_10_), channel_id=1, source_target_pairs={{0,8},{8,0},{16,24},{24,16},{1,9},{9,1},{17,25},{25,17},{2,10},{10... | collective-permute-start | bytes 884744 | tf_op jit(solution)/shard_map/ppermute | solution.py:320
  86.6 14.9 %collective-permute-start.38 = (bf16[512,256]{1,0:T(8,128)(2,1)S(1)}, bf16[512,256]{1,0:T(8,128)(2,1)S(1)}, u32[]{:S(2)}, u32[]{:S(2)}) collective-permute-start(bf16[512,256]{1,0:T(8,128)(2,1)S(1)} %get-tuple-element.62.refs_2_), channel_id=1, source_target_pairs={{0,16},{8,24},{16,0},{24,8},{1,17},{9,25},{17,1},{25,9},{2,18},{10... | collective-permute-start | bytes 786440 | tf_op jit(solution)/shard_map/ppermute | solution.py:320
  100.9 2.8 %collective-permute-start.42 = (bf16[576,256]{1,0:T(8,128)(2,1)S(1)}, bf16[576,256]{1,0:T(8,128)(2,1)S(1)}, u32[]{:S(2)}, u32[]{:S(2)}) collective-permute-start(bf16[576,256]{1,0:T(8,128)(2,1)S(1)} %collective-permute-done.41.refs_8_), channel_id=1, source_target_pairs={{0,8},{8,0},{16,24},{24,16},{1,9},{9,1},{17,25},{25,17},{2,10},{10... | collective-permute-start | bytes 884744 | tf_op jit(solution)/shard_map/ppermute | solution.py:320
  101.1 1.8 %collective-permute-start.37 = (bf16[512,256]{1,0:T(8,128)(2,1)S(1)}, bf16[512,256]{1,0:T(8,128)(2,1)S(1)}, u32[]{:S(2)}, u32[]{:S(2)}) collective-permute-start(bf16[512,256]{1,0:T(8,128)(2,1)S(1)} %get-tuple-element.62.refs_2_), channel_id=1, source_target_pairs={{0,8},{8,0},{16,24},{24,16},{1,9},{9,1},{17,25},{25,17},{2,10},{10... | collective-permute-start | bytes 786440 | tf_op jit(solution)/shard_map/ppermute | solution.py:320
  101.5 2.2 %collective-permute-start.39 = (bf16[512,256]{1,0:T(8,128)(2,1)S(1)}, bf16[512,256]{1,0:T(8,128)(2,1)S(1)}, u32[]{:S(2)}, u32[]{:S(2)}) collective-permute-start(bf16[512,256]{1,0:T(8,128)(2,1)S(1)} %collective-permute-done.38.refs_4_), channel_id=1, source_target_pairs={{0,8},{8,0},{16,24},{24,16},{1,9},{9,1},{17,25},{25,17},{2,10},{10... | collective-permute-start | bytes 786440 | tf_op jit(solution)/shard_map/ppermute | solution.py:320
  101.7 15.4 %collective-permute-start.47 = (bf16[512,256]{1,0:T(8,128)(2,1)S(1)}, bf16[512,256]{1,0:T(8,128)(2,1)S(1)}, u32[]{:S(2)}, u32[]{:S(2)}) collective-permute-start(bf16[512,256]{1,0:T(8,128)(2,1)S(1)} %get-tuple-element.75.refs_2_), channel_id=1, source_target_pairs={{0,16},{8,24},{16,0},{24,8},{1,17},{9,25},{17,1},{25,9},{2,18},{10... | collective-permute-start | bytes 786440 | tf_op jit(solution)/shard_map/ppermute | solution.py:320
  102.9 13.6 %collective-permute-start.50 = (bf16[576,256]{1,0:T(8,128)(2,1)S(1)}, bf16[576,256]{1,0:T(8,128)(2,1)S(1)}, u32[]{:S(2)}, u32[]{:S(2)}) collective-permute-start(bf16[576,256]{1,0:T(8,128)(2,1)S(1)} %get-tuple-element.77.refs_6_.refs_10_), channel_id=1, source_target_pairs={{0,16},{8,24},{16,0},{24,8},{1,17},{9,25},{17,1},{25,9},{2,18},{10... | collective-permute-start | bytes 884744 | tf_op jit(solution)/shard_map/ppermute | solution.py:320
  103.7 15.9 %collective-permute-start.49 = (bf16[576,256]{1,0:T(8,128)(2,1)S(1)}, bf16[576,256]{1,0:T(8,128)(2,1)S(1)}, u32[]{:S(2)}, u32[]{:S(2)}) collective-permute-start(bf16[576,256]{1,0:T(8,128)(2,1)S(1)} %get-tuple-element.77.refs_6_.refs_10_), channel_id=1, source_target_pairs={{0,8},{8,0},{16,24},{24,16},{1,9},{9,1},{17,25},{25,17},{2,10},{10... | collective-permute-start | bytes 884744 | tf_op jit(solution)/shard_map/ppermute | solution.py:320
  116.5 3.0 %collective-permute-start.51 = (bf16[576,256]{1,0:T(8,128)(2,1)S(1)}, bf16[576,256]{1,0:T(8,128)(2,1)S(1)}, u32[]{:S(2)}, u32[]{:S(2)}) collective-permute-start(bf16[576,256]{1,0:T(8,128)(2,1)S(1)} %collective-permute-done.50.refs_8_), channel_id=1, source_target_pairs={{0,8},{8,0},{16,24},{24,16},{1,9},{9,1},{17,25},{25,17},{2,10},{10... | collective-permute-start | bytes 884744 | tf_op jit(solution)/shard_map/ppermute | solution.py:320
  116.6 1.9 %collective-permute-start.46 = (bf16[512,256]{1,0:T(8,128)(2,1)S(1)}, bf16[512,256]{1,0:T(8,128)(2,1)S(1)}, u32[]{:S(2)}, u32[]{:S(2)}) collective-permute-start(bf16[512,256]{1,0:T(8,128)(2,1)S(1)} %get-tuple-element.75.refs_2_), channel_id=1, source_target_pairs={{0,8},{8,0},{16,24},{24,16},{1,9},{9,1},{17,25},{25,17},{2,10},{10... | collective-permute-start | bytes 786440 | tf_op jit(solution)/shard_map/ppermute | solution.py:320
  117.1 2.4 %collective-permute-start.48 = (bf16[512,256]{1,0:T(8,128)(2,1)S(1)}, bf16[512,256]{1,0:T(8,128)(2,1)S(1)}, u32[]{:S(2)}, u32[]{:S(2)}) collective-permute-start(bf16[512,256]{1,0:T(8,128)(2,1)S(1)} %collective-permute-done.47.refs_4_), channel_id=1, source_target_pairs={{0,8},{8,0},{16,24},{24,16},{1,9},{9,1},{17,25},{25,17},{2,10},{10... | collective-permute-start | bytes 786440 | tf_op jit(solution)/shard_map/ppermute | solution.py:320
  117.1 15.5 %collective-permute-start.36 = (bf16[512,256]{1,0:T(8,128)(2,1)S(1)}, bf16[512,256]{1,0:T(8,128)(2,1)S(1)}, u32[]{:S(2)}, u32[]{:S(2)}) collective-permute-start(bf16[512,256]{1,0:T(8,128)(2,1)S(1)} %get-tuple-element.60.refs_2_), channel_id=1, source_target_pairs={{0,16},{8,24},{16,0},{24,8},{1,17},{9,25},{17,1},{25,9},{2,18},{10... | collective-permute-start | bytes 786440 | tf_op jit(solution)/shard_map/ppermute | solution.py:320
  118.5 13.6 %collective-permute-start.45 = (bf16[576,256]{1,0:T(8,128)(2,1)S(1)}, bf16[576,256]{1,0:T(8,128)(2,1)S(1)}, u32[]{:S(2)}, u32[]{:S(2)}) collective-permute-start(bf16[576,256]{1,0:T(8,128)(2,1)S(1)} %get-tuple-element.73.refs_6_.refs_10_), channel_id=1, source_target_pairs={{0,16},{8,24},{16,0},{24,8},{1,17},{9,25},{17,1},{25,9},{2,18},{10... | collective-permute-start | bytes 884744 | tf_op jit(solution)/shard_map/ppermute | solution.py:320
  119.5 14.9 %collective-permute-start.44 = (bf16[576,256]{1,0:T(8,128)(2,1)S(1)}, bf16[576,256]{1,0:T(8,128)(2,1)S(1)}, u32[]{:S(2)}, u32[]{:S(2)}) collective-permute-start(bf16[576,256]{1,0:T(8,128)(2,1)S(1)} %get-tuple-element.73.refs_6_.refs_10_), channel_id=1, source_target_pairs={{0,8},{8,0},{16,24},{24,16},{1,9},{9,1},{17,25},{25,17},{2,10},{10... | collective-permute-start | bytes 884744 | tf_op jit(solution)/shard_map/ppermute | solution.py:320
  132.1 2.3 %collective-permute-start.52 = (bf16[576,256]{1,0:T(8,128)(2,1)S(1)}, bf16[576,256]{1,0:T(8,128)(2,1)S(1)}, u32[]{:S(2)}, u32[]{:S(2)}) collective-permute-start(bf16[576,256]{1,0:T(8,128)(2,1)S(1)} %collective-permute-done.45.refs_8_), channel_id=1, source_target_pairs={{0,8},{8,0},{16,24},{24,16},{1,9},{9,1},{17,25},{25,17},{2,10},{10... | collective-permute-start | bytes 884744 | tf_op jit(solution)/shard_map/ppermute | solution.py:320
  132.1 2.0 %collective-permute-start.35 = (bf16[512,256]{1,0:T(8,128)(2,1)S(1)}, bf16[512,256]{1,0:T(8,128)(2,1)S(1)}, u32[]{:S(2)}, u32[]{:S(2)}) collective-permute-start(bf16[512,256]{1,0:T(8,128)(2,1)S(1)} %get-tuple-element.60.refs_2_), channel_id=1, source_target_pairs={{0,8},{8,0},{16,24},{24,16},{1,9},{9,1},{17,25},{25,17},{2,10},{10... | collective-permute-start | bytes 786440 | tf_op jit(solution)/shard_map/ppermute | solution.py:320
  132.6 1.8 %collective-permute-start.43 = (bf16[512,256]{1,0:T(8,128)(2,1)S(1)}, bf16[512,256]{1,0:T(8,128)(2,1)S(1)}, u32[]{:S(2)}, u32[]{:S(2)}) collective-permute-start(bf16[512,256]{1,0:T(8,128)(2,1)S(1)} %collective-permute-done.36.refs_4_), channel_id=1, source_target_pairs={{0,8},{8,0},{16,24},{24,16},{1,9},{9,1},{17,25},{25,17},{2,10},{10... | collective-permute-start | bytes 786440 | tf_op jit(solution)/shard_map/ppermute | solution.py:320

commit v2 on v1

--- a/solution.py
+++ b/solution.py
@@ -386,7 +386,7 @@
 
     pieces = over_panel(child_updates, panel_count)
     if small:
-        columns = over_panel(after(column, pieces[4]), panel_count)
+        columns = over_panel(column, panel_count)
         root_all = jnp.zeros((STEPS + 1, *column.shape), BF16)
         for x in (0, 4, 1, 2, 3, 5, 6, 7):
             slot = jnp.minimum(panel ^ x, STEPS)
@@ -433,12 +433,14 @@
         return [every[x] for x in range(need)]
 
     xa, xr, ys, factors = [], [], [], []
-    early = 2 if small else 1
+    early = 3 if small else 1
+    if small:
+        root_own = root_pieces(after(high.astype(BF16), pieces[1]))
+        picked = [after(picked[0], root_own[-1]), *picked[1:]]
     cols = [over_leaf(picked[step], leaf_count) for step in range(early)]
     if small:
         own_col = over_leaf(picked[STEPS], leaf_count)
-        root_own = root_pieces(after(high.astype(BF16), pieces[1]))
-        root_all = after(root_all, row_map, place, own_col[-1], *[c[-1] for c in cols])
+        root_all = after(root_all, row_map, place, own_col[-1], cols[0][-1], cols[1][-1])
         roots = [root_pieces(root_all[0])]
     else:
         roots = [root_pieces(root_all[0])]
@@ -510,9 +512,9 @@
             rest_block = out[5]
         done.append(out[0])
         if small and not last:
-            if step + 2 < STEPS:
+            roots.append(root_pieces(root_all[step + 1], done[step], done[step + 1]))
+            if step and step + 2 < STEPS:
                 cols.append(over_leaf(picked[step + 2], leaf_count, done[step], done[step + 1]))
-            roots.append(root_pieces(root_all[step + 1], done[step], done[step + 1]))
 
 
 def solution(mesh):

time: 149 us -> 147 us (0.987)
  waiting for transfers between devices: 36.6 us -> 31.8 us
  starting transfers between devices: 42.2 us -> 44.9 us
    ppermute x53, waiting for transfers between devices: 36.6 us -> 31.8 us  [flip(): return lax.ppermute(value, axis, [(i, i ^ bits) for i in range(count)])]
    ppermute x53, starting transfers between devices: 42.2 us -> 44.9 us  [flip(): return lax.ppermute(value, axis, [(i, i ^ bits) for i in range(count)])]
  transfers between devices with their start and end apart: 53 -> 53, of which waited for: 20 -> 17; matrix products, arithmetic and copies ran while one was open for 3% -> 3% of each run, Pallas kernels for 34% -> 34%
where the time goes in v2:
time: 147 us
  Pallas kernels  64.6 us (44%)
  starting transfers between devices  44.9 us (31%)
  waiting for transfers between devices  31.8 us (22%)
  local copies, waits for them, and re-layouts  2.42 us (2%)
  other arithmetic  2.35 us (2%)
    pallas_call x5, Pallas kernels, per_device(): pl.pallas_call(functools.partial(step_kernel, step, leaf_count, spots), i...  61.4 us
    ppermute x53, starting transfers between devices, flip(): return lax.ppermute(value, axis, [(i, i ^ bits) for i in range(count)])  44.9 us
    ppermute x53, waiting for transfers between devices, flip(): return lax.ppermute(value, axis, [(i, i ^ bits) for i in range(count)])  31.8 us
    pallas_call x2, Pallas kernels, select(): pl.pallas_call(select_kernel, in_specs=[SMEM_SPEC, SMEM_SPEC, VMEM_SPEC]...  3.21 us
  transfers between devices with their start and end apart: 53, of which 17 were waited for; matrix products, arithmetic and copies ran while one was open for 3% of the time, Pallas kernels for 34%

profile of v2, /device:TPU:0, one launch (start us, length us, event | category | flops | bytes accessed | tf_op | source)
XLA Modules:
  0.0 146.5 jit_solution(3549610398820007885)
XLA Ops:
  0.0 4.1 %collective-permute-start.3 = (bf16[512,128]{1,0:T(8,128)(2,1)}, bf16[512,128]{1,0:T(8,128)(2,1)S(1)}, u32[]{:S(2)}, u32[]{:S(2)}) collective-permute-start(bf16[512,128]{1,0:T(8,128)(2,1)} %refs_0_.3), channel_id=1, source_target_pairs={{0,4},{1,5},{2,6},{3,7},{4,0},{5,1},{6,2},{7,3},{8,12},{9,13},{10,... | collective-permute-start | bytes 393224 | tf_op jit(solution)/shard_map/ppermute | solution.py:320
  4.1 1.5 %collective-permute-start = (bf16[512,128]{1,0:T(8,128)(2,1)}, bf16[512,128]{1,0:T(8,128)(2,1)S(1)}, u32[]{:S(2)}, u32[]{:S(2)}) collective-permute-start(bf16[512,128]{1,0:T(8,128)(2,1)} %refs_0_.3), channel_id=1, source_target_pairs={{0,1},{1,0},{2,3},{3,2},{4,5},{5,4},{6,7},{7,6},{8,9},{9,8},{10,11... | collective-permute-start | bytes 393224 | tf_op jit(solution)/shard_map/ppermute | solution.py:320
  5.6 1.1 reduce-precision_convert_fusion
  6.7 1.0 fusion
  7.7 0.5 collective-permute-start.10
  8.2 1.2 collective-permute-start.11
  9.4 0.3 collective-permute-start.12
  9.9 0.6 gather_fusion.1
  10.8 0.6 gather_fusion.2
  11.4 0.6 gather_fusion
  12.0 1.6 %collective-permute-start.1 = (bf16[512,128]{1,0:T(8,128)(2,1)S(1)}, bf16[512,128]{1,0:T(8,128)(2,1)S(1)}, u32[]{:S(2)}, u32[]{:S(2)}) collective-permute-start(bf16[512,128]{1,0:T(8,128)(2,1)S(1)} %copy-done.1), channel_id=1, source_target_pairs={{0,2},{1,3},{2,0},{3,1},{4,6},{5,7},{6,4},{7,5},{8,10},{9,11},{10,... | collective-permute-start | bytes 393224 | tf_op jit(solution)/shard_map/ppermute | solution.py:320
  13.7 0.4 collective-permute-start.2
  14.1 1.6 %collective-permute-start.4 = (bf16[512,128]{1,0:T(8,128)(2,1)S(1)}, bf16[512,128]{1,0:T(8,128)(2,1)S(1)}, u32[]{:S(2)}, u32[]{:S(2)}) collective-permute-start(bf16[512,128]{1,0:T(8,128)(2,1)S(1)} %collective-permute-done.3.refs_4_), channel_id=1, source_target_pairs={{0,1},{1,0},{2,3},{3,2},{4,5},{5,4},{6,7},{7,6},{8,9},{9,8},{10,11... | collective-permute-start | bytes 393224 | tf_op jit(solution)/shard_map/ppermute | solution.py:320
  15.7 1.6 %collective-permute-start.5 = (bf16[512,128]{1,0:T(8,128)(2,1)S(1)}, bf16[512,128]{1,0:T(8,128)(2,1)S(1)}, u32[]{:S(2)}, u32[]{:S(2)}) collective-permute-start(bf16[512,128]{1,0:T(8,128)(2,1)S(1)} %collective-permute-done.3.refs_4_), channel_id=1, source_target_pairs={{0,2},{1,3},{2,0},{3,1},{4,6},{5,7},{6,4},{7,5},{8,10},{9,11},{10,... | collective-permute-start | bytes 393224 | tf_op jit(solution)/shard_map/ppermute | solution.py:320
  17.3 0.4 collective-permute-start.6
  17.9 0.5 collective-permute-done.1.refs_2_
  18.4 0.3 collective-permute-start.13
  18.7 2.3 %collective-permute-done.2.refs_3_ = bf16[512,128]{1,0:T(8,128)(2,1)S(1)} collective-permute-done((bf16[512,128]{1,0:T(8,128)(2,1)S(1)}, bf16[512,128]{1,0:T(8,128)(2,1)S(1)}, u32[]{:S(2)}, u32[]{:S(2)}) %collective-permute-start.2) | collective-permute-done | bytes 131104 | tf_op jit(solution)/shard_map/ppermute | solution.py:320
  21.1 6.9 %collective-permute-start.14 = (bf16[576,256]{1,0:T(8,128)(2,1)S(1)}, bf16[576,256]{1,0:T(8,128)(2,1)S(1)}, u32[]{:S(2)}, u32[]{:S(2)}) collective-permute-start(bf16[576,256]{1,0:T(8,128)(2,1)S(1)} %pad_maximum_fusion), channel_id=1, source_target_pairs={{0,1},{1,0},{2,3},{3,2},{4,5},{5,4},{6,7},{7,6},{8,9},{9,8},{10,11... | collective-permute-start | bytes 884744 | tf_op jit(solution)/shard_map/ppermute | solution.py:320
  28.0 1.6 %collective-permute-done.5.refs_6_ = bf16[512,128]{1,0:T(8,128)(2,1)S(1)} collective-permute-done((bf16[512,128]{1,0:T(8,128)(2,1)S(1)}, bf16[512,128]{1,0:T(8,128)(2,1)S(1)}, u32[]{:S(2)}, u32[]{:S(2)}) %collective-permute-start.5) | collective-permute-done | bytes 131104 | tf_op jit(solution)/shard_map/ppermute | solution.py:320
  29.5 2.0 %collective-permute-done.6.refs_7_ = bf16[512,128]{1,0:T(8,128)(2,1)S(1)} collective-permute-done((bf16[512,128]{1,0:T(8,128)(2,1)S(1)}, bf16[512,128]{1,0:T(8,128)(2,1)S(1)}, u32[]{:S(2)}, u32[]{:S(2)}) %collective-permute-start.6) | collective-permute-done | bytes 131104 | tf_op jit(solution)/shard_map/ppermute | solution.py:320
  31.5 1.5 %collective-permute-start.22 = (bf16[512,256]{1,0:T(8,128)(2,1)S(1)}, bf16[512,256]{1,0:T(8,128)(2,1)S(1)}, u32[]{:S(2)}, u32[]{:S(2)}) collective-permute-start(bf16[512,256]{1,0:T(8,128)(2,1)S(1)} %get-tuple-element.49.refs_15_), channel_id=1, source_target_pairs={{0,16},{8,24},{16,0},{24,8},{1,17},{9,25},{17,1},{25,9},{2,18},{10... | collective-permute-start | bytes 786440 | tf_op jit(solution)/shard_map/ppermute | solution.py:320
  33.0 2.1 %shard_map.46 = (bf16[512,256]{1,0:T(8,128)(2,1)S(1)}, bf16[512,256]{1,0:T(8,128)(2,1)S(1)}, bf16[512,256]{1,0:T(8,128)(2,1)S(1)}, bf16[512,256]{1,0:T(8,128)(2,1)S(1)}, bf16[512,256]{1,0:T(8,128)(2,1)S(1)}) custom-call(s32[5]{0:T(128)S(1)} %pad_add_fusion.1.bases_ref, s32[4,8]{1,0:T(4,128)S(1)} %convert_bitcast_fusion.keep_ref, s32[1,1024]{1,0:T(1,128)S(1)} %bitcast.51, ...), custom_call_target="tpu_custom_call" | custom-call | flops 5000000000 | bytes 1048576 | tf_op jit(solution)/shard_map/pallas_call | solution.py:406
  35.1 1.1 shard_map.47.refs_2_
  36.3 0.6 collective-permute-start.20
  36.9 1.5 %collective-permute-start.8 = (bf16[512,256]{1,0:T(8,128)(2,1)S(1)}, bf16[512,256]{1,0:T(8,128)(2,1)S(1)}, u32[]{:S(2)}, u32[]{:S(2)}) collective-permute-start(bf16[512,256]{1,0:T(8,128)(2,1)S(1)} %get-tuple-element.47.refs_2_), channel_id=1, source_target_pairs={{0,16},{8,24},{16,0},{24,8},{1,17},{9,25},{17,1},{25,9},{2,18},{10... | collective-permute-start | bytes 786440 | tf_op jit(solution)/shard_map/ppermute | solution.py:320
  38.4 1.8 %collective-permute-done.22.refs_17_ = bf16[512,256]{1,0:T(8,128)(2,1)S(1)} collective-permute-done((bf16[512,256]{1,0:T(8,128)(2,1)S(1)}, bf16[512,256]{1,0:T(8,128)(2,1)S(1)}, u32[]{:S(2)}, u32[]{:S(2)}) %collective-permute-start.22) | collective-permute-done | bytes 262176 | tf_op jit(solution)/shard_map/ppermute | solution.py:320
  40.3 2.3 %collective-permute-start.17 = (bf16[576,256]{1,0:T(8,128)(2,1)S(1)}, bf16[576,256]{1,0:T(8,128)(2,1)S(1)}, u32[]{:S(2)}, u32[]{:S(2)}) collective-permute-start(bf16[576,256]{1,0:T(8,128)(2,1)S(1)} %collective-permute-done.13), channel_id=1, source_target_pairs={{0,1},{1,0},{2,3},{3,2},{4,5},{5,4},{6,7},{7,6},{8,9},{9,8},{10,11... | collective-permute-start | bytes 884744 | tf_op jit(solution)/shard_map/ppermute | solution.py:320
  42.7 2.5 %collective-permute-done.16 = bf16[576,256]{1,0:T(8,128)(2,1)S(1)} collective-permute-done((bf16[576,256]{1,0:T(8,128)(2,1)S(1)}, bf16[576,256]{1,0:T(8,128)(2,1)S(1)}, u32[]{:S(2)}, u32[]{:S(2)}) %collective-permute-start.16) | collective-permute-done | bytes 294944 | tf_op jit(solution)/shard_map/ppermute | solution.py:320
  45.2 1.2 collective-permute-start.24
  46.5 2.6 %collective-permute-start.19 = (bf16[576,256]{1,0:T(8,128)(2,1)S(1)}, bf16[576,256]{1,0:T(8,128)(2,1)S(1)}, u32[]{:S(2)}, u32[]{:S(2)}) collective-permute-start(bf16[576,256]{1,0:T(8,128)(2,1)S(1)} %collective-permute-done.13), channel_id=1, source_target_pairs={{0,3},{1,2},{2,1},{3,0},{4,7},{5,6},{6,5},{7,4},{8,11},{9,10},{10,... | collective-permute-start | bytes 884744 | tf_op jit(solution)/shard_map/ppermute | solution.py:320
  49.1 2.4 %collective-permute-done.8.refs_4_ = bf16[512,256]{1,0:T(8,128)(2,1)S(1)} collective-permute-done((bf16[512,256]{1,0:T(8,128)(2,1)S(1)}, bf16[512,256]{1,0:T(8,128)(2,1)S(1)}, u32[]{:S(2)}, u32[]{:S(2)}) %collective-permute-start.8) | collective-permute-done | bytes 262176 | tf_op jit(solution)/shard_map/ppermute | solution.py:320
  51.5 0.5 collective-permute-start.9
  52.0 3.7 %collective-permute-done.24.refs_4_ = bf16[512,256]{1,0:T(8,128)(2,1)S(1)} collective-permute-done((bf16[512,256]{1,0:T(8,128)(2,1)S(1)}, bf16[512,256]{1,0:T(8,128)(2,1)S(1)}, u32[]{:S(2)}, u32[]{:S(2)}) %collective-permute-start.24) | collective-permute-done | bytes 262176 | tf_op jit(solution)/shard_map/ppermute | solution.py:320
  55.7 3.1 %collective-permute-done.19 = bf16[576,256]{1,0:T(8,128)(2,1)S(1)} collective-permute-done((bf16[576,256]{1,0:T(8,128)(2,1)S(1)}, bf16[576,256]{1,0:T(8,128)(2,1)S(1)}, u32[]{:S(2)}, u32[]{:S(2)}) %collective-permute-start.19) | collective-permute-done | bytes 294944 | tf_op jit(solution)/shard_map/ppermute | solution.py:320
  59.0 2.5 %collective-permute-start.26 = (bf16[576,256]{1,0:T(8,128)(2,1)S(1)}, bf16[576,256]{1,0:T(8,128)(2,1)S(1)}, u32[]{:S(2)}, u32[]{:S(2)}) collective-permute-start(bf16[576,256]{1,0:T(8,128)(2,1)S(1)} %get-tuple-element.90.refs_6_.refs_10_), channel_id=1, source_target_pairs={{0,16},{8,24},{16,0},{24,8},{1,17},{9,25},{17,1},{25,9},{2,18},{10... | collective-permute-start | bytes 884744 | tf_op jit(solution)/shard_map/ppermute | solution.py:320
  61.6 6.5 %collective-permute-done.26.refs_8_ = bf16[576,256]{1,0:T(8,128)(2,1)S(1)} collective-permute-done((bf16[576,256]{1,0:T(8,128)(2,1)S(1)}, bf16[576,256]{1,0:T(8,128)(2,1)S(1)}, u32[]{:S(2)}, u32[]{:S(2)}) %collective-permute-start.26) | collective-permute-done | bytes 294944 | tf_op jit(solution)/shard_map/ppermute | solution.py:320
  68.1 0.5 collective-permute-start.31
  68.6 1.1 collective-permute-done.27.refs_9_
  69.6 1.7 %collective-permute-start.29 = (bf16[576,256]{1,0:T(8,128)(2,1)S(1)}, bf16[576,256]{1,0:T(8,128)(2,1)S(1)}, u32[]{:S(2)}, u32[]{:S(2)}) collective-permute-start(bf16[576,256]{1,0:T(8,128)(2,1)S(1)} %get-tuple-element.52.refs_6_.refs_10_), channel_id=1, source_target_pairs={{0,16},{8,24},{16,0},{24,8},{1,17},{9,25},{17,1},{25,9},{2,18},{10... | collective-permute-start | bytes 884744 | tf_op jit(solution)/shard_map/ppermute | solution.py:320
  71.4 10.2 %shard_map.48 = (bf16[1024,256]{1,0:T(8,128)(2,1)S(1)}, f32[512,256]{1,0:T(8,128)S(1)}, f32[5,128,128]{2,1,0:T(8,128)S(1)}) custom-call(s32[6]{0:T(128)S(1)} %pad_add_fusion.refs_0_, s32[1,2048]{1,0:T(1,128)S(1)} %bitcast.46, bf16[512,256]{1,0:T(8,128)(2,1)S(1)} %shard_map.47.refs_2_, bf16[512,256]{1,0:T(8,128)(2,1)S(1)} %collective-permute-done.30.refs_3_, ...), custom_call_target="tpu_custom_call" | custom-call | flops 15000000512 | bytes 4194304 | tf_op jit(solution)/shard_map/pallas_call | solution.py:492
  81.7 0.6 collective-permute-start.32
  82.3 0.4 collective-permute-start.33
  82.8 1.0 collective-permute-done.34.refs_16_
  83.8 0.7 collective-permute-start.38
  84.5 1.4 collective-permute-start.41
  85.9 12.9 %shard_map.49 = (bf16[768,256]{1,0:T(8,128)(2,1)S(1)}, f32[512,256]{1,0:T(8,128)S(1)}, f32[5,128,128]{2,1,0:T(8,128)S(1)}, bf16[512,256]{1,0:T(8,128)(2,1)S(1)},...) custom-call(s32[6]{0:T(128)S(1)} %pad_add_fusion.refs_0_, s32[1,2048]{1,0:T(1,128)S(1)} %bitcast.47, ...), custom_call_target="tpu_custom_call" | custom-call | flops 15000000512 | bytes 4194304 | tf_op jit(solution)/shard_map/pallas_call | solution.py:492
  98.8 0.6 collective-permute-start.42
  99.4 0.4 collective-permute-start.39
  99.9 0.6 collective-permute-start.47
  100.5 0.4 collective-permute-done.37.refs_3_
  100.9 1.0 collective-permute-start.50
  101.9 12.3 %shard_map.50 = (bf16[512,256]{1,0:T(8,128)(2,1)S(1)}, f32[512,256]{1,0:T(8,128)S(1)}, f32[5,128,128]{2,1,0:T(8,128)S(1)}, bf16[512,256]{1,0:T(8,128)(2,1)S(1)},...) custom-call(s32[6]{0:T(128)S(1)} %pad_add_fusion.refs_0_, s32[1,2048]{1,0:T(1,128)S(1)} %bitcast.48, ...), custom_call_target="tpu_custom_call" | custom-call | flops 15000000512 | bytes 4194304 | tf_op jit(solution)/shard_map/pallas_call | solution.py:492
  114.3 0.2 collective-permute-done.50.refs_8_
  114.5 0.3 collective-permute-start.51
  115.0 0.3 collective-permute-start.48
  115.3 1.1 collective-permute-start.36
  116.4 1.0 collective-permute-start.45
  117.6 11.7 %shard_map.51 = (bf16[256,256]{1,0:T(8,128)(2,1)S(1)}, f32[512,256]{1,0:T(8,128)S(1)}, f32[5,128,128]{2,1,0:T(8,128)S(1)}, bf16[512,256]{1,0:T(8,128)(2,1)S(1)},...) custom-call(s32[6]{0:T(128)S(1)} %pad_add_fusion.refs_0_, s32[1,2048]{1,0:T(1,128)S(1)} %bitcast.49, ...), custom_call_target="tpu_custom_call" | custom-call | flops 15000000512 | bytes 4194304 | tf_op jit(solution)/shard_map/pallas_call | solution.py:492
  129.3 0.7 collective-permute-done.45.refs_8_
  130.0 0.5 collective-permute-start.35
  130.6 1.4 collective-permute-done.35.refs_3_
  132.0 0.4 collective-permute-done.43.refs_5_
  132.4 14.2 %shard_map.52 = f32[512,256]{1,0:T(8,128)} custom-call(s32[6]{0:T(128)S(1)} %pad_add_fusion.refs_0_, s32[1,2048]{1,0:T(1,128)S(1)} %bitcast.50, bf16[512,256]{1,0:T(8,128)(2,1)S(1)} %get-tuple-element.58.refs_2_, bf16[512,256]{1,0:T(8,128)(2,1)S(1)} %collective-permute-done.35.refs_3_, bf16[512,256]{1,0:T(8,128)(2,1)S(1)} %collective-permute-done.36.refs_4_, ...), custom_call_target="tpu_custom_call" | custom-call | flops 15000000512 | bytes 4194304 | tf_op jit(solution)/shard_map/pallas_call | solution.py:492
  (93 shorter events, 1.8 us)
Async XLA Ops:
  0.0 12.0 %copy-start.1 = (bf16[512,128]{1,0:T(8,128)(2,1)S(1)}, bf16[512,128]{1,0:T(8,128)(2,1)}, u32[]{:S(2)}) copy-start(bf16[512,128]{1,0:T(8,128)(2,1)} %refs_0_.3) | copy-start | bytes 393220
  0.0 9.7 %copy-start.3 = (s32[2,8,8]{2,1,0:T(8,128)S(1)}, s32[2,8,8]{2,1,0:T(8,128)}, u32[]{:S(2)}) copy-start(s32[2,8,8]{2,1,0:T(8,128)} %param.7) | copy-start | bytes 1540
  0.0 10.5 %copy-start.2 = (s32[2,1024]{1,0:T(2,128)S(1)}, s32[2,1024]{1,0:T(2,128)}, u32[]{:S(2)}) copy-start(s32[2,1024]{1,0:T(2,128)} %param.6) | copy-start | bytes 24580
  0.0 14.1 %collective-permute-start.3 = (bf16[512,128]{1,0:T(8,128)(2,1)}, bf16[512,128]{1,0:T(8,128)(2,1)S(1)}, u32[]{:S(2)}, u32[]{:S(2)}) collective-permute-start(bf16[512,128]{1,0:T(8,128)(2,1)} %refs_0_.3), channel_id=1, source_target_pairs={{0,4},{1,5},{2,6},{3,7},{4,0},{5,1},{6,2},{7,3},{8,12},{9,13},{10,... | collective-permute-start | bytes 393224 | tf_op jit(solution)/shard_map/ppermute | solution.py:320
  4.1 13.1 %collective-permute-start = (bf16[512,128]{1,0:T(8,128)(2,1)}, bf16[512,128]{1,0:T(8,128)(2,1)S(1)}, u32[]{:S(2)}, u32[]{:S(2)}) collective-permute-start(bf16[512,128]{1,0:T(8,128)(2,1)} %refs_0_.3), channel_id=1, source_target_pairs={{0,1},{1,0},{2,3},{3,2},{4,5},{5,4},{6,7},{7,6},{8,9},{9,8},{10,11... | collective-permute-start | bytes 393224 | tf_op jit(solution)/shard_map/ppermute | solution.py:320
  7.7 4.3 %collective-permute-start.10 = (bf16[64,256]{1,0:T(8,128)(2,1)S(1)}, bf16[64,256]{1,0:T(8,128)(2,1)S(1)}, u32[]{:S(2)}, u32[]{:S(2)}) collective-permute-start(bf16[64,256]{1,0:T(8,128)(2,1)S(1)} %get-tuple-element.96), channel_id=1, source_target_pairs={{0,24},{8,16},{16,8},{24,0},{1,25},{9,17},{17,9},{25,1},{2,26},{10... | collective-permute-start | bytes 98312 | tf_op jit(solution)/shard_map/ppermute | solution.py:320
  8.2 5.5 %collective-permute-start.11 = (bf16[64,256]{1,0:T(8,128)(2,1)S(1)}, bf16[64,256]{1,0:T(8,128)(2,1)S(1)}, u32[]{:S(2)}, u32[]{:S(2)}) collective-permute-start(bf16[64,256]{1,0:T(8,128)(2,1)S(1)} %get-tuple-element.95), channel_id=1, source_target_pairs={{0,16},{8,24},{16,0},{24,8},{1,17},{9,25},{17,1},{25,9},{2,18},{10... | collective-permute-start | bytes 98312 | tf_op jit(solution)/shard_map/ppermute | solution.py:320
  9.4 4.7 %collective-permute-start.12 = (bf16[64,256]{1,0:T(8,128)(2,1)S(1)}, bf16[64,256]{1,0:T(8,128)(2,1)S(1)}, u32[]{:S(2)}, u32[]{:S(2)}) collective-permute-start(bf16[64,256]{1,0:T(8,128)(2,1)S(1)} %get-tuple-element.94), channel_id=1, source_target_pairs={{0,8},{8,0},{16,24},{24,16},{1,9},{9,1},{17,25},{25,17},{2,10},{10... | collective-permute-start | bytes 98312 | tf_op jit(solution)/shard_map/ppermute | solution.py:320
  12.0 6.4 %collective-permute-start.1 = (bf16[512,128]{1,0:T(8,128)(2,1)S(1)}, bf16[512,128]{1,0:T(8,128)(2,1)S(1)}, u32[]{:S(2)}, u32[]{:S(2)}) collective-permute-start(bf16[512,128]{1,0:T(8,128)(2,1)S(1)} %copy-done.1), channel_id=1, source_target_pairs={{0,2},{1,3},{2,0},{3,1},{4,6},{5,7},{6,4},{7,5},{8,10},{9,11},{10,... | collective-permute-start | bytes 393224 | tf_op jit(solution)/shard_map/ppermute | solution.py:320
  13.7 7.4 %collective-permute-start.2 = (bf16[512,128]{1,0:T(8,128)(2,1)S(1)}, bf16[512,128]{1,0:T(8,128)(2,1)S(1)}, u32[]{:S(2)}, u32[]{:S(2)}) collective-permute-start(bf16[512,128]{1,0:T(8,128)(2,1)S(1)} %copy-done.1), channel_id=1, source_target_pairs={{0,3},{1,2},{2,1},{3,0},{4,7},{5,6},{6,5},{7,4},{8,11},{9,10},{10,... | collective-permute-start | bytes 393224 | tf_op jit(solution)/shard_map/ppermute | solution.py:320
  14.1 13.8 %collective-permute-start.4 = (bf16[512,128]{1,0:T(8,128)(2,1)S(1)}, bf16[512,128]{1,0:T(8,128)(2,1)S(1)}, u32[]{:S(2)}, u32[]{:S(2)}) collective-permute-start(bf16[512,128]{1,0:T(8,128)(2,1)S(1)} %collective-permute-done.3.refs_4_), channel_id=1, source_target_pairs={{0,1},{1,0},{2,3},{3,2},{4,5},{5,4},{6,7},{7,6},{8,9},{9,8},{10,11... | collective-permute-start | bytes 393224 | tf_op jit(solution)/shard_map/ppermute | solution.py:320
  15.7 13.8 %collective-permute-start.5 = (bf16[512,128]{1,0:T(8,128)(2,1)S(1)}, bf16[512,128]{1,0:T(8,128)(2,1)S(1)}, u32[]{:S(2)}, u32[]{:S(2)}) collective-permute-start(bf16[512,128]{1,0:T(8,128)(2,1)S(1)} %collective-permute-done.3.refs_4_), channel_id=1, source_target_pairs={{0,2},{1,3},{2,0},{3,1},{4,6},{5,7},{6,4},{7,5},{8,10},{9,11},{10,... | collective-permute-start | bytes 393224 | tf_op jit(solution)/shard_map/ppermute | solution.py:320
  17.3 14.3 %collective-permute-start.6 = (bf16[512,128]{1,0:T(8,128)(2,1)S(1)}, bf16[512,128]{1,0:T(8,128)(2,1)S(1)}, u32[]{:S(2)}, u32[]{:S(2)}) collective-permute-start(bf16[512,128]{1,0:T(8,128)(2,1)S(1)} %collective-permute-done.3.refs_4_), channel_id=1, source_target_pairs={{0,3},{1,2},{2,1},{3,0},{4,7},{5,6},{6,5},{7,4},{8,11},{9,10},{10,... | collective-permute-start | bytes 393224 | tf_op jit(solution)/shard_map/ppermute | solution.py:320
  18.4 17.8 %collective-permute-start.13 = (bf16[576,256]{1,0:T(8,128)(2,1)S(1)}, bf16[576,256]{1,0:T(8,128)(2,1)S(1)}, u32[]{:S(2)}, u32[]{:S(2)}) collective-permute-start(bf16[576,256]{1,0:T(8,128)(2,1)S(1)} %pad_maximum_fusion), channel_id=1, source_target_pairs={{0,4},{1,5},{2,6},{3,7},{4,0},{5,1},{6,2},{7,3},{8,12},{9,13},{10,... | collective-permute-start | bytes 884744 | tf_op jit(solution)/shard_map/ppermute | solution.py:320
  21.1 15.8 %collective-permute-start.14 = (bf16[576,256]{1,0:T(8,128)(2,1)S(1)}, bf16[576,256]{1,0:T(8,128)(2,1)S(1)}, u32[]{:S(2)}, u32[]{:S(2)}) collective-permute-start(bf16[576,256]{1,0:T(8,128)(2,1)S(1)} %pad_maximum_fusion), channel_id=1, source_target_pairs={{0,1},{1,0},{2,3},{3,2},{4,5},{5,4},{6,7},{7,6},{8,9},{9,8},{10,11... | collective-permute-start | bytes 884744 | tf_op jit(solution)/shard_map/ppermute | solution.py:320
  27.9 12.3 %collective-permute-start.15 = (bf16[576,256]{1,0:T(8,128)(2,1)S(1)}, bf16[576,256]{1,0:T(8,128)(2,1)S(1)}, u32[]{:S(2)}, u32[]{:S(2)}) collective-permute-start(bf16[576,256]{1,0:T(8,128)(2,1)S(1)} %pad_maximum_fusion), channel_id=1, source_target_pairs={{0,2},{1,3},{2,0},{3,1},{4,6},{5,7},{6,4},{7,5},{8,10},{9,11},{10,... | collective-permute-start | bytes 884744 | tf_op jit(solution)/shard_map/ppermute | solution.py:320
  29.5 15.7 %collective-permute-start.16 = (bf16[576,256]{1,0:T(8,128)(2,1)S(1)}, bf16[576,256]{1,0:T(8,128)(2,1)S(1)}, u32[]{:S(2)}, u32[]{:S(2)}) collective-permute-start(bf16[576,256]{1,0:T(8,128)(2,1)S(1)} %pad_maximum_fusion), channel_id=1, source_target_pairs={{0,3},{1,2},{2,1},{3,0},{4,7},{5,6},{6,5},{7,4},{8,11},{9,10},{10,... | collective-permute-start | bytes 884744 | tf_op jit(solution)/shard_map/ppermute | solution.py:320
  31.5 8.7 %collective-permute-start.22 = (bf16[512,256]{1,0:T(8,128)(2,1)S(1)}, bf16[512,256]{1,0:T(8,128)(2,1)S(1)}, u32[]{:S(2)}, u32[]{:S(2)}) collective-permute-start(bf16[512,256]{1,0:T(8,128)(2,1)S(1)} %get-tuple-element.49.refs_15_), channel_id=1, source_target_pairs={{0,16},{8,24},{16,0},{24,8},{1,17},{9,25},{17,1},{25,9},{2,18},{10... | collective-permute-start | bytes 786440 | tf_op jit(solution)/shard_map/ppermute | solution.py:320
  36.3 10.2 %collective-permute-start.20 = (bf16[512,256]{1,0:T(8,128)(2,1)S(1)}, bf16[512,256]{1,0:T(8,128)(2,1)S(1)}, u32[]{:S(2)}, u32[]{:S(2)}) collective-permute-start(bf16[512,256]{1,0:T(8,128)(2,1)S(1)} %get-tuple-element.48.refs_11_), channel_id=1, source_target_pairs={{0,16},{8,24},{16,0},{24,8},{1,17},{9,25},{17,1},{25,9},{2,18},{10... | collective-permute-start | bytes 786440 | tf_op jit(solution)/shard_map/ppermute | solution.py:320
  36.9 14.6 %collective-permute-start.8 = (bf16[512,256]{1,0:T(8,128)(2,1)S(1)}, bf16[512,256]{1,0:T(8,128)(2,1)S(1)}, u32[]{:S(2)}, u32[]{:S(2)}) collective-permute-start(bf16[512,256]{1,0:T(8,128)(2,1)S(1)} %get-tuple-element.47.refs_2_), channel_id=1, source_target_pairs={{0,16},{8,24},{16,0},{24,8},{1,17},{9,25},{17,1},{25,9},{2,18},{10... | collective-permute-start | bytes 786440 | tf_op jit(solution)/shard_map/ppermute | solution.py:320
  40.2 2.4 %collective-permute-start.23 = (bf16[512,256]{1,0:T(8,128)(2,1)S(1)}, bf16[512,256]{1,0:T(8,128)(2,1)S(1)}, u32[]{:S(2)}, u32[]{:S(2)}) collective-permute-start(bf16[512,256]{1,0:T(8,128)(2,1)S(1)} %collective-permute-done.22.refs_17_), channel_id=1, source_target_pairs={{0,8},{8,0},{16,24},{24,16},{1,9},{9,1},{17,25},{25,17},{2,10},{10... | collective-permute-start | bytes 786440 | tf_op jit(solution)/shard_map/ppermute | solution.py:320
  40.3 11.2 %collective-permute-start.17 = (bf16[576,256]{1,0:T(8,128)(2,1)S(1)}, bf16[576,256]{1,0:T(8,128)(2,1)S(1)}, u32[]{:S(2)}, u32[]{:S(2)}) collective-permute-start(bf16[576,256]{1,0:T(8,128)(2,1)S(1)} %collective-permute-done.13), channel_id=1, source_target_pairs={{0,1},{1,0},{2,3},{3,2},{4,5},{5,4},{6,7},{7,6},{8,9},{9,8},{10,11... | collective-permute-start | bytes 884744 | tf_op jit(solution)/shard_map/ppermute | solution.py:320
  42.7 13.0 %collective-permute-start.18 = (bf16[576,256]{1,0:T(8,128)(2,1)S(1)}, bf16[576,256]{1,0:T(8,128)(2,1)S(1)}, u32[]{:S(2)}, u32[]{:S(2)}) collective-permute-start(bf16[576,256]{1,0:T(8,128)(2,1)S(1)} %collective-permute-done.13), channel_id=1, source_target_pairs={{0,2},{1,3},{2,0},{3,1},{4,6},{5,7},{6,4},{7,5},{8,10},{9,11},{10,... | collective-permute-start | bytes 884744 | tf_op jit(solution)/shard_map/ppermute | solution.py:320
  45.2 10.4 %collective-permute-start.24 = (bf16[512,256]{1,0:T(8,128)(2,1)S(1)}, bf16[512,256]{1,0:T(8,128)(2,1)S(1)}, u32[]{:S(2)}, u32[]{:S(2)}) collective-permute-start(bf16[512,256]{1,0:T(8,128)(2,1)S(1)} %shard_map.47.refs_2_), channel_id=1, source_target_pairs={{0,16},{8,24},{16,0},{24,8},{1,17},{9,25},{17,1},{25,9},{2,18},{10... | collective-permute-start | bytes 786440 | tf_op jit(solution)/shard_map/ppermute | solution.py:320
  46.5 12.4 %collective-permute-start.19 = (bf16[576,256]{1,0:T(8,128)(2,1)S(1)}, bf16[576,256]{1,0:T(8,128)(2,1)S(1)}, u32[]{:S(2)}, u32[]{:S(2)}) collective-permute-start(bf16[576,256]{1,0:T(8,128)(2,1)S(1)} %collective-permute-done.13), channel_id=1, source_target_pairs={{0,3},{1,2},{2,1},{3,0},{4,7},{5,6},{6,5},{7,4},{8,11},{9,10},{10,... | collective-permute-start | bytes 884744 | tf_op jit(solution)/shard_map/ppermute | solution.py:320
  51.5 7.4 %collective-permute-start.21 = (bf16[512,256]{1,0:T(8,128)(2,1)S(1)}, bf16[512,256]{1,0:T(8,128)(2,1)S(1)}, u32[]{:S(2)}, u32[]{:S(2)}) collective-permute-start(bf16[512,256]{1,0:T(8,128)(2,1)S(1)} %collective-permute-done.20.refs_13_), channel_id=1, source_target_pairs={{0,8},{8,0},{16,24},{24,16},{1,9},{9,1},{17,25},{25,17},{2,10},{10... | collective-permute-start | bytes 786440 | tf_op jit(solution)/shard_map/ppermute | solution.py:320
  51.5 7.4 %collective-permute-start.9 = (bf16[512,256]{1,0:T(8,128)(2,1)S(1)}, bf16[512,256]{1,0:T(8,128)(2,1)S(1)}, u32[]{:S(2)}, u32[]{:S(2)}) collective-permute-start(bf16[512,256]{1,0:T(8,128)(2,1)S(1)} %collective-permute-done.8.refs_4_), channel_id=1, source_target_pairs={{0,8},{8,0},{16,24},{24,16},{1,9},{9,1},{17,25},{25,17},{2,10},{10... | collective-permute-start | bytes 786440 | tf_op jit(solution)/shard_map/ppermute | solution.py:320
  55.7 3.2 %collective-permute-start.25 = (bf16[512,256]{1,0:T(8,128)(2,1)S(1)}, bf16[512,256]{1,0:T(8,128)(2,1)S(1)}, u32[]{:S(2)}, u32[]{:S(2)}) collective-permute-start(bf16[512,256]{1,0:T(8,128)(2,1)S(1)} %collective-permute-done.24.refs_4_), channel_id=1, source_target_pairs={{0,8},{8,0},{16,24},{24,16},{1,9},{9,1},{17,25},{25,17},{2,10},{10... | collective-permute-start | bytes 786440 | tf_op jit(solution)/shard_map/ppermute | solution.py:320
  59.0 9.0 %collective-permute-start.26 = (bf16[576,256]{1,0:T(8,128)(2,1)S(1)}, bf16[576,256]{1,0:T(8,128)(2,1)S(1)}, u32[]{:S(2)}, u32[]{:S(2)}) collective-permute-start(bf16[576,256]{1,0:T(8,128)(2,1)S(1)} %get-tuple-element.90.refs_6_.refs_10_), channel_id=1, source_target_pairs={{0,16},{8,24},{16,0},{24,8},{1,17},{9,25},{17,1},{25,9},{2,18},{10... | collective-permute-start | bytes 884744 | tf_op jit(solution)/shard_map/ppermute | solution.py:320
  68.1 1.6 %collective-permute-start.27 = (bf16[576,256]{1,0:T(8,128)(2,1)S(1)}, bf16[576,256]{1,0:T(8,128)(2,1)S(1)}, u32[]{:S(2)}, u32[]{:S(2)}) collective-permute-start(bf16[576,256]{1,0:T(8,128)(2,1)S(1)} %collective-permute-done.26.refs_8_), channel_id=1, source_target_pairs={{0,8},{8,0},{16,24},{24,16},{1,9},{9,1},{17,25},{25,17},{2,10},{10... | collective-permute-start | bytes 884744 | tf_op jit(solution)/shard_map/ppermute | solution.py:320
  68.1 3.3 %collective-permute-start.31 = (bf16[576,256]{1,0:T(8,128)(2,1)S(1)}, bf16[576,256]{1,0:T(8,128)(2,1)S(1)}, u32[]{:S(2)}, u32[]{:S(2)}) collective-permute-start(bf16[576,256]{1,0:T(8,128)(2,1)S(1)} %get-tuple-element.90.refs_6_.refs_10_), channel_id=1, source_target_pairs={{0,8},{8,0},{16,24},{24,16},{1,9},{9,1},{17,25},{25,17},{2,10},{10... | collective-permute-start | bytes 884744 | tf_op jit(solution)/shard_map/ppermute | solution.py:320
  68.6 2.8 %collective-permute-start.30 = (bf16[512,256]{1,0:T(8,128)(2,1)S(1)}, bf16[512,256]{1,0:T(8,128)(2,1)S(1)}, u32[]{:S(2)}, u32[]{:S(2)}) collective-permute-start(bf16[512,256]{1,0:T(8,128)(2,1)S(1)} %shard_map.47.refs_2_), channel_id=1, source_target_pairs={{0,8},{8,0},{16,24},{24,16},{1,9},{9,1},{17,25},{25,17},{2,10},{10... | collective-permute-start | bytes 786440 | tf_op jit(solution)/shard_map/ppermute | solution.py:320
  69.6 16.2 %copy-start = (f32[512,256]{1,0:T(8,128)S(1)}, f32[512,256]{1,0:T(8,128)}, u32[]{:S(2)}) copy-start(f32[512,256]{1,0:T(8,128)} %refs_21_.1) | copy-start | bytes 1572868
  69.6 12.0 %collective-permute-start.29 = (bf16[576,256]{1,0:T(8,128)(2,1)S(1)}, bf16[576,256]{1,0:T(8,128)(2,1)S(1)}, u32[]{:S(2)}, u32[]{:S(2)}) collective-permute-start(bf16[576,256]{1,0:T(8,128)(2,1)S(1)} %get-tuple-element.52.refs_6_.refs_10_), channel_id=1, source_target_pairs={{0,16},{8,24},{16,0},{24,8},{1,17},{9,25},{17,1},{25,9},{2,18},{10... | collective-permute-start | bytes 884744 | tf_op jit(solution)/shard_map/ppermute | solution.py:320
  71.4 14.5 %collective-permute-start.28 = (bf16[576,256]{1,0:T(8,128)(2,1)S(1)}, bf16[576,256]{1,0:T(8,128)(2,1)S(1)}, u32[]{:S(2)}, u32[]{:S(2)}) collective-permute-start(bf16[576,256]{1,0:T(8,128)(2,1)S(1)} %get-tuple-element.52.refs_6_.refs_10_), channel_id=1, source_target_pairs={{0,8},{8,0},{16,24},{24,16},{1,9},{9,1},{17,25},{25,17},{2,10},{10... | collective-permute-start | bytes 884744 | tf_op jit(solution)/shard_map/ppermute | solution.py:320
  81.7 4.2 %collective-permute-start.32 = (bf16[576,256]{1,0:T(8,128)(2,1)S(1)}, bf16[576,256]{1,0:T(8,128)(2,1)S(1)}, u32[]{:S(2)}, u32[]{:S(2)}) collective-permute-start(bf16[576,256]{1,0:T(8,128)(2,1)S(1)} %collective-permute-done.29.refs_8_), channel_id=1, source_target_pairs={{0,8},{8,0},{16,24},{24,16},{1,9},{9,1},{17,25},{25,17},{2,10},{10... | collective-permute-start | bytes 884744 | tf_op jit(solution)/shard_map/ppermute | solution.py:320
  82.2 1.6 %collective-permute-start.34 = (bf16[512,256]{1,0:T(8,128)(2,1)S(1)}, bf16[512,256]{1,0:T(8,128)(2,1)S(1)}, u32[]{:S(2)}, u32[]{:S(2)}) collective-permute-start(bf16[512,256]{1,0:T(8,128)(2,1)S(1)} %get-tuple-element.49.refs_15_), channel_id=1, source_target_pairs={{0,8},{8,0},{16,24},{24,16},{1,9},{9,1},{17,25},{25,17},{2,10},{10... | collective-permute-start | bytes 786440 | tf_op jit(solution)/shard_map/ppermute | solution.py:320
  82.3 2.2 %collective-permute-start.33 = (bf16[512,256]{1,0:T(8,128)(2,1)S(1)}, bf16[512,256]{1,0:T(8,128)(2,1)S(1)}, u32[]{:S(2)}, u32[]{:S(2)}) collective-permute-start(bf16[512,256]{1,0:T(8,128)(2,1)S(1)} %get-tuple-element.48.refs_11_), channel_id=1, source_target_pairs={{0,8},{8,0},{16,24},{24,16},{1,9},{9,1},{17,25},{25,17},{2,10},{10... | collective-permute-start | bytes 786440 | tf_op jit(solution)/shard_map/ppermute | solution.py:320
  82.7 3.1 %collective-permute-start.7 = (bf16[512,256]{1,0:T(8,128)(2,1)S(1)}, bf16[512,256]{1,0:T(8,128)(2,1)S(1)}, u32[]{:S(2)}, u32[]{:S(2)}) collective-permute-start(bf16[512,256]{1,0:T(8,128)(2,1)S(1)} %get-tuple-element.47.refs_2_), channel_id=1, source_target_pairs={{0,8},{8,0},{16,24},{24,16},{1,9},{9,1},{17,25},{25,17},{2,10},{10... | collective-permute-start | bytes 786440 | tf_op jit(solution)/shard_map/ppermute | solution.py:320
  83.8 15.6 %collective-permute-start.38 = (bf16[512,256]{1,0:T(8,128)(2,1)S(1)}, bf16[512,256]{1,0:T(8,128)(2,1)S(1)}, u32[]{:S(2)}, u32[]{:S(2)}) collective-permute-start(bf16[512,256]{1,0:T(8,128)(2,1)S(1)} %get-tuple-element.59.refs_2_), channel_id=1, source_target_pairs={{0,16},{8,24},{16,0},{24,8},{1,17},{9,25},{17,1},{25,9},{2,18},{10... | collective-permute-start | bytes 786440 | tf_op jit(solution)/shard_map/ppermute | solution.py:320
  84.5 14.3 %collective-permute-start.41 = (bf16[576,256]{1,0:T(8,128)(2,1)S(1)}, bf16[576,256]{1,0:T(8,128)(2,1)S(1)}, u32[]{:S(2)}, u32[]{:S(2)}) collective-permute-start(bf16[576,256]{1,0:T(8,128)(2,1)S(1)} %get-tuple-element.60.refs_6_.refs_10_), channel_id=1, source_target_pairs={{0,16},{8,24},{16,0},{24,8},{1,17},{9,25},{17,1},{25,9},{2,18},{10... | collective-permute-start | bytes 884744 | tf_op jit(solution)/shard_map/ppermute | solution.py:320
  85.9 16.1 %collective-permute-start.40 = (bf16[576,256]{1,0:T(8,128)(2,1)S(1)}, bf16[576,256]{1,0:T(8,128)(2,1)S(1)}, u32[]{:S(2)}, u32[]{:S(2)}) collective-permute-start(bf16[576,256]{1,0:T(8,128)(2,1)S(1)} %get-tuple-element.60.refs_6_.refs_10_), channel_id=1, source_target_pairs={{0,8},{8,0},{16,24},{24,16},{1,9},{9,1},{17,25},{25,17},{2,10},{10... | collective-permute-start | bytes 884744 | tf_op jit(solution)/shard_map/ppermute | solution.py:320
  98.8 3.1 %collective-permute-start.42 = (bf16[576,256]{1,0:T(8,128)(2,1)S(1)}, bf16[576,256]{1,0:T(8,128)(2,1)S(1)}, u32[]{:S(2)}, u32[]{:S(2)}) collective-permute-start(bf16[576,256]{1,0:T(8,128)(2,1)S(1)} %collective-permute-done.41.refs_8_), channel_id=1, source_target_pairs={{0,8},{8,0},{16,24},{24,16},{1,9},{9,1},{17,25},{25,17},{2,10},{10... | collective-permute-start | bytes 884744 | tf_op jit(solution)/shard_map/ppermute | solution.py:320
  99.4 1.6 %collective-permute-start.37 = (bf16[512,256]{1,0:T(8,128)(2,1)S(1)}, bf16[512,256]{1,0:T(8,128)(2,1)S(1)}, u32[]{:S(2)}, u32[]{:S(2)}) collective-permute-start(bf16[512,256]{1,0:T(8,128)(2,1)S(1)} %get-tuple-element.59.refs_2_), channel_id=1, source_target_pairs={{0,8},{8,0},{16,24},{24,16},{1,9},{9,1},{17,25},{25,17},{2,10},{10... | collective-permute-start | bytes 786440 | tf_op jit(solution)/shard_map/ppermute | solution.py:320
  99.4 2.5 %collective-permute-start.39 = (bf16[512,256]{1,0:T(8,128)(2,1)S(1)}, bf16[512,256]{1,0:T(8,128)(2,1)S(1)}, u32[]{:S(2)}, u32[]{:S(2)}) collective-permute-start(bf16[512,256]{1,0:T(8,128)(2,1)S(1)} %collective-permute-done.38.refs_4_), channel_id=1, source_target_pairs={{0,8},{8,0},{16,24},{24,16},{1,9},{9,1},{17,25},{25,17},{2,10},{10... | collective-permute-start | bytes 786440 | tf_op jit(solution)/shard_map/ppermute | solution.py:320
  99.9 15.1 %collective-permute-start.47 = (bf16[512,256]{1,0:T(8,128)(2,1)S(1)}, bf16[512,256]{1,0:T(8,128)(2,1)S(1)}, u32[]{:S(2)}, u32[]{:S(2)}) collective-permute-start(bf16[512,256]{1,0:T(8,128)(2,1)S(1)} %get-tuple-element.71.refs_2_), channel_id=1, source_target_pairs={{0,16},{8,24},{16,0},{24,8},{1,17},{9,25},{17,1},{25,9},{2,18},{10... | collective-permute-start | bytes 786440 | tf_op jit(solution)/shard_map/ppermute | solution.py:320
  100.9 13.5 %collective-permute-start.50 = (bf16[576,256]{1,0:T(8,128)(2,1)S(1)}, bf16[576,256]{1,0:T(8,128)(2,1)S(1)}, u32[]{:S(2)}, u32[]{:S(2)}) collective-permute-start(bf16[576,256]{1,0:T(8,128)(2,1)S(1)} %get-tuple-element.73.refs_6_.refs_10_), channel_id=1, source_target_pairs={{0,16},{8,24},{16,0},{24,8},{1,17},{9,25},{17,1},{25,9},{2,18},{10... | collective-permute-start | bytes 884744 | tf_op jit(solution)/shard_map/ppermute | solution.py:320
  101.9 15.7 %collective-permute-start.49 = (bf16[576,256]{1,0:T(8,128)(2,1)S(1)}, bf16[576,256]{1,0:T(8,128)(2,1)S(1)}, u32[]{:S(2)}, u32[]{:S(2)}) collective-permute-start(bf16[576,256]{1,0:T(8,128)(2,1)S(1)} %get-tuple-element.73.refs_6_.refs_10_), channel_id=1, source_target_pairs={{0,8},{8,0},{16,24},{24,16},{1,9},{9,1},{17,25},{25,17},{2,10},{10... | collective-permute-start | bytes 884744 | tf_op jit(solution)/shard_map/ppermute | solution.py:320
  114.5 3.1 %collective-permute-start.51 = (bf16[576,256]{1,0:T(8,128)(2,1)S(1)}, bf16[576,256]{1,0:T(8,128)(2,1)S(1)}, u32[]{:S(2)}, u32[]{:S(2)}) collective-permute-start(bf16[576,256]{1,0:T(8,128)(2,1)S(1)} %collective-permute-done.50.refs_8_), channel_id=1, source_target_pairs={{0,8},{8,0},{16,24},{24,16},{1,9},{9,1},{17,25},{25,17},{2,10},{10... | collective-permute-start | bytes 884744 | tf_op jit(solution)/shard_map/ppermute | solution.py:320
  114.8 1.6 %collective-permute-start.46 = (bf16[512,256]{1,0:T(8,128)(2,1)S(1)}, bf16[512,256]{1,0:T(8,128)(2,1)S(1)}, u32[]{:S(2)}, u32[]{:S(2)}) collective-permute-start(bf16[512,256]{1,0:T(8,128)(2,1)S(1)} %get-tuple-element.71.refs_2_), channel_id=1, source_target_pairs={{0,8},{8,0},{16,24},{24,16},{1,9},{9,1},{17,25},{25,17},{2,10},{10... | collective-permute-start | bytes 786440 | tf_op jit(solution)/shard_map/ppermute | solution.py:320
  115.0 2.5 %collective-permute-start.48 = (bf16[512,256]{1,0:T(8,128)(2,1)S(1)}, bf16[512,256]{1,0:T(8,128)(2,1)S(1)}, u32[]{:S(2)}, u32[]{:S(2)}) collective-permute-start(bf16[512,256]{1,0:T(8,128)(2,1)S(1)} %collective-permute-done.47.refs_4_), channel_id=1, source_target_pairs={{0,8},{8,0},{16,24},{24,16},{1,9},{9,1},{17,25},{25,17},{2,10},{10... | collective-permute-start | bytes 786440 | tf_op jit(solution)/shard_map/ppermute | solution.py:320
  115.3 15.2 %collective-permute-start.36 = (bf16[512,256]{1,0:T(8,128)(2,1)S(1)}, bf16[512,256]{1,0:T(8,128)(2,1)S(1)}, u32[]{:S(2)}, u32[]{:S(2)}) collective-permute-start(bf16[512,256]{1,0:T(8,128)(2,1)S(1)} %get-tuple-element.58.refs_2_), channel_id=1, source_target_pairs={{0,16},{8,24},{16,0},{24,8},{1,17},{9,25},{17,1},{25,9},{2,18},{10... | collective-permute-start | bytes 786440 | tf_op jit(solution)/shard_map/ppermute | solution.py:320
  116.4 13.6 %collective-permute-start.45 = (bf16[576,256]{1,0:T(8,128)(2,1)S(1)}, bf16[576,256]{1,0:T(8,128)(2,1)S(1)}, u32[]{:S(2)}, u32[]{:S(2)}) collective-permute-start(bf16[576,256]{1,0:T(8,128)(2,1)S(1)} %get-tuple-element.69.refs_6_.refs_10_), channel_id=1, source_target_pairs={{0,16},{8,24},{16,0},{24,8},{1,17},{9,25},{17,1},{25,9},{2,18},{10... | collective-permute-start | bytes 884744 | tf_op jit(solution)/shard_map/ppermute | solution.py:320
  117.5 14.9 %collective-permute-start.44 = (bf16[576,256]{1,0:T(8,128)(2,1)S(1)}, bf16[576,256]{1,0:T(8,128)(2,1)S(1)}, u32[]{:S(2)}, u32[]{:S(2)}) collective-permute-start(bf16[576,256]{1,0:T(8,128)(2,1)S(1)} %get-tuple-element.69.refs_6_.refs_10_), channel_id=1, source_target_pairs={{0,8},{8,0},{16,24},{24,16},{1,9},{9,1},{17,25},{25,17},{2,10},{10... | collective-permute-start | bytes 884744 | tf_op jit(solution)/shard_map/ppermute | solution.py:320
  130.0 2.3 %collective-permute-start.52 = (bf16[576,256]{1,0:T(8,128)(2,1)S(1)}, bf16[576,256]{1,0:T(8,128)(2,1)S(1)}, u32[]{:S(2)}, u32[]{:S(2)}) collective-permute-start(bf16[576,256]{1,0:T(8,128)(2,1)S(1)} %collective-permute-done.45.refs_8_), channel_id=1, source_target_pairs={{0,8},{8,0},{16,24},{24,16},{1,9},{9,1},{17,25},{25,17},{2,10},{10... | collective-permute-start | bytes 884744 | tf_op jit(solution)/shard_map/ppermute | solution.py:320
  130.0 2.0 %collective-permute-start.35 = (bf16[512,256]{1,0:T(8,128)(2,1)S(1)}, bf16[512,256]{1,0:T(8,128)(2,1)S(1)}, u32[]{:S(2)}, u32[]{:S(2)}) collective-permute-start(bf16[512,256]{1,0:T(8,128)(2,1)S(1)} %get-tuple-element.58.refs_2_), channel_id=1, source_target_pairs={{0,8},{8,0},{16,24},{24,16},{1,9},{9,1},{17,25},{25,17},{2,10},{10... | collective-permute-start | bytes 786440 | tf_op jit(solution)/shard_map/ppermute | solution.py:320
  130.6 1.8 %collective-permute-start.43 = (bf16[512,256]{1,0:T(8,128)(2,1)S(1)}, bf16[512,256]{1,0:T(8,128)(2,1)S(1)}, u32[]{:S(2)}, u32[]{:S(2)}) collective-permute-start(bf16[512,256]{1,0:T(8,128)(2,1)S(1)} %collective-permute-done.36.refs_4_), channel_id=1, source_target_pairs={{0,8},{8,0},{16,24},{24,16},{1,9},{9,1},{17,25},{25,17},{2,10},{10... | collective-permute-start | bytes 786440 | tf_op jit(solution)/shard_map/ppermute | solution.py:320

commit v3 on v2

--- a/solution.py
+++ b/solution.py
@@ -415,8 +415,7 @@
         )(bases, keep, col_map, *pieces)
 
     starts = jnp.arange(STEPS, dtype=jnp.int32) * PANEL
-    picked = select(starts[:1])
-    picked += select(jnp.concatenate([starts[1:], (panel * PANEL)[None].astype(jnp.int32)]))
+    picked = select(jnp.concatenate([starts, (panel * PANEL)[None].astype(jnp.int32)]))
 
     leaf_order = leaf ^ jnp.arange(leaf_count, dtype=jnp.int32)
     row_map = child_map.reshape(leaf_count, device_rows)[leaf_order].reshape(1, 2 * child_order)

time: 147 us -> 147 us (level)
    pallas_call x2 -> x1, Pallas kernels: 3.21 us -> 2.4 us  [select(): pl.pallas_call(select_kernel, in_specs=[SMEM_SPEC, SMEM_SPEC, VMEM_SPEC]...]
where the time goes in v3:
time: 147 us
  Pallas kernels  63.8 us (43%)
  starting transfers between devices  44.7 us (30%)
  waiting for transfers between devices  33.1 us (23%)
  local copies, waits for them, and re-layouts  2.35 us (2%)
  other arithmetic  2.35 us (2%)
    pallas_call x5, Pallas kernels, per_device(): pl.pallas_call(functools.partial(step_kernel, step, leaf_count, spots), i...  61.4 us
    ppermute x53, starting transfers between devices, flip(): return lax.ppermute(value, axis, [(i, i ^ bits) for i in range(count)])  44.7 us
    ppermute x53, waiting for transfers between devices, flip(): return lax.ppermute(value, axis, [(i, i ^ bits) for i in range(count)])  33.1 us
  transfers between devices with their start and end apart: 53, of which 17 were waited for; matrix products, arithmetic and copies ran while one was open for 3% of the time, Pallas kernels for 34%

profile of v3, /device:TPU:0, one launch (start us, length us, event | category | flops | bytes accessed | tf_op | source)
XLA Modules:
  0.0 146.7 jit_solution(1750993670775898334)
XLA Ops:
  0.0 4.1 %collective-permute-start.3 = (bf16[512,128]{1,0:T(8,128)(2,1)}, bf16[512,128]{1,0:T(8,128)(2,1)S(1)}, u32[]{:S(2)}, u32[]{:S(2)}) collective-permute-start(bf16[512,128]{1,0:T(8,128)(2,1)} %refs_0_.1), channel_id=1, source_target_pairs={{0,4},{1,5},{2,6},{3,7},{4,0},{5,1},{6,2},{7,3},{8,12},{9,13},{10,... | collective-permute-start | bytes 393224 | tf_op jit(solution)/shard_map/ppermute | solution.py:320
  4.1 1.5 %collective-permute-start = (bf16[512,128]{1,0:T(8,128)(2,1)}, bf16[512,128]{1,0:T(8,128)(2,1)S(1)}, u32[]{:S(2)}, u32[]{:S(2)}) collective-permute-start(bf16[512,128]{1,0:T(8,128)(2,1)} %refs_0_.1), channel_id=1, source_target_pairs={{0,1},{1,0},{2,3},{3,2},{4,5},{5,4},{6,7},{7,6},{8,9},{9,8},{10,11... | collective-permute-start | bytes 393224 | tf_op jit(solution)/shard_map/ppermute | solution.py:320
  5.6 1.1 reduce-precision_convert_fusion
  6.7 1.0 fusion
  7.7 0.5 collective-permute-start.10
  8.2 1.2 collective-permute-start.11
  9.4 0.3 collective-permute-start.12
  9.9 0.6 gather_fusion.1
  10.8 0.6 gather_fusion.2
  11.3 0.6 gather_fusion
  12.0 1.6 %collective-permute-start.1 = (bf16[512,128]{1,0:T(8,128)(2,1)S(1)}, bf16[512,128]{1,0:T(8,128)(2,1)S(1)}, u32[]{:S(2)}, u32[]{:S(2)}) collective-permute-start(bf16[512,128]{1,0:T(8,128)(2,1)S(1)} %copy-done.1), channel_id=1, source_target_pairs={{0,2},{1,3},{2,0},{3,1},{4,6},{5,7},{6,4},{7,5},{8,10},{9,11},{10,... | collective-permute-start | bytes 393224 | tf_op jit(solution)/shard_map/ppermute | solution.py:320
  13.6 0.4 collective-permute-start.2
  14.1 1.6 %collective-permute-start.4 = (bf16[512,128]{1,0:T(8,128)(2,1)S(1)}, bf16[512,128]{1,0:T(8,128)(2,1)S(1)}, u32[]{:S(2)}, u32[]{:S(2)}) collective-permute-start(bf16[512,128]{1,0:T(8,128)(2,1)S(1)} %collective-permute-done.3.refs_4_), channel_id=1, source_target_pairs={{0,1},{1,0},{2,3},{3,2},{4,5},{5,4},{6,7},{7,6},{8,9},{9,8},{10,11... | collective-permute-start | bytes 393224 | tf_op jit(solution)/shard_map/ppermute | solution.py:320
  15.6 1.6 %collective-permute-start.5 = (bf16[512,128]{1,0:T(8,128)(2,1)S(1)}, bf16[512,128]{1,0:T(8,128)(2,1)S(1)}, u32[]{:S(2)}, u32[]{:S(2)}) collective-permute-start(bf16[512,128]{1,0:T(8,128)(2,1)S(1)} %collective-permute-done.3.refs_4_), channel_id=1, source_target_pairs={{0,2},{1,3},{2,0},{3,1},{4,6},{5,7},{6,4},{7,5},{8,10},{9,11},{10,... | collective-permute-start | bytes 393224 | tf_op jit(solution)/shard_map/ppermute | solution.py:320
  17.2 0.4 collective-permute-start.6
  17.8 0.5 collective-permute-done.1.refs_2_
  18.4 0.3 collective-permute-start.13
  18.7 2.3 %collective-permute-done.2.refs_3_ = bf16[512,128]{1,0:T(8,128)(2,1)S(1)} collective-permute-done((bf16[512,128]{1,0:T(8,128)(2,1)S(1)}, bf16[512,128]{1,0:T(8,128)(2,1)S(1)}, u32[]{:S(2)}, u32[]{:S(2)}) %collective-permute-start.2) | collective-permute-done | bytes 131104 | tf_op jit(solution)/shard_map/ppermute | solution.py:320
  21.0 6.9 %collective-permute-start.14 = (bf16[576,256]{1,0:T(8,128)(2,1)S(1)}, bf16[576,256]{1,0:T(8,128)(2,1)S(1)}, u32[]{:S(2)}, u32[]{:S(2)}) collective-permute-start(bf16[576,256]{1,0:T(8,128)(2,1)S(1)} %pad_maximum_fusion), channel_id=1, source_target_pairs={{0,1},{1,0},{2,3},{3,2},{4,5},{5,4},{6,7},{7,6},{8,9},{9,8},{10,11... | collective-permute-start | bytes 884744 | tf_op jit(solution)/shard_map/ppermute | solution.py:320
  27.9 1.6 %collective-permute-done.5.refs_6_ = bf16[512,128]{1,0:T(8,128)(2,1)S(1)} collective-permute-done((bf16[512,128]{1,0:T(8,128)(2,1)S(1)}, bf16[512,128]{1,0:T(8,128)(2,1)S(1)}, u32[]{:S(2)}, u32[]{:S(2)}) %collective-permute-start.5) | collective-permute-done | bytes 131104 | tf_op jit(solution)/shard_map/ppermute | solution.py:320
  29.4 2.0 %collective-permute-done.6.refs_7_ = bf16[512,128]{1,0:T(8,128)(2,1)S(1)} collective-permute-done((bf16[512,128]{1,0:T(8,128)(2,1)S(1)}, bf16[512,128]{1,0:T(8,128)(2,1)S(1)}, u32[]{:S(2)}, u32[]{:S(2)}) %collective-permute-start.6) | collective-permute-done | bytes 131104 | tf_op jit(solution)/shard_map/ppermute | solution.py:320
  31.5 1.5 %collective-permute-start.22 = (bf16[512,256]{1,0:T(8,128)(2,1)S(1)}, bf16[512,256]{1,0:T(8,128)(2,1)S(1)}, u32[]{:S(2)}, u32[]{:S(2)}) collective-permute-start(bf16[512,256]{1,0:T(8,128)(2,1)S(1)} %get-tuple-element.51.refs_15_), channel_id=1, source_target_pairs={{0,16},{8,24},{16,0},{24,8},{1,17},{9,25},{17,1},{25,9},{2,18},{10... | collective-permute-start | bytes 786440 | tf_op jit(solution)/shard_map/ppermute | solution.py:320
  33.0 2.4 %shard_map.46 = (bf16[512,256]{1,0:T(8,128)(2,1)S(1)}, bf16[512,256]{1,0:T(8,128)(2,1)S(1)}, bf16[512,256]{1,0:T(8,128)(2,1)S(1)}, bf16[512,256]{1,0:T(8,128)(2,...) custom-call(s32[6]{0:T(128)S(1)} %pad_add_fusion.1.bases_ref, ...), custom_call_target="tpu_custom_call" | custom-call | flops 6000000000 | bytes 1048576 | tf_op jit(solution)/shard_map/pallas_call | solution.py:406
  35.4 0.6 collective-permute-start.20
  36.0 1.5 %collective-permute-start.8 = (bf16[512,256]{1,0:T(8,128)(2,1)S(1)}, bf16[512,256]{1,0:T(8,128)(2,1)S(1)}, u32[]{:S(2)}, u32[]{:S(2)}) collective-permute-start(bf16[512,256]{1,0:T(8,128)(2,1)S(1)} %get-tuple-element.48.refs_2_), channel_id=1, source_target_pairs={{0,16},{8,24},{16,0},{24,8},{1,17},{9,25},{17,1},{25,9},{2,18},{10... | collective-permute-start | bytes 786440 | tf_op jit(solution)/shard_map/ppermute | solution.py:320
  37.6 3.1 %collective-permute-done.22.refs_17_ = bf16[512,256]{1,0:T(8,128)(2,1)S(1)} collective-permute-done((bf16[512,256]{1,0:T(8,128)(2,1)S(1)}, bf16[512,256]{1,0:T(8,128)(2,1)S(1)}, u32[]{:S(2)}, u32[]{:S(2)}) %collective-permute-start.22) | collective-permute-done | bytes 262176 | tf_op jit(solution)/shard_map/ppermute | solution.py:320
  40.8 2.4 %collective-permute-start.17 = (bf16[576,256]{1,0:T(8,128)(2,1)S(1)}, bf16[576,256]{1,0:T(8,128)(2,1)S(1)}, u32[]{:S(2)}, u32[]{:S(2)}) collective-permute-start(bf16[576,256]{1,0:T(8,128)(2,1)S(1)} %collective-permute-done.13), channel_id=1, source_target_pairs={{0,1},{1,0},{2,3},{3,2},{4,5},{5,4},{6,7},{7,6},{8,9},{9,8},{10,11... | collective-permute-start | bytes 884744 | tf_op jit(solution)/shard_map/ppermute | solution.py:320
  43.2 1.9 %collective-permute-done.16 = bf16[576,256]{1,0:T(8,128)(2,1)S(1)} collective-permute-done((bf16[576,256]{1,0:T(8,128)(2,1)S(1)}, bf16[576,256]{1,0:T(8,128)(2,1)S(1)}, u32[]{:S(2)}, u32[]{:S(2)}) %collective-permute-start.16) | collective-permute-done | bytes 294944 | tf_op jit(solution)/shard_map/ppermute | solution.py:320
  45.1 1.2 collective-permute-start.24
  46.4 2.6 %collective-permute-start.19 = (bf16[576,256]{1,0:T(8,128)(2,1)S(1)}, bf16[576,256]{1,0:T(8,128)(2,1)S(1)}, u32[]{:S(2)}, u32[]{:S(2)}) collective-permute-start(bf16[576,256]{1,0:T(8,128)(2,1)S(1)} %collective-permute-done.13), channel_id=1, source_target_pairs={{0,3},{1,2},{2,1},{3,0},{4,7},{5,6},{6,5},{7,4},{8,11},{9,10},{10,... | collective-permute-start | bytes 884744 | tf_op jit(solution)/shard_map/ppermute | solution.py:320
  49.0 2.9 %collective-permute-done.8.refs_4_ = bf16[512,256]{1,0:T(8,128)(2,1)S(1)} collective-permute-done((bf16[512,256]{1,0:T(8,128)(2,1)S(1)}, bf16[512,256]{1,0:T(8,128)(2,1)S(1)}, u32[]{:S(2)}, u32[]{:S(2)}) %collective-permute-start.8) | collective-permute-done | bytes 262176 | tf_op jit(solution)/shard_map/ppermute | solution.py:320
  52.0 0.5 collective-permute-start.9
  52.5 3.1 %collective-permute-done.24.refs_4_ = bf16[512,256]{1,0:T(8,128)(2,1)S(1)} collective-permute-done((bf16[512,256]{1,0:T(8,128)(2,1)S(1)}, bf16[512,256]{1,0:T(8,128)(2,1)S(1)}, u32[]{:S(2)}, u32[]{:S(2)}) %collective-permute-start.24) | collective-permute-done | bytes 262176 | tf_op jit(solution)/shard_map/ppermute | solution.py:320
  55.7 3.7 %collective-permute-done.19 = bf16[576,256]{1,0:T(8,128)(2,1)S(1)} collective-permute-done((bf16[576,256]{1,0:T(8,128)(2,1)S(1)}, bf16[576,256]{1,0:T(8,128)(2,1)S(1)}, u32[]{:S(2)}, u32[]{:S(2)}) %collective-permute-start.19) | collective-permute-done | bytes 294944 | tf_op jit(solution)/shard_map/ppermute | solution.py:320
  59.5 2.3 %collective-permute-start.26 = (bf16[576,256]{1,0:T(8,128)(2,1)S(1)}, bf16[576,256]{1,0:T(8,128)(2,1)S(1)}, u32[]{:S(2)}, u32[]{:S(2)}) collective-permute-start(bf16[576,256]{1,0:T(8,128)(2,1)S(1)} %get-tuple-element.92.refs_6_.refs_10_), channel_id=1, source_target_pairs={{0,16},{8,24},{16,0},{24,8},{1,17},{9,25},{17,1},{25,9},{2,18},{10... | collective-permute-start | bytes 884744 | tf_op jit(solution)/shard_map/ppermute | solution.py:320
  61.8 6.5 %collective-permute-done.26.refs_8_ = bf16[576,256]{1,0:T(8,128)(2,1)S(1)} collective-permute-done((bf16[576,256]{1,0:T(8,128)(2,1)S(1)}, bf16[576,256]{1,0:T(8,128)(2,1)S(1)}, u32[]{:S(2)}, u32[]{:S(2)}) %collective-permute-start.26) | collective-permute-done | bytes 294944 | tf_op jit(solution)/shard_map/ppermute | solution.py:320
  68.3 0.5 collective-permute-start.31
  68.8 1.1 collective-permute-done.27.refs_9_
  69.8 1.7 %collective-permute-start.29 = (bf16[576,256]{1,0:T(8,128)(2,1)S(1)}, bf16[576,256]{1,0:T(8,128)(2,1)S(1)}, u32[]{:S(2)}, u32[]{:S(2)}) collective-permute-start(bf16[576,256]{1,0:T(8,128)(2,1)S(1)} %get-tuple-element.54.refs_6_.refs_10_), channel_id=1, source_target_pairs={{0,16},{8,24},{16,0},{24,8},{1,17},{9,25},{17,1},{25,9},{2,18},{10... | collective-permute-start | bytes 884744 | tf_op jit(solution)/shard_map/ppermute | solution.py:320
  71.6 10.2 %shard_map.47 = (bf16[1024,256]{1,0:T(8,128)(2,1)S(1)}, f32[512,256]{1,0:T(8,128)S(1)}, f32[5,128,128]{2,1,0:T(8,128)S(1)}) custom-call(s32[6]{0:T(128)S(1)} %pad_add_fusion.refs_0_, s32[1,2048]{1,0:T(1,128)S(1)} %bitcast.45, bf16[512,256]{1,0:T(8,128)(2,1)S(1)} %get-tuple-element.52.refs_2_, bf16[512,256]{1,0:T(8,128)(2,1)S(1)} %collective-permute-done.30.refs_3_, ...), custom_call_target="tpu_custom_call" | custom-call | flops 15000000512 | bytes 4194304 | tf_op jit(solution)/shard_map/pallas_call | solution.py:491
  81.8 0.6 collective-permute-start.32
  82.5 0.4 collective-permute-start.33
  83.0 1.0 collective-permute-done.34.refs_16_
  84.0 0.7 collective-permute-start.38
  84.7 1.4 collective-permute-start.41
  86.1 12.9 %shard_map.48 = (bf16[768,256]{1,0:T(8,128)(2,1)S(1)}, f32[512,256]{1,0:T(8,128)S(1)}, f32[5,128,128]{2,1,0:T(8,128)S(1)}, bf16[512,256]{1,0:T(8,128)(2,1)S(1)},...) custom-call(s32[6]{0:T(128)S(1)} %pad_add_fusion.refs_0_, s32[1,2048]{1,0:T(1,128)S(1)} %bitcast.46, ...), custom_call_target="tpu_custom_call" | custom-call | flops 15000000512 | bytes 4194304 | tf_op jit(solution)/shard_map/pallas_call | solution.py:491
  99.0 0.6 collective-permute-start.42
  99.6 0.4 collective-permute-start.39
  100.1 0.6 collective-permute-start.47
  100.7 0.4 collective-permute-done.37.refs_3_
  101.1 1.0 collective-permute-start.50
  102.1 12.3 %shard_map.49 = (bf16[512,256]{1,0:T(8,128)(2,1)S(1)}, f32[512,256]{1,0:T(8,128)S(1)}, f32[5,128,128]{2,1,0:T(8,128)S(1)}, bf16[512,256]{1,0:T(8,128)(2,1)S(1)},...) custom-call(s32[6]{0:T(128)S(1)} %pad_add_fusion.refs_0_, s32[1,2048]{1,0:T(1,128)S(1)} %bitcast.47, ...), custom_call_target="tpu_custom_call" | custom-call | flops 15000000512 | bytes 4194304 | tf_op jit(solution)/shard_map/pallas_call | solution.py:491
  114.5 0.2 collective-permute-done.50.refs_8_
  114.7 0.3 collective-permute-start.51
  115.0 0.2 collective-permute-start.46
  115.2 0.3 collective-permute-start.48
  115.5 1.1 collective-permute-start.36
  116.6 1.0 collective-permute-start.45
  117.8 11.7 %shard_map.50 = (bf16[256,256]{1,0:T(8,128)(2,1)S(1)}, f32[512,256]{1,0:T(8,128)S(1)}, f32[5,128,128]{2,1,0:T(8,128)S(1)}, bf16[512,256]{1,0:T(8,128)(2,1)S(1)},...) custom-call(s32[6]{0:T(128)S(1)} %pad_add_fusion.refs_0_, s32[1,2048]{1,0:T(1,128)S(1)} %bitcast.48, ...), custom_call_target="tpu_custom_call" | custom-call | flops 15000000512 | bytes 4194304 | tf_op jit(solution)/shard_map/pallas_call | solution.py:491
  129.5 0.7 collective-permute-done.45.refs_8_
  130.2 0.5 collective-permute-start.35
  130.8 1.4 collective-permute-done.35.refs_3_
  132.2 0.4 collective-permute-done.43.refs_5_
  132.6 14.2 %shard_map.51 = f32[512,256]{1,0:T(8,128)} custom-call(s32[6]{0:T(128)S(1)} %pad_add_fusion.refs_0_, s32[1,2048]{1,0:T(1,128)S(1)} %bitcast.49, bf16[512,256]{1,0:T(8,128)(2,1)S(1)} %get-tuple-element.60.refs_2_, bf16[512,256]{1,0:T(8,128)(2,1)S(1)} %collective-permute-done.35.refs_3_, bf16[512,256]{1,0:T(8,128)(2,1)S(1)} %collective-permute-done.36.refs_4_, ...), custom_call_target="tpu_custom_call" | custom-call | flops 15000000512 | bytes 4194304 | tf_op jit(solution)/shard_map/pallas_call | solution.py:491
  (91 shorter events, 1.5 us)
Async XLA Ops:
  0.0 11.9 %copy-start.1 = (bf16[512,128]{1,0:T(8,128)(2,1)S(1)}, bf16[512,128]{1,0:T(8,128)(2,1)}, u32[]{:S(2)}) copy-start(bf16[512,128]{1,0:T(8,128)(2,1)} %refs_0_.1) | copy-start | bytes 393220
  0.0 9.7 %copy-start.3 = (s32[2,8,8]{2,1,0:T(8,128)S(1)}, s32[2,8,8]{2,1,0:T(8,128)}, u32[]{:S(2)}) copy-start(s32[2,8,8]{2,1,0:T(8,128)} %param.7) | copy-start | bytes 1540
  0.0 10.5 %copy-start.2 = (s32[2,1024]{1,0:T(2,128)S(1)}, s32[2,1024]{1,0:T(2,128)}, u32[]{:S(2)}) copy-start(s32[2,1024]{1,0:T(2,128)} %param.6) | copy-start | bytes 24580
  0.0 14.0 %collective-permute-start.3 = (bf16[512,128]{1,0:T(8,128)(2,1)}, bf16[512,128]{1,0:T(8,128)(2,1)S(1)}, u32[]{:S(2)}, u32[]{:S(2)}) collective-permute-start(bf16[512,128]{1,0:T(8,128)(2,1)} %refs_0_.1), channel_id=1, source_target_pairs={{0,4},{1,5},{2,6},{3,7},{4,0},{5,1},{6,2},{7,3},{8,12},{9,13},{10,... | collective-permute-start | bytes 393224 | tf_op jit(solution)/shard_map/ppermute | solution.py:320
  4.1 13.1 %collective-permute-start = (bf16[512,128]{1,0:T(8,128)(2,1)}, bf16[512,128]{1,0:T(8,128)(2,1)S(1)}, u32[]{:S(2)}, u32[]{:S(2)}) collective-permute-start(bf16[512,128]{1,0:T(8,128)(2,1)} %refs_0_.1), channel_id=1, source_target_pairs={{0,1},{1,0},{2,3},{3,2},{4,5},{5,4},{6,7},{7,6},{8,9},{9,8},{10,11... | collective-permute-start | bytes 393224 | tf_op jit(solution)/shard_map/ppermute | solution.py:320
  7.7 4.2 %collective-permute-start.10 = (bf16[64,256]{1,0:T(8,128)(2,1)S(1)}, bf16[64,256]{1,0:T(8,128)(2,1)S(1)}, u32[]{:S(2)}, u32[]{:S(2)}) collective-permute-start(bf16[64,256]{1,0:T(8,128)(2,1)S(1)} %get-tuple-element.98), channel_id=1, source_target_pairs={{0,24},{8,16},{16,8},{24,0},{1,25},{9,17},{17,9},{25,1},{2,26},{10... | collective-permute-start | bytes 98312 | tf_op jit(solution)/shard_map/ppermute | solution.py:320
  8.2 5.4 %collective-permute-start.11 = (bf16[64,256]{1,0:T(8,128)(2,1)S(1)}, bf16[64,256]{1,0:T(8,128)(2,1)S(1)}, u32[]{:S(2)}, u32[]{:S(2)}) collective-permute-start(bf16[64,256]{1,0:T(8,128)(2,1)S(1)} %get-tuple-element.97), channel_id=1, source_target_pairs={{0,16},{8,24},{16,0},{24,8},{1,17},{9,25},{17,1},{25,9},{2,18},{10... | collective-permute-start | bytes 98312 | tf_op jit(solution)/shard_map/ppermute | solution.py:320
  9.4 4.6 %collective-permute-start.12 = (bf16[64,256]{1,0:T(8,128)(2,1)S(1)}, bf16[64,256]{1,0:T(8,128)(2,1)S(1)}, u32[]{:S(2)}, u32[]{:S(2)}) collective-permute-start(bf16[64,256]{1,0:T(8,128)(2,1)S(1)} %get-tuple-element.96), channel_id=1, source_target_pairs={{0,8},{8,0},{16,24},{24,16},{1,9},{9,1},{17,25},{25,17},{2,10},{10... | collective-permute-start | bytes 98312 | tf_op jit(solution)/shard_map/ppermute | solution.py:320
  12.0 6.4 %collective-permute-start.1 = (bf16[512,128]{1,0:T(8,128)(2,1)S(1)}, bf16[512,128]{1,0:T(8,128)(2,1)S(1)}, u32[]{:S(2)}, u32[]{:S(2)}) collective-permute-start(bf16[512,128]{1,0:T(8,128)(2,1)S(1)} %copy-done.1), channel_id=1, source_target_pairs={{0,2},{1,3},{2,0},{3,1},{4,6},{5,7},{6,4},{7,5},{8,10},{9,11},{10,... | collective-permute-start | bytes 393224 | tf_op jit(solution)/shard_map/ppermute | solution.py:320
  13.6 7.4 %collective-permute-start.2 = (bf16[512,128]{1,0:T(8,128)(2,1)S(1)}, bf16[512,128]{1,0:T(8,128)(2,1)S(1)}, u32[]{:S(2)}, u32[]{:S(2)}) collective-permute-start(bf16[512,128]{1,0:T(8,128)(2,1)S(1)} %copy-done.1), channel_id=1, source_target_pairs={{0,3},{1,2},{2,1},{3,0},{4,7},{5,6},{6,5},{7,4},{8,11},{9,10},{10,... | collective-permute-start | bytes 393224 | tf_op jit(solution)/shard_map/ppermute | solution.py:320
  14.1 13.8 %collective-permute-start.4 = (bf16[512,128]{1,0:T(8,128)(2,1)S(1)}, bf16[512,128]{1,0:T(8,128)(2,1)S(1)}, u32[]{:S(2)}, u32[]{:S(2)}) collective-permute-start(bf16[512,128]{1,0:T(8,128)(2,1)S(1)} %collective-permute-done.3.refs_4_), channel_id=1, source_target_pairs={{0,1},{1,0},{2,3},{3,2},{4,5},{5,4},{6,7},{7,6},{8,9},{9,8},{10,11... | collective-permute-start | bytes 393224 | tf_op jit(solution)/shard_map/ppermute | solution.py:320
  15.6 13.8 %collective-permute-start.5 = (bf16[512,128]{1,0:T(8,128)(2,1)S(1)}, bf16[512,128]{1,0:T(8,128)(2,1)S(1)}, u32[]{:S(2)}, u32[]{:S(2)}) collective-permute-start(bf16[512,128]{1,0:T(8,128)(2,1)S(1)} %collective-permute-done.3.refs_4_), channel_id=1, source_target_pairs={{0,2},{1,3},{2,0},{3,1},{4,6},{5,7},{6,4},{7,5},{8,10},{9,11},{10,... | collective-permute-start | bytes 393224 | tf_op jit(solution)/shard_map/ppermute | solution.py:320
  17.2 14.3 %collective-permute-start.6 = (bf16[512,128]{1,0:T(8,128)(2,1)S(1)}, bf16[512,128]{1,0:T(8,128)(2,1)S(1)}, u32[]{:S(2)}, u32[]{:S(2)}) collective-permute-start(bf16[512,128]{1,0:T(8,128)(2,1)S(1)} %collective-permute-done.3.refs_4_), channel_id=1, source_target_pairs={{0,3},{1,2},{2,1},{3,0},{4,7},{5,6},{6,5},{7,4},{8,11},{9,10},{10,... | collective-permute-start | bytes 393224 | tf_op jit(solution)/shard_map/ppermute | solution.py:320
  18.4 17.0 %collective-permute-start.13 = (bf16[576,256]{1,0:T(8,128)(2,1)S(1)}, bf16[576,256]{1,0:T(8,128)(2,1)S(1)}, u32[]{:S(2)}, u32[]{:S(2)}) collective-permute-start(bf16[576,256]{1,0:T(8,128)(2,1)S(1)} %pad_maximum_fusion), channel_id=1, source_target_pairs={{0,4},{1,5},{2,6},{3,7},{4,0},{5,1},{6,2},{7,3},{8,12},{9,13},{10,... | collective-permute-start | bytes 884744 | tf_op jit(solution)/shard_map/ppermute | solution.py:320
  21.0 15.0 %collective-permute-start.14 = (bf16[576,256]{1,0:T(8,128)(2,1)S(1)}, bf16[576,256]{1,0:T(8,128)(2,1)S(1)}, u32[]{:S(2)}, u32[]{:S(2)}) collective-permute-start(bf16[576,256]{1,0:T(8,128)(2,1)S(1)} %pad_maximum_fusion), channel_id=1, source_target_pairs={{0,1},{1,0},{2,3},{3,2},{4,5},{5,4},{6,7},{7,6},{8,9},{9,8},{10,11... | collective-permute-start | bytes 884744 | tf_op jit(solution)/shard_map/ppermute | solution.py:320
  27.9 12.9 %collective-permute-start.15 = (bf16[576,256]{1,0:T(8,128)(2,1)S(1)}, bf16[576,256]{1,0:T(8,128)(2,1)S(1)}, u32[]{:S(2)}, u32[]{:S(2)}) collective-permute-start(bf16[576,256]{1,0:T(8,128)(2,1)S(1)} %pad_maximum_fusion), channel_id=1, source_target_pairs={{0,2},{1,3},{2,0},{3,1},{4,6},{5,7},{6,4},{7,5},{8,10},{9,11},{10,... | collective-permute-start | bytes 884744 | tf_op jit(solution)/shard_map/ppermute | solution.py:320
  29.4 15.7 %collective-permute-start.16 = (bf16[576,256]{1,0:T(8,128)(2,1)S(1)}, bf16[576,256]{1,0:T(8,128)(2,1)S(1)}, u32[]{:S(2)}, u32[]{:S(2)}) collective-permute-start(bf16[576,256]{1,0:T(8,128)(2,1)S(1)} %pad_maximum_fusion), channel_id=1, source_target_pairs={{0,3},{1,2},{2,1},{3,0},{4,7},{5,6},{6,5},{7,4},{8,11},{9,10},{10,... | collective-permute-start | bytes 884744 | tf_op jit(solution)/shard_map/ppermute | solution.py:320
  31.5 9.2 %collective-permute-start.22 = (bf16[512,256]{1,0:T(8,128)(2,1)S(1)}, bf16[512,256]{1,0:T(8,128)(2,1)S(1)}, u32[]{:S(2)}, u32[]{:S(2)}) collective-permute-start(bf16[512,256]{1,0:T(8,128)(2,1)S(1)} %get-tuple-element.51.refs_15_), channel_id=1, source_target_pairs={{0,16},{8,24},{16,0},{24,8},{1,17},{9,25},{17,1},{25,9},{2,18},{10... | collective-permute-start | bytes 786440 | tf_op jit(solution)/shard_map/ppermute | solution.py:320
  35.4 11.0 %collective-permute-start.20 = (bf16[512,256]{1,0:T(8,128)(2,1)S(1)}, bf16[512,256]{1,0:T(8,128)(2,1)S(1)}, u32[]{:S(2)}, u32[]{:S(2)}) collective-permute-start(bf16[512,256]{1,0:T(8,128)(2,1)S(1)} %get-tuple-element.49.refs_11_), channel_id=1, source_target_pairs={{0,16},{8,24},{16,0},{24,8},{1,17},{9,25},{17,1},{25,9},{2,18},{10... | collective-permute-start | bytes 786440 | tf_op jit(solution)/shard_map/ppermute | solution.py:320
  36.0 15.9 %collective-permute-start.8 = (bf16[512,256]{1,0:T(8,128)(2,1)S(1)}, bf16[512,256]{1,0:T(8,128)(2,1)S(1)}, u32[]{:S(2)}, u32[]{:S(2)}) collective-permute-start(bf16[512,256]{1,0:T(8,128)(2,1)S(1)} %get-tuple-element.48.refs_2_), channel_id=1, source_target_pairs={{0,16},{8,24},{16,0},{24,8},{1,17},{9,25},{17,1},{25,9},{2,18},{10... | collective-permute-start | bytes 786440 | tf_op jit(solution)/shard_map/ppermute | solution.py:320
  40.7 2.4 %collective-permute-start.23 = (bf16[512,256]{1,0:T(8,128)(2,1)S(1)}, bf16[512,256]{1,0:T(8,128)(2,1)S(1)}, u32[]{:S(2)}, u32[]{:S(2)}) collective-permute-start(bf16[512,256]{1,0:T(8,128)(2,1)S(1)} %collective-permute-done.22.refs_17_), channel_id=1, source_target_pairs={{0,8},{8,0},{16,24},{24,16},{1,9},{9,1},{17,25},{25,17},{2,10},{10... | collective-permute-start | bytes 786440 | tf_op jit(solution)/shard_map/ppermute | solution.py:320
  40.8 11.2 %collective-permute-start.17 = (bf16[576,256]{1,0:T(8,128)(2,1)S(1)}, bf16[576,256]{1,0:T(8,128)(2,1)S(1)}, u32[]{:S(2)}, u32[]{:S(2)}) collective-permute-start(bf16[576,256]{1,0:T(8,128)(2,1)S(1)} %collective-permute-done.13), channel_id=1, source_target_pairs={{0,1},{1,0},{2,3},{3,2},{4,5},{5,4},{6,7},{7,6},{8,9},{9,8},{10,11... | collective-permute-start | bytes 884744 | tf_op jit(solution)/shard_map/ppermute | solution.py:320
  43.1 12.5 %collective-permute-start.18 = (bf16[576,256]{1,0:T(8,128)(2,1)S(1)}, bf16[576,256]{1,0:T(8,128)(2,1)S(1)}, u32[]{:S(2)}, u32[]{:S(2)}) collective-permute-start(bf16[576,256]{1,0:T(8,128)(2,1)S(1)} %collective-permute-done.13), channel_id=1, source_target_pairs={{0,2},{1,3},{2,0},{3,1},{4,6},{5,7},{6,4},{7,5},{8,10},{9,11},{10,... | collective-permute-start | bytes 884744 | tf_op jit(solution)/shard_map/ppermute | solution.py:320
  45.1 10.5 %collective-permute-start.24 = (bf16[512,256]{1,0:T(8,128)(2,1)S(1)}, bf16[512,256]{1,0:T(8,128)(2,1)S(1)}, u32[]{:S(2)}, u32[]{:S(2)}) collective-permute-start(bf16[512,256]{1,0:T(8,128)(2,1)S(1)} %get-tuple-element.52.refs_2_), channel_id=1, source_target_pairs={{0,16},{8,24},{16,0},{24,8},{1,17},{9,25},{17,1},{25,9},{2,18},{10... | collective-permute-start | bytes 786440 | tf_op jit(solution)/shard_map/ppermute | solution.py:320
  46.4 13.0 %collective-permute-start.19 = (bf16[576,256]{1,0:T(8,128)(2,1)S(1)}, bf16[576,256]{1,0:T(8,128)(2,1)S(1)}, u32[]{:S(2)}, u32[]{:S(2)}) collective-permute-start(bf16[576,256]{1,0:T(8,128)(2,1)S(1)} %collective-permute-done.13), channel_id=1, source_target_pairs={{0,3},{1,2},{2,1},{3,0},{4,7},{5,6},{6,5},{7,4},{8,11},{9,10},{10,... | collective-permute-start | bytes 884744 | tf_op jit(solution)/shard_map/ppermute | solution.py:320
  51.9 7.4 %collective-permute-start.21 = (bf16[512,256]{1,0:T(8,128)(2,1)S(1)}, bf16[512,256]{1,0:T(8,128)(2,1)S(1)}, u32[]{:S(2)}, u32[]{:S(2)}) collective-permute-start(bf16[512,256]{1,0:T(8,128)(2,1)S(1)} %collective-permute-done.20.refs_13_), channel_id=1, source_target_pairs={{0,8},{8,0},{16,24},{24,16},{1,9},{9,1},{17,25},{25,17},{2,10},{10... | collective-permute-start | bytes 786440 | tf_op jit(solution)/shard_map/ppermute | solution.py:320
  52.0 7.4 %collective-permute-start.9 = (bf16[512,256]{1,0:T(8,128)(2,1)S(1)}, bf16[512,256]{1,0:T(8,128)(2,1)S(1)}, u32[]{:S(2)}, u32[]{:S(2)}) collective-permute-start(bf16[512,256]{1,0:T(8,128)(2,1)S(1)} %collective-permute-done.8.refs_4_), channel_id=1, source_target_pairs={{0,8},{8,0},{16,24},{24,16},{1,9},{9,1},{17,25},{25,17},{2,10},{10... | collective-permute-start | bytes 786440 | tf_op jit(solution)/shard_map/ppermute | solution.py:320
  55.6 3.8 %collective-permute-start.25 = (bf16[512,256]{1,0:T(8,128)(2,1)S(1)}, bf16[512,256]{1,0:T(8,128)(2,1)S(1)}, u32[]{:S(2)}, u32[]{:S(2)}) collective-permute-start(bf16[512,256]{1,0:T(8,128)(2,1)S(1)} %collective-permute-done.24.refs_4_), channel_id=1, source_target_pairs={{0,8},{8,0},{16,24},{24,16},{1,9},{9,1},{17,25},{25,17},{2,10},{10... | collective-permute-start | bytes 786440 | tf_op jit(solution)/shard_map/ppermute | solution.py:320
  59.5 8.7 %collective-permute-start.26 = (bf16[576,256]{1,0:T(8,128)(2,1)S(1)}, bf16[576,256]{1,0:T(8,128)(2,1)S(1)}, u32[]{:S(2)}, u32[]{:S(2)}) collective-permute-start(bf16[576,256]{1,0:T(8,128)(2,1)S(1)} %get-tuple-element.92.refs_6_.refs_10_), channel_id=1, source_target_pairs={{0,16},{8,24},{16,0},{24,8},{1,17},{9,25},{17,1},{25,9},{2,18},{10... | collective-permute-start | bytes 884744 | tf_op jit(solution)/shard_map/ppermute | solution.py:320
  68.3 1.6 %collective-permute-start.27 = (bf16[576,256]{1,0:T(8,128)(2,1)S(1)}, bf16[576,256]{1,0:T(8,128)(2,1)S(1)}, u32[]{:S(2)}, u32[]{:S(2)}) collective-permute-start(bf16[576,256]{1,0:T(8,128)(2,1)S(1)} %collective-permute-done.26.refs_8_), channel_id=1, source_target_pairs={{0,8},{8,0},{16,24},{24,16},{1,9},{9,1},{17,25},{25,17},{2,10},{10... | collective-permute-start | bytes 884744 | tf_op jit(solution)/shard_map/ppermute | solution.py:320
  68.3 3.3 %collective-permute-start.31 = (bf16[576,256]{1,0:T(8,128)(2,1)S(1)}, bf16[576,256]{1,0:T(8,128)(2,1)S(1)}, u32[]{:S(2)}, u32[]{:S(2)}) collective-permute-start(bf16[576,256]{1,0:T(8,128)(2,1)S(1)} %get-tuple-element.92.refs_6_.refs_10_), channel_id=1, source_target_pairs={{0,8},{8,0},{16,24},{24,16},{1,9},{9,1},{17,25},{25,17},{2,10},{10... | collective-permute-start | bytes 884744 | tf_op jit(solution)/shard_map/ppermute | solution.py:320
  68.8 2.8 %collective-permute-start.30 = (bf16[512,256]{1,0:T(8,128)(2,1)S(1)}, bf16[512,256]{1,0:T(8,128)(2,1)S(1)}, u32[]{:S(2)}, u32[]{:S(2)}) collective-permute-start(bf16[512,256]{1,0:T(8,128)(2,1)S(1)} %get-tuple-element.52.refs_2_), channel_id=1, source_target_pairs={{0,8},{8,0},{16,24},{24,16},{1,9},{9,1},{17,25},{25,17},{2,10},{10... | collective-permute-start | bytes 786440 | tf_op jit(solution)/shard_map/ppermute | solution.py:320
  69.8 16.2 %copy-start = (f32[512,256]{1,0:T(8,128)S(1)}, f32[512,256]{1,0:T(8,128)}, u32[]{:S(2)}) copy-start(f32[512,256]{1,0:T(8,128)} %refs_21_.1) | copy-start | bytes 1572868
  69.8 12.0 %collective-permute-start.29 = (bf16[576,256]{1,0:T(8,128)(2,1)S(1)}, bf16[576,256]{1,0:T(8,128)(2,1)S(1)}, u32[]{:S(2)}, u32[]{:S(2)}) collective-permute-start(bf16[576,256]{1,0:T(8,128)(2,1)S(1)} %get-tuple-element.54.refs_6_.refs_10_), channel_id=1, source_target_pairs={{0,16},{8,24},{16,0},{24,8},{1,17},{9,25},{17,1},{25,9},{2,18},{10... | collective-permute-start | bytes 884744 | tf_op jit(solution)/shard_map/ppermute | solution.py:320
  71.6 14.5 %collective-permute-start.28 = (bf16[576,256]{1,0:T(8,128)(2,1)S(1)}, bf16[576,256]{1,0:T(8,128)(2,1)S(1)}, u32[]{:S(2)}, u32[]{:S(2)}) collective-permute-start(bf16[576,256]{1,0:T(8,128)(2,1)S(1)} %get-tuple-element.54.refs_6_.refs_10_), channel_id=1, source_target_pairs={{0,8},{8,0},{16,24},{24,16},{1,9},{9,1},{17,25},{25,17},{2,10},{10... | collective-permute-start | bytes 884744 | tf_op jit(solution)/shard_map/ppermute | solution.py:320
  81.8 4.2 %collective-permute-start.32 = (bf16[576,256]{1,0:T(8,128)(2,1)S(1)}, bf16[576,256]{1,0:T(8,128)(2,1)S(1)}, u32[]{:S(2)}, u32[]{:S(2)}) collective-permute-start(bf16[576,256]{1,0:T(8,128)(2,1)S(1)} %collective-permute-done.29.refs_8_), channel_id=1, source_target_pairs={{0,8},{8,0},{16,24},{24,16},{1,9},{9,1},{17,25},{25,17},{2,10},{10... | collective-permute-start | bytes 884744 | tf_op jit(solution)/shard_map/ppermute | solution.py:320
  82.4 1.6 %collective-permute-start.34 = (bf16[512,256]{1,0:T(8,128)(2,1)S(1)}, bf16[512,256]{1,0:T(8,128)(2,1)S(1)}, u32[]{:S(2)}, u32[]{:S(2)}) collective-permute-start(bf16[512,256]{1,0:T(8,128)(2,1)S(1)} %get-tuple-element.51.refs_15_), channel_id=1, source_target_pairs={{0,8},{8,0},{16,24},{24,16},{1,9},{9,1},{17,25},{25,17},{2,10},{10... | collective-permute-start | bytes 786440 | tf_op jit(solution)/shard_map/ppermute | solution.py:320
  82.5 2.2 %collective-permute-start.33 = (bf16[512,256]{1,0:T(8,128)(2,1)S(1)}, bf16[512,256]{1,0:T(8,128)(2,1)S(1)}, u32[]{:S(2)}, u32[]{:S(2)}) collective-permute-start(bf16[512,256]{1,0:T(8,128)(2,1)S(1)} %get-tuple-element.49.refs_11_), channel_id=1, source_target_pairs={{0,8},{8,0},{16,24},{24,16},{1,9},{9,1},{17,25},{25,17},{2,10},{10... | collective-permute-start | bytes 786440 | tf_op jit(solution)/shard_map/ppermute | solution.py:320
  82.9 3.1 %collective-permute-start.7 = (bf16[512,256]{1,0:T(8,128)(2,1)S(1)}, bf16[512,256]{1,0:T(8,128)(2,1)S(1)}, u32[]{:S(2)}, u32[]{:S(2)}) collective-permute-start(bf16[512,256]{1,0:T(8,128)(2,1)S(1)} %get-tuple-element.48.refs_2_), channel_id=1, source_target_pairs={{0,8},{8,0},{16,24},{24,16},{1,9},{9,1},{17,25},{25,17},{2,10},{10... | collective-permute-start | bytes 786440 | tf_op jit(solution)/shard_map/ppermute | solution.py:320
  84.0 15.6 %collective-permute-start.38 = (bf16[512,256]{1,0:T(8,128)(2,1)S(1)}, bf16[512,256]{1,0:T(8,128)(2,1)S(1)}, u32[]{:S(2)}, u32[]{:S(2)}) collective-permute-start(bf16[512,256]{1,0:T(8,128)(2,1)S(1)} %get-tuple-element.61.refs_2_), channel_id=1, source_target_pairs={{0,16},{8,24},{16,0},{24,8},{1,17},{9,25},{17,1},{25,9},{2,18},{10... | collective-permute-start | bytes 786440 | tf_op jit(solution)/shard_map/ppermute | solution.py:320
  84.7 14.3 %collective-permute-start.41 = (bf16[576,256]{1,0:T(8,128)(2,1)S(1)}, bf16[576,256]{1,0:T(8,128)(2,1)S(1)}, u32[]{:S(2)}, u32[]{:S(2)}) collective-permute-start(bf16[576,256]{1,0:T(8,128)(2,1)S(1)} %get-tuple-element.62.refs_6_.refs_10_), channel_id=1, source_target_pairs={{0,16},{8,24},{16,0},{24,8},{1,17},{9,25},{17,1},{25,9},{2,18},{10... | collective-permute-start | bytes 884744 | tf_op jit(solution)/shard_map/ppermute | solution.py:320
  86.0 16.1 %collective-permute-start.40 = (bf16[576,256]{1,0:T(8,128)(2,1)S(1)}, bf16[576,256]{1,0:T(8,128)(2,1)S(1)}, u32[]{:S(2)}, u32[]{:S(2)}) collective-permute-start(bf16[576,256]{1,0:T(8,128)(2,1)S(1)} %get-tuple-element.62.refs_6_.refs_10_), channel_id=1, source_target_pairs={{0,8},{8,0},{16,24},{24,16},{1,9},{9,1},{17,25},{25,17},{2,10},{10... | collective-permute-start | bytes 884744 | tf_op jit(solution)/shard_map/ppermute | solution.py:320
  99.0 3.1 %collective-permute-start.42 = (bf16[576,256]{1,0:T(8,128)(2,1)S(1)}, bf16[576,256]{1,0:T(8,128)(2,1)S(1)}, u32[]{:S(2)}, u32[]{:S(2)}) collective-permute-start(bf16[576,256]{1,0:T(8,128)(2,1)S(1)} %collective-permute-done.41.refs_8_), channel_id=1, source_target_pairs={{0,8},{8,0},{16,24},{24,16},{1,9},{9,1},{17,25},{25,17},{2,10},{10... | collective-permute-start | bytes 884744 | tf_op jit(solution)/shard_map/ppermute | solution.py:320
  99.6 1.6 %collective-permute-start.37 = (bf16[512,256]{1,0:T(8,128)(2,1)S(1)}, bf16[512,256]{1,0:T(8,128)(2,1)S(1)}, u32[]{:S(2)}, u32[]{:S(2)}) collective-permute-start(bf16[512,256]{1,0:T(8,128)(2,1)S(1)} %get-tuple-element.61.refs_2_), channel_id=1, source_target_pairs={{0,8},{8,0},{16,24},{24,16},{1,9},{9,1},{17,25},{25,17},{2,10},{10... | collective-permute-start | bytes 786440 | tf_op jit(solution)/shard_map/ppermute | solution.py:320
  99.6 2.5 %collective-permute-start.39 = (bf16[512,256]{1,0:T(8,128)(2,1)S(1)}, bf16[512,256]{1,0:T(8,128)(2,1)S(1)}, u32[]{:S(2)}, u32[]{:S(2)}) collective-permute-start(bf16[512,256]{1,0:T(8,128)(2,1)S(1)} %collective-permute-done.38.refs_4_), channel_id=1, source_target_pairs={{0,8},{8,0},{16,24},{24,16},{1,9},{9,1},{17,25},{25,17},{2,10},{10... | collective-permute-start | bytes 786440 | tf_op jit(solution)/shard_map/ppermute | solution.py:320
  100.1 15.1 %collective-permute-start.47 = (bf16[512,256]{1,0:T(8,128)(2,1)S(1)}, bf16[512,256]{1,0:T(8,128)(2,1)S(1)}, u32[]{:S(2)}, u32[]{:S(2)}) collective-permute-start(bf16[512,256]{1,0:T(8,128)(2,1)S(1)} %get-tuple-element.73.refs_2_), channel_id=1, source_target_pairs={{0,16},{8,24},{16,0},{24,8},{1,17},{9,25},{17,1},{25,9},{2,18},{10... | collective-permute-start | bytes 786440 | tf_op jit(solution)/shard_map/ppermute | solution.py:320
  101.1 13.5 %collective-permute-start.50 = (bf16[576,256]{1,0:T(8,128)(2,1)S(1)}, bf16[576,256]{1,0:T(8,128)(2,1)S(1)}, u32[]{:S(2)}, u32[]{:S(2)}) collective-permute-start(bf16[576,256]{1,0:T(8,128)(2,1)S(1)} %get-tuple-element.75.refs_6_.refs_10_), channel_id=1, source_target_pairs={{0,16},{8,24},{16,0},{24,8},{1,17},{9,25},{17,1},{25,9},{2,18},{10... | collective-permute-start | bytes 884744 | tf_op jit(solution)/shard_map/ppermute | solution.py:320
  102.1 15.7 %collective-permute-start.49 = (bf16[576,256]{1,0:T(8,128)(2,1)S(1)}, bf16[576,256]{1,0:T(8,128)(2,1)S(1)}, u32[]{:S(2)}, u32[]{:S(2)}) collective-permute-start(bf16[576,256]{1,0:T(8,128)(2,1)S(1)} %get-tuple-element.75.refs_6_.refs_10_), channel_id=1, source_target_pairs={{0,8},{8,0},{16,24},{24,16},{1,9},{9,1},{17,25},{25,17},{2,10},{10... | collective-permute-start | bytes 884744 | tf_op jit(solution)/shard_map/ppermute | solution.py:320
  114.7 3.1 %collective-permute-start.51 = (bf16[576,256]{1,0:T(8,128)(2,1)S(1)}, bf16[576,256]{1,0:T(8,128)(2,1)S(1)}, u32[]{:S(2)}, u32[]{:S(2)}) collective-permute-start(bf16[576,256]{1,0:T(8,128)(2,1)S(1)} %collective-permute-done.50.refs_8_), channel_id=1, source_target_pairs={{0,8},{8,0},{16,24},{24,16},{1,9},{9,1},{17,25},{25,17},{2,10},{10... | collective-permute-start | bytes 884744 | tf_op jit(solution)/shard_map/ppermute | solution.py:320
  115.0 1.6 %collective-permute-start.46 = (bf16[512,256]{1,0:T(8,128)(2,1)S(1)}, bf16[512,256]{1,0:T(8,128)(2,1)S(1)}, u32[]{:S(2)}, u32[]{:S(2)}) collective-permute-start(bf16[512,256]{1,0:T(8,128)(2,1)S(1)} %get-tuple-element.73.refs_2_), channel_id=1, source_target_pairs={{0,8},{8,0},{16,24},{24,16},{1,9},{9,1},{17,25},{25,17},{2,10},{10... | collective-permute-start | bytes 786440 | tf_op jit(solution)/shard_map/ppermute | solution.py:320
  115.2 2.5 %collective-permute-start.48 = (bf16[512,256]{1,0:T(8,128)(2,1)S(1)}, bf16[512,256]{1,0:T(8,128)(2,1)S(1)}, u32[]{:S(2)}, u32[]{:S(2)}) collective-permute-start(bf16[512,256]{1,0:T(8,128)(2,1)S(1)} %collective-permute-done.47.refs_4_), channel_id=1, source_target_pairs={{0,8},{8,0},{16,24},{24,16},{1,9},{9,1},{17,25},{25,17},{2,10},{10... | collective-permute-start | bytes 786440 | tf_op jit(solution)/shard_map/ppermute | solution.py:320
  115.5 15.2 %collective-permute-start.36 = (bf16[512,256]{1,0:T(8,128)(2,1)S(1)}, bf16[512,256]{1,0:T(8,128)(2,1)S(1)}, u32[]{:S(2)}, u32[]{:S(2)}) collective-permute-start(bf16[512,256]{1,0:T(8,128)(2,1)S(1)} %get-tuple-element.60.refs_2_), channel_id=1, source_target_pairs={{0,16},{8,24},{16,0},{24,8},{1,17},{9,25},{17,1},{25,9},{2,18},{10... | collective-permute-start | bytes 786440 | tf_op jit(solution)/shard_map/ppermute | solution.py:320
  116.6 13.6 %collective-permute-start.45 = (bf16[576,256]{1,0:T(8,128)(2,1)S(1)}, bf16[576,256]{1,0:T(8,128)(2,1)S(1)}, u32[]{:S(2)}, u32[]{:S(2)}) collective-permute-start(bf16[576,256]{1,0:T(8,128)(2,1)S(1)} %get-tuple-element.71.refs_6_.refs_10_), channel_id=1, source_target_pairs={{0,16},{8,24},{16,0},{24,8},{1,17},{9,25},{17,1},{25,9},{2,18},{10... | collective-permute-start | bytes 884744 | tf_op jit(solution)/shard_map/ppermute | solution.py:320
  117.7 14.9 %collective-permute-start.44 = (bf16[576,256]{1,0:T(8,128)(2,1)S(1)}, bf16[576,256]{1,0:T(8,128)(2,1)S(1)}, u32[]{:S(2)}, u32[]{:S(2)}) collective-permute-start(bf16[576,256]{1,0:T(8,128)(2,1)S(1)} %get-tuple-element.71.refs_6_.refs_10_), channel_id=1, source_target_pairs={{0,8},{8,0},{16,24},{24,16},{1,9},{9,1},{17,25},{25,17},{2,10},{10... | collective-permute-start | bytes 884744 | tf_op jit(solution)/shard_map/ppermute | solution.py:320
  130.2 2.3 %collective-permute-start.52 = (bf16[576,256]{1,0:T(8,128)(2,1)S(1)}, bf16[576,256]{1,0:T(8,128)(2,1)S(1)}, u32[]{:S(2)}, u32[]{:S(2)}) collective-permute-start(bf16[576,256]{1,0:T(8,128)(2,1)S(1)} %collective-permute-done.45.refs_8_), channel_id=1, source_target_pairs={{0,8},{8,0},{16,24},{24,16},{1,9},{9,1},{17,25},{25,17},{2,10},{10... | collective-permute-start | bytes 884744 | tf_op jit(solution)/shard_map/ppermute | solution.py:320
  130.2 2.0 %collective-permute-start.35 = (bf16[512,256]{1,0:T(8,128)(2,1)S(1)}, bf16[512,256]{1,0:T(8,128)(2,1)S(1)}, u32[]{:S(2)}, u32[]{:S(2)}) collective-permute-start(bf16[512,256]{1,0:T(8,128)(2,1)S(1)} %get-tuple-element.60.refs_2_), channel_id=1, source_target_pairs={{0,8},{8,0},{16,24},{24,16},{1,9},{9,1},{17,25},{25,17},{2,10},{10... | collective-permute-start | bytes 786440 | tf_op jit(solution)/shard_map/ppermute | solution.py:320
  130.7 1.8 %collective-permute-start.43 = (bf16[512,256]{1,0:T(8,128)(2,1)S(1)}, bf16[512,256]{1,0:T(8,128)(2,1)S(1)}, u32[]{:S(2)}, u32[]{:S(2)}) collective-permute-start(bf16[512,256]{1,0:T(8,128)(2,1)S(1)} %collective-permute-done.36.refs_4_), channel_id=1, source_target_pairs={{0,8},{8,0},{16,24},{24,16},{1,9},{9,1},{17,25},{25,17},{2,10},{10... | collective-permute-start | bytes 786440 | tf_op jit(solution)/shard_map/ppermute | solution.py:320
